TPU v7x, 32 devices: a whole 2x2x4 slice. The times are simulated.
32 devices in a mesh: fsdp: 8 (over y, x, core), tp: 4 (over z).
Axes of the slice: x: 2, y: 2, z: 4, core: 2. Of those that a mesh axis runs over, the one named last changes fastest.
Arguments:
- hidden_in: bfloat16 [8192, 2048], P(('fsdp', 'tp')), may hold values from -6 to 6
- grad_out: bfloat16 [8192, 2048], P(('fsdp', 'tp')), may hold values from -6 to 6
- prefix_len: int32 [8], P('fsdp'), may hold values from 102 to 512
- positions: int32 [8192], P('fsdp'), may hold values from 0 to 4092, as said below
- g_attn: bfloat16 [2048], P('fsdp'), may hold values from 0.5 to 1.5
- w_query: bfloat16 [2048, 2048], P('fsdp', 'tp'), may hold values from -0.125 to 0.125
- w_key: bfloat16 [2048, 1024], P('fsdp', 'tp'), may hold values from -0.125 to 0.125
- w_value: bfloat16 [2048, 1024], P('fsdp', 'tp'), may hold values from -0.125 to 0.125
- w_out: bfloat16 [2048, 2048], P('tp', 'fsdp'), may hold values from -0.375 to 0.375
- q_gain: bfloat16 [128], P('fsdp'), may hold values from 0.796875 to 1.796875
- k_gain: bfloat16 [128], P('fsdp'), may hold values from 0.796875 to 1.796875
- g_ffn: bfloat16 [2048], P('fsdp'), may hold values from 0.5 to 1.5
- w_gate: bfloat16 [2048, 6144], P('fsdp', 'tp'), may hold values from -0.125 to 0.125
- w_up: bfloat16 [2048, 6144], P('fsdp', 'tp'), may hold values from -0.125 to 0.125
- w_down: bfloat16 [6144, 2048], P('tp', 'fsdp'), may hold values from -0.15625 to 0.15625
Outputs:
- out: bfloat16 [8192, 2048], P(('fsdp', 'tp'))
- d_x: float32 [8192, 2048], P(('fsdp', 'tp'))
- grad_g_attn: float32 [2048], P('fsdp')
- grad_w_query: float32 [2048, 2048], P('fsdp', 'tp')
- grad_w_key: float32 [2048, 1024], P('fsdp', 'tp')
- grad_w_value: float32 [2048, 1024], P('fsdp', 'tp')
- grad_w_out: float32 [2048, 2048], P('tp', 'fsdp')
- grad_q_gain: float32 [128], P('fsdp')
- grad_k_gain: float32 [128], P('fsdp')
- grad_g_ffn: float32 [2048], P('fsdp')
- grad_w_gate: float32 [2048, 6144], P('fsdp', 'tp')
- grad_w_up: float32 [2048, 6144], P('fsdp', 'tp')
- grad_w_down: float32 [6144, 2048], P('tp', 'fsdp')
Inputs may be any that keep to these rules, and one draw needn't show every extreme that they name: The keys of sequence s at places below prefix_len[s] are seen by every query of that sequence. Within each sequence positions start at 0 and rise by 1 to 4 from token to token; in one sequence every rise is 4.
All inputs are finite; a program needn't handle non-finite values.
Results may differ from a plain program's by a relative error of at most 0.025.
Values may be sent and summed in bfloat16 or wider, within the bound.
A program may use at most 256 MiB of HBM per device.

v0:
```python
import functools
import math

import jax
import jax.numpy as jnp
from jax import lax
from jax.sharding import PartitionSpec as P

HD = 128


EPS = 1e-06
ROPE_BASE = 1000000.0


def rms_scale(value):
    return lax.rsqrt(jnp.mean(value * value, axis=-1, keepdims=True) + EPS)


def norm_gain(value, gain):
    return value * rms_scale(value) * gain


def rope_tables(places):
    half = HD // 2
    ladder = jnp.arange(half, dtype=jnp.float32) * (2.0 / HD)
    frequency = jnp.exp(-ladder * math.log(ROPE_BASE))
    angle = places.astype(jnp.float32)[:, None] * frequency[None, :]
    return (jnp.cos(angle)[:, None, :], jnp.sin(angle)[:, None, :])


def rotate(value, cosine, sine):
    half = value.shape[-1] // 2
    first = value[..., :half]
    second = value[..., half:]
    return jnp.concatenate(
        [first * cosine - second * sine, second * cosine + first * sine], axis=-1
    )


def head_prep(raw, gain, cosine, sine):
    return rotate(norm_gain(raw, gain), cosine, sine)


def visibility(length, prefix):
    places = jnp.arange(length, dtype=jnp.int32)
    return (places[None, :] <= places[:, None]) | (places[None, :] < prefix)


def masked_scores(query, keys, prefix):
    scale = 1.0 / math.sqrt(HD)
    scores = jnp.einsum("qkgd,pkd->kgqp", query, keys, preferred_element_type=jnp.float32) * scale
    return jnp.where(visibility(query.shape[0], prefix), scores, -1e30)


def attend_forward(item):
    query, keys, values, prefix = item
    scores = masked_scores(query, keys, prefix)
    peak = jnp.max(scores, axis=-1, keepdims=True)
    raised = jnp.exp(scores - peak)
    total = jnp.sum(raised, axis=-1, keepdims=True)
    shares = raised / total
    mixed = jnp.einsum(
        "kgqp,pkd->qkgd", shares.astype(jnp.bfloat16), values, preferred_element_type=jnp.float32
    )
    return (mixed, (peak + jnp.log(total))[..., 0])


def attend_backward(item):
    query, keys, values, grad_mixed, log_total, prefix = item
    scale = 1.0 / math.sqrt(HD)
    scores = masked_scores(query, keys, prefix)
    shares = jnp.exp(scores - log_total[..., None])
    grad_shares = jnp.einsum(
        "qkgd,pkd->kgqp", grad_mixed, values, preferred_element_type=jnp.float32
    )
    grad_scores = shares * (grad_shares - jnp.sum(grad_shares * shares, axis=-1, keepdims=True))
    grad_low = (grad_scores * scale).astype(jnp.bfloat16)
    grad_query = jnp.einsum("kgqp,pkd->qkgd", grad_low, keys, preferred_element_type=jnp.float32)
    grad_keys = jnp.einsum("kgqp,qkgd->pkd", grad_low, query, preferred_element_type=jnp.float32)
    grad_values = jnp.einsum(
        "kgqp,qkgd->pkd",
        shares.astype(jnp.bfloat16),
        grad_mixed,
        preferred_element_type=jnp.float32,
    )
    return (grad_query, grad_keys, grad_values)


def fetch_attention(g_attn, w_query, w_key, w_value, w_out, q_gain, k_gain):
    return (
        lax.all_gather(w_query, "fsdp", axis=0, tiled=True),
        lax.all_gather(w_key, "fsdp", axis=0, tiled=True),
        lax.all_gather(w_value, "fsdp", axis=0, tiled=True),
        lax.all_gather(w_out, "fsdp", axis=1, tiled=True),
        lax.all_gather(g_attn, "fsdp", axis=0, tiled=True),
        lax.all_gather(q_gain, "fsdp", axis=0, tiled=True),
        lax.all_gather(k_gain, "fsdp", axis=0, tiled=True),
    )


def fetch_ffn(g_ffn, w_gate, w_up, w_down):
    return (
        lax.all_gather(w_gate, "fsdp", axis=0, tiled=True),
        lax.all_gather(w_up, "fsdp", axis=0, tiled=True),
        lax.all_gather(w_down, "fsdp", axis=1, tiled=True),
        lax.all_gather(g_ffn, "fsdp", axis=0, tiled=True),
    )


def per_device(
    hidden_in,
    grad_out,
    prefix_len,
    positions,
    g_attn,
    w_query,
    w_key,
    w_value,
    w_out,
    q_gain,
    k_gain,
    g_ffn,
    w_gate,
    w_up,
    w_down,
):
    parts = lax.axis_size("tp")
    own_rows = hidden_in.shape[0]
    group_rows = own_rows * parts
    count = prefix_len.shape[0]
    length = group_rows // count
    attn_set = fetch_attention(g_attn, w_query, w_key, w_value, w_out, q_gain, k_gain)
    full_query, full_key, full_value, full_out, gain_attn, gain_query, gain_key = attn_set
    first_gain = gain_attn.astype(jnp.float32)
    query_gain = gain_query.astype(jnp.float32)
    key_gain = gain_key.astype(jnp.float32)
    tokens_all = lax.all_gather(hidden_in, "tp", axis=0, tiled=True)
    tokens_float = tokens_all.astype(jnp.float32)
    own_float = hidden_in.astype(jnp.float32)
    normed = norm_gain(tokens_float, first_gain).astype(jnp.bfloat16)
    query_raw = jnp.dot(normed, full_query, preferred_element_type=jnp.float32).reshape(
        group_rows, -1, HD
    )
    keys_raw = jnp.dot(normed, full_key, preferred_element_type=jnp.float32).reshape(
        group_rows, -1, HD
    )
    values_low = (
        jnp.dot(normed, full_value, preferred_element_type=jnp.float32)
        .astype(jnp.bfloat16)
        .reshape(group_rows, -1, HD)
    )
    kv_local = keys_raw.shape[1]
    grouping = query_raw.shape[1] // kv_local
    cosine, sine = rope_tables(positions)
    query_low = head_prep(query_raw, query_gain, cosine, sine).astype(jnp.bfloat16)
    keys_low = head_prep(keys_raw, key_gain, cosine, sine).astype(jnp.bfloat16)
    query_seq = query_low.reshape(count, length, kv_local, grouping, HD)
    keys_seq = keys_low.reshape(count, length, kv_local, HD)
    values_seq = values_low.reshape(count, length, kv_local, HD)
    mixed, log_total = lax.map(attend_forward, (query_seq, keys_seq, values_seq, prefix_len))
    mixed_low = mixed.reshape(group_rows, -1).astype(jnp.bfloat16)
    attn_part = jnp.dot(mixed_low, full_out, preferred_element_type=jnp.float32)
    ffn_set = fetch_ffn(g_ffn, w_gate, w_up, w_down)
    full_gate, full_up, full_down, gain_ffn = ffn_set
    second_gain = gain_ffn.astype(jnp.float32)
    middle = own_float + lax.psum_scatter(
        attn_part.astype(jnp.bfloat16), "tp", scatter_dimension=0, tiled=True
    ).astype(jnp.float32)
    branch = lax.all_gather(
        norm_gain(middle, second_gain).astype(jnp.bfloat16), "tp", axis=0, tiled=True
    )
    gate = jnp.dot(branch, full_gate, preferred_element_type=jnp.float32)
    upward = jnp.dot(branch, full_up, preferred_element_type=jnp.float32)
    sigmoid_gate = jax.nn.sigmoid(gate)
    silu_gate = gate * sigmoid_gate
    product = (silu_gate * upward).astype(jnp.bfloat16)
    ffn_part = jnp.dot(product, full_down, preferred_element_type=jnp.float32)
    result = middle + lax.psum_scatter(
        ffn_part.astype(jnp.bfloat16), "tp", scatter_dimension=0, tiled=True
    ).astype(jnp.float32)
    out = result.astype(jnp.bfloat16)
    grad_all = lax.all_gather(grad_out, "tp", axis=0, tiled=True)
    full_gate, full_up, full_down, gain_ffn = fetch_ffn(g_ffn, w_gate, w_up, w_down)
    grad_product = jnp.einsum("td,fd->tf", grad_all, full_down, preferred_element_type=jnp.float32)
    grad_w_down = jnp.einsum("tf,td->fd", product, grad_all, preferred_element_type=jnp.float32)
    grad_gate = (
        grad_product * upward * (sigmoid_gate * (1.0 + gate * (1.0 - sigmoid_gate)))
    ).astype(jnp.bfloat16)
    grad_up = (grad_product * silu_gate).astype(jnp.bfloat16)
    grad_w_gate = jnp.einsum("td,tf->df", branch, grad_gate, preferred_element_type=jnp.float32)
    grad_w_up = jnp.einsum("td,tf->df", branch, grad_up, preferred_element_type=jnp.float32)
    grad_branch = jnp.einsum("tf,df->td", grad_gate, full_gate, preferred_element_type=jnp.float32)
    grad_branch = grad_branch + jnp.einsum(
        "tf,df->td", grad_up, full_up, preferred_element_type=jnp.float32
    )
    grad_branch_own = lax.psum_scatter(
        grad_branch.astype(jnp.bfloat16), "tp", scatter_dimension=0, tiled=True
    ).astype(jnp.float32)
    unused_second, pull_second = jax.vjp(norm_gain, middle, second_gain)
    grad_mid_norm, grad_second = pull_second(grad_branch_own)
    grad_middle = grad_out.astype(jnp.float32) + grad_mid_norm
    grad_mid_all = lax.all_gather(grad_middle.astype(jnp.bfloat16), "tp", axis=0, tiled=True)
    ffn_grads = (
        lax.psum_scatter(
            grad_w_gate.astype(jnp.bfloat16), "fsdp", scatter_dimension=0, tiled=True
        ).astype(jnp.float32),
        lax.psum_scatter(
            grad_w_up.astype(jnp.bfloat16), "fsdp", scatter_dimension=0, tiled=True
        ).astype(jnp.float32),
        lax.psum_scatter(
            grad_w_down.astype(jnp.bfloat16), "fsdp", scatter_dimension=1, tiled=True
        ).astype(jnp.float32),
        lax.psum_scatter(
            grad_second.astype(jnp.bfloat16), "fsdp", scatter_dimension=0, tiled=True
        ).astype(jnp.float32),
    )
    full_query, full_key, full_value, full_out, gain_attn, gain_query, gain_key = fetch_attention(
        g_attn, w_query, w_key, w_value, w_out, q_gain, k_gain
    )
    grad_mixed = jnp.einsum(
        "td,hd->th", grad_mid_all, full_out, preferred_element_type=jnp.float32
    ).astype(jnp.bfloat16)
    grad_w_out = jnp.einsum(
        "th,td->hd", mixed_low, grad_mid_all, preferred_element_type=jnp.float32
    )
    grad_mixed_seq = grad_mixed.reshape(count, length, kv_local, grouping, HD)
    grads_query, grads_keys, grads_values = lax.map(
        attend_backward, (query_seq, keys_seq, values_seq, grad_mixed_seq, log_total, prefix_len)
    )
    unused_query, pull_query = jax.vjp(
        functools.partial(head_prep, cosine=cosine, sine=sine), query_raw, query_gain
    )
    grad_query_raw, grad_q_gain = pull_query(grads_query.reshape(group_rows, -1, HD))
    unused_keys, pull_keys = jax.vjp(
        functools.partial(head_prep, cosine=cosine, sine=sine), keys_raw, key_gain
    )
    grad_keys_raw, grad_k_gain = pull_keys(grads_keys.reshape(group_rows, -1, HD))
    grad_query_low = grad_query_raw.reshape(group_rows, -1).astype(jnp.bfloat16)
    grad_keys_low = grad_keys_raw.reshape(group_rows, -1).astype(jnp.bfloat16)
    grad_values_low = grads_values.reshape(group_rows, -1).astype(jnp.bfloat16)
    grad_w_query = jnp.einsum(
        "td,th->dh", normed, grad_query_low, preferred_element_type=jnp.float32
    )
    grad_w_key = jnp.einsum("td,th->dh", normed, grad_keys_low, preferred_element_type=jnp.float32)
    grad_w_value = jnp.einsum(
        "td,th->dh", normed, grad_values_low, preferred_element_type=jnp.float32
    )
    grad_normed = jnp.einsum(
        "th,dh->td", grad_query_low, full_query, preferred_element_type=jnp.float32
    )
    grad_normed = grad_normed + jnp.einsum(
        "th,dh->td", grad_keys_low, full_key, preferred_element_type=jnp.float32
    )
    grad_normed = grad_normed + jnp.einsum(
        "th,dh->td", grad_values_low, full_value, preferred_element_type=jnp.float32
    )
    grad_normed_own = lax.psum_scatter(
        grad_normed.astype(jnp.bfloat16), "tp", scatter_dimension=0, tiled=True
    ).astype(jnp.float32)
    unused_first, pull_first = jax.vjp(norm_gain, own_float, first_gain)
    grad_tokens, grad_first = pull_first(grad_normed_own)
    grad_in = grad_middle + grad_tokens
    attn_grads = (
        lax.psum_scatter(
            grad_w_query.astype(jnp.bfloat16), "fsdp", scatter_dimension=0, tiled=True
        ).astype(jnp.float32),
        lax.psum_scatter(
            grad_w_key.astype(jnp.bfloat16), "fsdp", scatter_dimension=0, tiled=True
        ).astype(jnp.float32),
        lax.psum_scatter(
            grad_w_value.astype(jnp.bfloat16), "fsdp", scatter_dimension=0, tiled=True
        ).astype(jnp.float32),
        lax.psum_scatter(
            grad_w_out.astype(jnp.bfloat16), "fsdp", scatter_dimension=1, tiled=True
        ).astype(jnp.float32),
        lax.psum_scatter(
            grad_first.astype(jnp.bfloat16), "fsdp", scatter_dimension=0, tiled=True
        ).astype(jnp.float32),
        lax.psum_scatter(
            grad_q_gain.astype(jnp.bfloat16), "fsdp", scatter_dimension=0, tiled=True
        ).astype(jnp.float32),
        lax.psum_scatter(
            grad_k_gain.astype(jnp.bfloat16), "fsdp", scatter_dimension=0, tiled=True
        ).astype(jnp.float32),
    )
    gain_totals = lax.psum((attn_grads[4], ffn_grads[3], attn_grads[5], attn_grads[6]), "tp")
    return (
        out,
        grad_in,
        gain_totals[0],
        attn_grads[0],
        attn_grads[1],
        attn_grads[2],
        attn_grads[3],
        gain_totals[2],
        gain_totals[3],
        gain_totals[1],
        ffn_grads[0],
        ffn_grads[1],
        ffn_grads[2],
    )


def solution(mesh):
    in_specs = (
        P(("fsdp", "tp"), None),
        P(("fsdp", "tp"), None),
        P("fsdp"),
        P("fsdp"),
        P("fsdp"),
        P("fsdp", "tp"),
        P("fsdp", "tp"),
        P("fsdp", "tp"),
        P("tp", "fsdp"),
        P("fsdp"),
        P("fsdp"),
        P("fsdp"),
        P("fsdp", "tp"),
        P("fsdp", "tp"),
        P("tp", "fsdp"),
    )
    out_specs = (
        P(("fsdp", "tp"), None),
        P(("fsdp", "tp"), None),
        P("fsdp"),
        P("fsdp", "tp"),
        P("fsdp", "tp"),
        P("fsdp", "tp"),
        P("tp", "fsdp"),
        P("fsdp"),
        P("fsdp"),
        P("fsdp"),
        P("fsdp", "tp"),
        P("fsdp", "tp"),
        P("tp", "fsdp"),
    )
    return jax.shard_map(
        per_device, mesh=mesh, in_specs=in_specs, out_specs=out_specs, check_vma=False
    )
```

profile of v0, /device:TPU:0, one launch (start us, length us, event | category | flops | bytes accessed | tf_op | source)
XLA Modules:
  0.0 1320.9 jit_solution(735477600602454414)
XLA Ops:
  15.0 15.2 %all-reduce.12 = (bf16[128]{0:T(256)(128)(2,1)S(1)}, bf16[128]{0:T(256)(128)(2,1)S(1)}) all-reduce(bf16[128]{0:T(256)(128)(2,1)S(1)} %dynamic-update-slice.1, bf16[128]{0:T(256)(128)(2,1)S(1)} %dynamic-update-slice), channel_id=1, replica_groups=mesh['fsdp'=8,'tp'=4] {'fsdp'}, use_global_device_ids=true, to_apply=%add.5 | all-reduce | flops 256 | bytes 1024
  31.6 7.9 all-gather
  42.3 50.8 %all-gather.14.cloned.1.call-done = bf16[1024,2048]{1,0:T(8,128)(2,1)} async-done(((bf16[256,2048]{1,0:T(8,128)(2,1)}), bf16[1024,2048]{1,0:T(8,128)(2,1)}) %all-gather.14.cloned.1.call-update) | async-done | bytes 4194320 | tf_op jit(solution)/shard_map/all_gather | solution.py:138
  99.5 17.3 %all-gather.18.cloned.1.call-done = bf16[2048,256]{1,0:T(8,128)(2,1)} async-done(((bf16[256,256]{1,0:T(8,128)(2,1)}), bf16[2048,256]{1,0:T(8,128)(2,1)}) %all-gather.18.cloned.1.call-update) | async-done | bytes 1048592 | tf_op jit(solution)/shard_map/all_gather | solution.py:93
  116.8 4.8 multiply_reduce_fusion.6
  123.2 23.3 %all-gather.20.cloned.1.call-done = bf16[2048,512]{1,0:T(8,128)(2,1)} async-done(((bf16[256,512]{1,0:T(8,128)(2,1)}), bf16[2048,512]{1,0:T(8,128)(2,1)}) %all-gather.20.cloned.1.call-update) | async-done | bytes 2097168 | tf_op jit(solution)/shard_map/all_gather | solution.py:92
  146.5 5.3 multiply_reduce_fusion.3
  160.3 11.4 all-gather.16.cloned.1.call-done
  171.7 3.9 convolution_convert_fusion.10
  175.6 8.6 fusion.51
  184.2 8.0 fusion.4
  192.2 7.7 fusion.29
  201.5 6.1 convolution_convert_fusion.4
  208.4 8.9 all-gather.1
  217.3 67.2 %reduce-scatter.12.cloned.1.call-done = bf16[256,2048]{1,0:T(8,128)(2,1)} async-done(((bf16[1024,2048]{1,0:T(8,128)(2,1)}), bf16[256,2048]{1,0:T(8,128)(2,1)}) %reduce-scatter.12.cloned.1.call-update) | async-done | bytes 1048592 | tf_op jit(solution)/shard_map/reduce_scatter | solution.py:167
  290.9 41.4 %all-gather.28.cloned.1.call-done = bf16[2048,1536]{1,0:T(8,128)(2,1)} async-done(((bf16[256,1536]{1,0:T(8,128)(2,1)}), bf16[2048,1536]{1,0:T(8,128)(2,1)}) %all-gather.28.cloned.1.call-update) | async-done | bytes 6291472 | tf_op jit(solution)/shard_map/all_gather | solution.py:105
  332.4 82.9 %all-gather.24.cloned.1.call-done = bf16[1024,2048]{1,0:T(8,128)(2,1)} async-done(((bf16[256,2048]{1,0:T(8,128)(2,1)}), bf16[1024,2048]{1,0:T(8,128)(2,1)}) %all-gather.24.cloned.1.call-update) | async-done | bytes 4194320 | tf_op jit(solution)/shard_map/all_gather | solution.py:170
  415.3 12.0 fusion.53
  427.3 33.8 %all-gather.26.cloned.1.call-done = bf16[2048,1536]{1,0:T(8,128)(2,1)} async-done(((bf16[256,1536]{1,0:T(8,128)(2,1)}), bf16[2048,1536]{1,0:T(8,128)(2,1)}) %all-gather.26.cloned.1.call-update) | async-done | bytes 6291472 | tf_op jit(solution)/shard_map/all_gather | solution.py:104
  461.1 11.7 fusion.52
  472.8 70.5 %all-gather.32.cloned.1.call-done = bf16[1024,2048]{1,0:T(8,128)(2,1)} async-done(((bf16[256,2048]{1,0:T(8,128)(2,1)}), bf16[1024,2048]{1,0:T(8,128)(2,1)}) %all-gather.32.cloned.1.call-update) | async-done | bytes 4194320 | tf_op jit(solution)/shard_map/all_gather | solution.py:183
  543.3 47.0 %all-gather.30.cloned.1.call-done = bf16[1536,2048]{1,0:T(8,128)(2,1)} async-done(((bf16[1536,256]{1,0:T(8,128)(2,1)}), bf16[1536,2048]{1,0:T(8,128)(2,1)}) %all-gather.30.cloned.1.call-update) | async-done | bytes 6291472 | tf_op jit(solution)/shard_map/all_gather | solution.py:106
  590.2 16.6 %multiply_convert_fusion = (bf16[1024,1536]{1,0:T(8,128)(2,1)}, bf16[1024,1536]{1,0:T(8,128)(2,1)S(1)}, bf16[1024,1536]{1,0:T(8,128)(2,1)}) fusion(f32[1024,1536]{1,0:T(8,128)} %fusion.52, f32[1024,1536]{1,0:T(8,128)} %fusion.53, bf16[1024,2048]{1,0:T(8,128)(2,1)} %all-gather.32.cloned.1.call-done, bf16[1536,2048]{1,0:T(8,128)(2,1)} %all-gather.30.cloned.1.call-done), kind=kOutput, calls=%fused_computation.25 | convolution fusion | flops 6466043904 | bytes 32505856 | tf_op jit(solution)/shard_map/td,fd->tf/dot_general | solution.py:185
  606.9 6.7 fusion.54
  613.6 11.2 add_convert_fusion.1
  624.9 76.9 %reduce-scatter.16.cloned.1.call-done = bf16[256,2048]{1,0:T(8,128)(2,1)} async-done(((bf16[1024,2048]{1,0:T(8,128)(2,1)}), bf16[256,2048]{1,0:T(8,128)(2,1)}) %reduce-scatter.16.cloned.1.call-update) | async-done | bytes 1048592 | tf_op jit(solution)/shard_map/reduce_scatter | solution.py:197
  707.5 11.3 convolution_convert_fusion
  718.8 11.8 convolution_convert_fusion.1
  730.7 11.4 convolution_convert_fusion.2
  742.7 46.1 %all-gather.34.cloned.1.call-done = bf16[1024,2048]{1,0:T(8,128)(2,1)} async-done(((bf16[256,2048]{1,0:T(8,128)(2,1)}), bf16[1024,2048]{1,0:T(8,128)(2,1)}) %all-gather.34.cloned.1.call-update) | async-done | bytes 4194320 | tf_op jit(solution)/shard_map/all_gather | solution.py:203
  788.8 5.2 convolution_convert_fusion.9
  794.1 11.1 fusion.34
  808.4 10.3 fusion.55
  819.0 24.6 %fusion.30 = f32[1024,2,128]{2,0,1:T(8,128)} fusion(f32[2,1024,1024,2]{2,1,3,0:T(8,128)} %fusion.55, f32[2,2,1024,1024]{2,3,1,0:T(8,128)} %get-tuple-element.105, f32[2,2,1024]{2,1,0:T(2,128)S(1)} %log_add_fusion, bf16[1024,2,2,64]{3,0,2,1:T(8,128)(2,1)} %bitcast.137, bf16[1024,2,2,64]{3,0,2,1:T(8,128)(2,1)} %bitcast.135), kind=kOutput, calls=%fused_computation.75 | convolution fusion | flops 1105204224 | bytes 35667968 | tf_op jit(solution)/shard_map/while/body/eval_jaxpr/kgqp,qkgd->pkd/dot_general | solution.py:80
  850.6 4.7 convolution_convert_fusion.8
  855.4 6.2 convolution_convert_fusion.5
  861.9 28.7 %fusion.16 = f32[2,128,2,1024]{3,1,2,0:T(8,128)} fusion(f32[2,1024,1024,2]{2,1,3,0:T(8,128)} %fusion.55, f32[2,2,1024,1024]{2,3,1,0:T(8,128)} %get-tuple-element.105, f32[2,2,1024]{2,1,0:T(2,128)S(1)} %log_add_fusion, bf16[1024,2,64]{2,0,1:T(8,128)(2,1)} %get-tuple-element.95, bf16[1024,2,64]{2,0,1:T(8,128)(2,1)} %get-tuple-element.94), kind=kOutput, calls=%fused_computation.32 | convolution fusion | flops 1104155648 | bytes 36192256 | tf_op jit(solution)/shard_map/while/body/eval_jaxpr/kgqp,pkd->qkgd/dot_general | solution.py:79
  909.3 11.2 convolution_convert_fusion.3
  926.7 55.6 %reduce-scatter.28.cloned.1.call-done = bf16[256,1536]{1,0:T(8,128)(2,1)} async-done(((bf16[2048,1536]{1,0:T(8,128)(2,1)}), bf16[256,1536]{1,0:T(8,128)(2,1)}) %reduce-scatter.28.cloned.1.call-update) | async-done | bytes 786448 | tf_op jit(solution)/shard_map/reduce_scatter | solution.py:205
  984.7 36.6 %reduce-scatter.24.cloned.1.call-done = bf16[256,256]{1,0:T(8,128)(2,1)} async-done(((bf16[2048,256]{1,0:T(8,128)(2,1)}), bf16[256,256]{1,0:T(8,128)(2,1)}) %reduce-scatter.24.cloned.1.call-update) | async-done | bytes 131088 | tf_op jit(solution)/shard_map/reduce_scatter | solution.py:271
  1022.9 37.4 %reduce-scatter.22.cloned.1.call-done = bf16[256,256]{1,0:T(8,128)(2,1)} async-done(((bf16[2048,256]{1,0:T(8,128)(2,1)}), bf16[256,256]{1,0:T(8,128)(2,1)}) %reduce-scatter.22.cloned.1.call-update) | async-done | bytes 131088 | tf_op jit(solution)/shard_map/reduce_scatter | solution.py:268
  1061.9 42.8 %reduce-scatter.26.cloned.1.call-done = bf16[512,256]{1,0:T(8,128)(2,1)} async-done(((bf16[512,2048]{1,0:T(8,128)(2,1)}), bf16[512,256]{1,0:T(8,128)(2,1)}) %reduce-scatter.26.cloned.1.call-update) | async-done | bytes 262160 | tf_op jit(solution)/shard_map/reduce_scatter | solution.py:274
  1106.5 43.1 %reduce-scatter.20.cloned.1.call-done = bf16[256,512]{1,0:T(8,128)(2,1)} async-done(((bf16[2048,512]{1,0:T(8,128)(2,1)}), bf16[256,512]{1,0:T(8,128)(2,1)}) %reduce-scatter.20.cloned.1.call-update) | async-done | bytes 262160 | tf_op jit(solution)/shard_map/reduce_scatter | solution.py:265
  1151.4 77.3 %reduce-scatter.18.cloned.1.call-done = bf16[256,2048]{1,0:T(8,128)(2,1)} async-done(((bf16[1024,2048]{1,0:T(8,128)(2,1)}), bf16[256,2048]{1,0:T(8,128)(2,1)}) %reduce-scatter.18.cloned.1.call-update) | async-done | bytes 1048592 | tf_op jit(solution)/shard_map/reduce_scatter | solution.py:258
  1231.0 13.8 %all-reduce.11 = (bf16[2048]{0:T(1024)(128)(2,1)S(1)}, bf16[128]{0:T(256)(128)(2,1)S(1)}, bf16[128]{0:T(256)(128)(2,1)S(1)}, bf16[2048]{0:T(1024)(128)(2,1)S(1)}) all-reduce(bf16[2048]{0:T(1024)(128)(2,1)S(1)} %get-tuple-element.70, bf16[128]{0:T(256)(128)(2,1)S(1)} %get-tuple-element.68, ...), channel_id=6, replica_groups=mesh['fsdp'=8,'tp'=4] {'fsdp'}, use_global_device_ids=true, to_apply=%region_17.18.clone | all-reduce | flops 4352 | bytes 17408
  1245.0 12.6 all-reduce.10
  1257.5 51.0 %reduce-scatter.14.cloned.1.call-done = bf16[256,2048]{1,0:T(8,128)(2,1)} async-done(((bf16[1024,2048]{1,0:T(8,128)(2,1)}), bf16[256,2048]{1,0:T(8,128)(2,1)}) %reduce-scatter.14.cloned.1.call-update) | async-done | bytes 1048592 | tf_op jit(solution)/shard_map/reduce_scatter | solution.py:179
  1308.6 5.1 fusion.26
  (202 shorter events, 87.9 us)
Async XLA Ops:
  7.2 85.9 %all-gather.14.cloned.1.call-start = ((), (), s32[]{:S(2)}) async-start(), calls=%async_computation.11 | async-start | bytes 5242880 | tf_op jit(solution)/shard_map/all_gather | solution.py:138
  7.9 108.9 %all-gather.18.cloned.1.call-start = ((), (), s32[]{:S(2)}) async-start(), calls=%async_computation.13 | async-start | bytes 1179648 | tf_op jit(solution)/shard_map/all_gather | solution.py:93
  8.7 137.9 %all-gather.20.cloned.1.call-start = ((), (), s32[]{:S(2)}) async-start(), calls=%async_computation.14 | async-start | bytes 2359296 | tf_op jit(solution)/shard_map/all_gather | solution.py:92
  9.4 162.3 %all-gather.16.cloned.1.call-start = ((), (), s32[]{:S(2)}) async-start(), calls=%async_computation.12 | async-start | bytes 1179648 | tf_op jit(solution)/shard_map/all_gather | solution.py:94
  10.0 191.6 %all-gather.22.cloned.1.call-start = ((), (), s32[]{:S(2)}) async-start(), calls=%async_computation.15 | async-start | bytes 2359296 | tf_op jit(solution)/shard_map/all_gather | solution.py:95
  10.6 274.0 %reduce-scatter.12.cloned.1.call-start = ((), (), s32[]{:S(2)}) async-start(), calls=%async_computation.16 | async-start | bytes 5242880 | tf_op jit(solution)/shard_map/reduce_scatter | solution.py:167
  30.2 121.6 %copy-start.39 = (f32[128]{0:T(128)}, f32[128]{0:T(128)S(1)}, u32[]{:S(2)}) copy-start(f32[128]{0:T(128)S(1)} %convert_element_type.193) | copy-start | bytes 1540
  30.2 128.3 %copy-start.37 = (f32[128]{0:T(128)}, f32[128]{0:T(128)S(1)}, u32[]{:S(2)}) copy-start(f32[128]{0:T(128)S(1)} %convert_element_type.191) | copy-start | bytes 1540
  39.5 60.0 %copy-start.31 = (f32[8,1,256]{2,1,0:T(1,128)}, f32[8,1,256]{2,1,0:T(1,128)S(1)}, u32[]{:S(2)}) copy-start(f32[8,1,256]{2,1,0:T(1,128)S(1)} %convert_element_type.246) | copy-start | bytes 24580
  40.5 113.1 %copy-start.10 = (f32[1024,64]{0,1:T(8,128)}, f32[1024,64]{0,1:T(8,128)S(1)}, u32[]{:S(2)}) copy-start(f32[1024,64]{0,1:T(8,128)S(1)} %get-tuple-element.96) | copy-start | bytes 786436
  40.5 113.1 %copy-start.12 = (f32[1024,64]{0,1:T(8,128)}, f32[1024,64]{0,1:T(8,128)S(1)}, u32[]{:S(2)}) copy-start(f32[1024,64]{0,1:T(8,128)S(1)} %get-tuple-element.97) | copy-start | bytes 786436
  40.7 118.1 %copy-start.8 = (f32[1024,64]{1,0:T(8,128)}, f32[1024,64]{1,0:T(8,128)S(1)}, u32[]{:S(2)}) copy-start(f32[1024,64]{1,0:T(8,128)S(1)} %copy.79) | copy-start | bytes 786436
  41.0 117.9 %copy-start.9 = (f32[1024,64]{1,0:T(8,128)}, f32[1024,64]{1,0:T(8,128)S(1)}, u32[]{:S(2)}) copy-start(f32[1024,64]{1,0:T(8,128)S(1)} %copy.80) | copy-start | bytes 786436
  93.0 3.4 copy-start.4
  123.1 35.4 %copy-start.5 = (f32[1024,2,128]{2,0,1:T(8,128)}, f32[1024,2,128]{2,0,1:T(8,128)S(1)}, u32[]{:S(2)}) copy-start(f32[1024,2,128]{2,0,1:T(8,128)S(1)} %copy.78) | copy-start | bytes 3145732
  123.2 35.3 %copy-start.29 = (f32[1024,2]{0,1:T(2,128)}, f32[1024,2]{0,1:T(2,128)S(1)}, u32[]{:S(2)}) copy-start(f32[1024,2]{0,1:T(2,128)S(1)} %fusion.39) | copy-start | bytes 24580
  160.3 15.2 %copy-start.19 = (bf16[1024,4,64]{2,0,1:T(8,128)(2,1)S(1)}, bf16[1024,4,64]{2,0,1:T(8,128)(2,1)}, u32[]{:S(2)}) copy-start(bf16[1024,4,64]{2,0,1:T(8,128)(2,1)} %copy.81) | copy-start | bytes 1572868
  160.3 15.3 %copy-start.20 = (bf16[1024,4,64]{2,0,1:T(8,128)(2,1)S(1)}, bf16[1024,4,64]{2,0,1:T(8,128)(2,1)}, u32[]{:S(2)}) copy-start(bf16[1024,4,64]{2,0,1:T(8,128)(2,1)} %copy.82) | copy-start | bytes 1572868
  160.3 15.3 %copy-start.21 = (pred[1024,1024]{0,1:T(8,128)(4,1)S(1)}, pred[1024,1024]{0,1:T(8,128)(4,1)}, u32[]{:S(2)}) copy-start(pred[1024,1024]{0,1:T(8,128)(4,1)} %fusion.17) | copy-start | bytes 3145732
  171.7 3.9 copy-start.25
  171.7 3.9 copy-start.26
  175.6 16.6 %copy-start.24 = (bf16[1024,256]{0,1:T(8,128)(2,1)}, bf16[1024,256]{0,1:T(8,128)(2,1)S(1)}, u32[]{:S(2)}) copy-start(bf16[1024,256]{0,1:T(8,128)(2,1)S(1)} %convolution_convert_fusion.10) | copy-start | bytes 1572868
  207.6 77.0 %copy-start = (bf16[256,2048]{1,0:T(8,128)(2,1)S(1)}, bf16[256,2048]{1,0:T(8,128)(2,1)}, u32[]{:S(2)}) copy-start(bf16[256,2048]{1,0:T(8,128)(2,1)} %param.15) | copy-start | bytes 3145732
  207.6 124.8 %all-gather.28.cloned.1.call-start = ((), (), s32[]{:S(2)}) async-start(), calls=%async_computation.19 | async-start | bytes 7077888 | tf_op jit(solution)/shard_map/all_gather | solution.py:105
  208.4 206.9 %all-gather.24.cloned.1.call-start = ((), (), s32[]{:S(2)}) async-start(), calls=%async_computation.17 | async-start | bytes 5242880 | tf_op jit(solution)/shard_map/all_gather | solution.py:170
  288.8 172.2 %all-gather.26.cloned.1.call-start = ((), (), s32[]{:S(2)}) async-start(), calls=%async_computation.18 | async-start | bytes 7077888 | tf_op jit(solution)/shard_map/all_gather | solution.py:104
  289.6 253.7 %all-gather.32.cloned.1.call-start = ((), (), s32[]{:S(2)}) async-start(), calls=%async_computation.22 | async-start | bytes 5242880 | tf_op jit(solution)/shard_map/all_gather | solution.py:183
  290.2 300.1 %all-gather.30.cloned.1.call-start = ((), (), s32[]{:S(2)}) async-start(), calls=%async_computation.20 | async-start | bytes 7077888 | tf_op jit(solution)/shard_map/all_gather | solution.py:106
  290.9 410.9 %reduce-scatter.16.cloned.1.call-start = ((), (), s32[]{:S(2)}) async-start(), calls=%async_computation.23 | async-start | bytes 5242880 | tf_op jit(solution)/shard_map/reduce_scatter | solution.py:197
  590.2 16.7 %copy-start.41 = (bf16[2048,1536]{1,0:T(8,128)(2,1)S(1)}, bf16[2048,1536]{1,0:T(8,128)(2,1)}, u32[]{:S(2)}) copy-start(bf16[2048,1536]{1,0:T(8,128)(2,1)} %all-gather.26.cloned.1.call-done) | copy-start | bytes 18874372
  606.9 6.7 copy-start.45
  624.9 77.0 %copy-start.3 = (bf16[256,2048]{1,0:T(8,128)(2,1)S(1)}, bf16[256,2048]{1,0:T(8,128)(2,1)}, u32[]{:S(2)}) copy-start(bf16[256,2048]{1,0:T(8,128)(2,1)} %reduce-scatter.12.cloned.1.call-done) | copy-start | bytes 3145732
  624.9 79.3 %copy-start.7 = (bf16[256,2048]{1,0:T(8,128)(2,1)S(1)}, bf16[256,2048]{1,0:T(8,128)(2,1)}, u32[]{:S(2)}) copy-start(bf16[256,2048]{1,0:T(8,128)(2,1)} %param.16) | copy-start | bytes 3145732
  624.9 163.9 %all-gather.34.cloned.1.call-start = ((), (), s32[]{:S(2)}) async-start(), calls=%async_computation.24 | async-start | bytes 5242880 | tf_op jit(solution)/shard_map/all_gather | solution.py:203
  707.4 214.4 %reduce-scatter.32.cloned.1.call-start = ((), (), s32[]{:S(2)}) async-start(), calls=%async_computation.32 | async-start | bytes 7077888 | tf_op jit(solution)/shard_map/reduce_scatter | solution.py:211
  718.8 205.4 %reduce-scatter.30.cloned.1.call-start = ((), (), s32[]{:S(2)}) async-start(), calls=%async_computation.31 | async-start | bytes 7077888 | tf_op jit(solution)/shard_map/reduce_scatter | solution.py:208
  730.6 251.6 %reduce-scatter.28.cloned.1.call-start = ((), (), s32[]{:S(2)}) async-start(), calls=%async_computation.30 | async-start | bytes 7077888 | tf_op jit(solution)/shard_map/reduce_scatter | solution.py:205
  742.1 279.1 %reduce-scatter.24.cloned.1.call-start = ((), (), s32[]{:S(2)}) async-start(), calls=%async_computation.28 | async-start | bytes 1179648 | tf_op jit(solution)/shard_map/reduce_scatter | solution.py:271
  794.0 11.2 copy-start.15
  794.1 11.9 copy-start.13
  818.7 241.5 %reduce-scatter.22.cloned.1.call-start = ((), (), s32[]{:S(2)}) async-start(), calls=%async_computation.27 | async-start | bytes 1179648 | tf_op jit(solution)/shard_map/reduce_scatter | solution.py:268
  843.6 3.2 copy-start.36
  855.3 249.4 %reduce-scatter.26.cloned.1.call-start = ((), (), s32[]{:S(2)}) async-start(), calls=%async_computation.29 | async-start | bytes 2359296 | tf_op jit(solution)/shard_map/reduce_scatter | solution.py:274
  861.6 29.0 %copy-start.11 = (f32[1024,64]{0,1:T(8,128)S(1)}, f32[1024,64]{0,1:T(8,128)}, u32[]{:S(2)}) copy-start(f32[1024,64]{0,1:T(8,128)} %copy-done.10) | copy-start | bytes 786436
  861.6 288.0 %reduce-scatter.20.cloned.1.call-start = ((), (), s32[]{:S(2)}) async-start(), calls=%async_computation.26 | async-start | bytes 2359296 | tf_op jit(solution)/shard_map/reduce_scatter | solution.py:265
  900.2 328.5 %reduce-scatter.18.cloned.1.call-start = ((), (), s32[]{:S(2)}) async-start(), calls=%async_computation.25 | async-start | bytes 5242880 | tf_op jit(solution)/shard_map/reduce_scatter | solution.py:258
  909.2 399.4 %reduce-scatter.14.cloned.1.call-start = ((), (), s32[]{:S(2)}) async-start(), calls=%async_computation.21 | async-start | bytes 5242880 | tf_op jit(solution)/shard_map/reduce_scatter | solution.py:179
  921.8 306.9 %copy-start.32 = (f32[8,1,256]{2,1,0:T(1,128)S(1)}, f32[8,1,256]{2,1,0:T(1,128)}, u32[]{:S(2)}) copy-start(f32[8,1,256]{2,1,0:T(1,128)} %copy-done.31) | copy-start | bytes 24580
  (20 other events, 40.2 us)
Sparse Core Ops, SparseCore 0:
  9.6 83.4 all-gather.13
  94.9 21.8 all-gather.17
  118.7 27.7 all-gather.19
  148.3 23.3 all-gather.15
  173.4 28.0 all-gather.21
  207.7 76.7 reduce-scatter.11
  286.5 45.8 all-gather.27
  334.5 80.7 all-gather.23
  417.2 43.8 all-gather.25
  462.5 80.7 all-gather.31
  545.1 45.0 all-gather.29
  625.0 76.7 reduce-scatter.15
  707.5 81.2 all-gather.33
  792.0 60.0 reduce-scatter.31
  855.4 61.7 reduce-scatter.29
  920.4 61.7 reduce-scatter.27
  985.2 35.9 reduce-scatter.23
  1024.3 35.9 reduce-scatter.21
  1063.5 41.1 reduce-scatter.25
  1108.4 41.1 reduce-scatter.19
  1151.9 76.7 reduce-scatter.17
  1231.0 77.5 reduce-scatter.13
where the time goes:
time: 1330 us; the launch traced here: 1320 us
  waiting for transfers between devices  920 us (69%)
  matrix products  246 us (18%)
  other arithmetic  60.5 us (5%)
  blocking collectives  58.4 us (4%)
  between operations  18.2 us (1%)
  local copies, waits for them, and re-layouts  16.2 us (1%)
    all_gather x1, waiting for transfers between devices, per_device(): lax.all_gather(norm_gain(middle, second_gain).astype(jnp.bfloat16), 'tp',...  82.9 us
    reduce_scatter x1, waiting for transfers between devices, per_device(): lax.psum_scatter(grad_normed.astype(jnp.bfloat16), 'tp', scatter_dimensio...  77.3 us
    reduce_scatter x1, waiting for transfers between devices, per_device(): lax.psum_scatter(grad_branch.astype(jnp.bfloat16), 'tp', scatter_dimensio...  76.9 us
    all_gather x1, waiting for transfers between devices, per_device(): grad_all = lax.all_gather(grad_out, 'tp', axis=0, tiled=True)  70.5 us
    reduce_scatter x1, waiting for transfers between devices, per_device(): lax.psum_scatter(attn_part.astype(jnp.bfloat16), 'tp', scatter_dimension=...  67.2 us
    reduce_scatter x1, waiting for transfers between devices, per_device(): lax.psum_scatter(grad_w_gate.astype(jnp.bfloat16), 'fsdp', scatter_dimens...  55.6 us
    reduce_scatter x1, waiting for transfers between devices, per_device(): lax.psum_scatter(ffn_part.astype(jnp.bfloat16), 'tp', scatter_dimension=0...  51 us
    all_gather x1, waiting for transfers between devices, per_device(): tokens_all = lax.all_gather(hidden_in, 'tp', axis=0, tiled=True)  50.8 us
  transfers between devices with their start and end apart: 22, of which 20 were waited for; matrix products, arithmetic and copies ran while one was open for 20% of the time, Pallas kernels for 0%

commit v1 on v0

v1 whole, which is shorter than its diff:
```python
import functools
import math

import jax
import jax.numpy as jnp
from jax import lax
from jax.experimental import pallas as pl
from jax.experimental.pallas import tpu as pltpu
from jax.sharding import PartitionSpec as P

MESH = pl.DeviceIdType.MESH

HD = 128


EPS = 1e-06
ROPE_BASE = 1000000.0


def rms_scale(value):
    return lax.rsqrt(jnp.mean(value * value, axis=-1, keepdims=True) + EPS)


def norm_gain(value, gain):
    return value * rms_scale(value) * gain


def rope_tables(places):
    half = HD // 2
    ladder = jnp.arange(half, dtype=jnp.float32) * (2.0 / HD)
    frequency = jnp.exp(-ladder * math.log(ROPE_BASE))
    angle = places.astype(jnp.float32)[:, None] * frequency[None, :]
    return (jnp.cos(angle)[:, None, :], jnp.sin(angle)[:, None, :])


def rotate(value, cosine, sine):
    half = value.shape[-1] // 2
    first = value[..., :half]
    second = value[..., half:]
    return jnp.concatenate(
        [first * cosine - second * sine, second * cosine + first * sine], axis=-1
    )


def head_prep(raw, gain, cosine, sine):
    return rotate(norm_gain(raw, gain), cosine, sine)


def visibility(length, prefix):
    places = jnp.arange(length, dtype=jnp.int32)
    return (places[None, :] <= places[:, None]) | (places[None, :] < prefix)


def masked_scores(query, keys, prefix):
    scale = 1.0 / math.sqrt(HD)
    scores = jnp.einsum("qkgd,pkd->kgqp", query, keys, preferred_element_type=jnp.float32) * scale
    return jnp.where(visibility(query.shape[0], prefix), scores, -1e30)


def attend_forward(item):
    query, keys, values, prefix = item
    scores = masked_scores(query, keys, prefix)
    peak = jnp.max(scores, axis=-1, keepdims=True)
    raised = jnp.exp(scores - peak)
    total = jnp.sum(raised, axis=-1, keepdims=True)
    shares = raised / total
    mixed = jnp.einsum(
        "kgqp,pkd->qkgd", shares.astype(jnp.bfloat16), values, preferred_element_type=jnp.float32
    )
    return (mixed, (peak + jnp.log(total))[..., 0])


def attend_backward(item):
    query, keys, values, grad_mixed, log_total, prefix = item
    scale = 1.0 / math.sqrt(HD)
    scores = masked_scores(query, keys, prefix)
    shares = jnp.exp(scores - log_total[..., None])
    grad_shares = jnp.einsum(
        "qkgd,pkd->kgqp", grad_mixed, values, preferred_element_type=jnp.float32
    )
    grad_scores = shares * (grad_shares - jnp.sum(grad_shares * shares, axis=-1, keepdims=True))
    grad_low = (grad_scores * scale).astype(jnp.bfloat16)
    grad_query = jnp.einsum("kgqp,pkd->qkgd", grad_low, keys, preferred_element_type=jnp.float32)
    grad_keys = jnp.einsum("kgqp,qkgd->pkd", grad_low, query, preferred_element_type=jnp.float32)
    grad_values = jnp.einsum(
        "kgqp,qkgd->pkd",
        shares.astype(jnp.bfloat16),
        grad_mixed,
        preferred_element_type=jnp.float32,
    )
    return (grad_query, grad_keys, grad_values)


def greet(me, n, axis):
    barrier = pltpu.get_barrier_semaphore()
    for d in (1, -1):
        @pl.when((me + d >= 0) & (me + d < n))
        def _():
            pl.semaphore_signal(barrier, inc=1, device_id={axis: me + d}, device_id_type=MESH)
    edge = (me == 0) | (me == n - 1)

    @pl.when(edge)
    def _():
        pl.semaphore_wait(barrier, 1)

    @pl.when(~edge)
    def _():
        pl.semaphore_wait(barrier, 2)

def inside(v, n):
    return (v >= 0) & (v < n)

def ag_kernel(n, S, axis, x_ref, o_ref, send_sem, recv_sem):
    me = lax.axis_index(axis)
    R = x_ref.shape[0]; sub = R // S
    greet(me, n, axis)
    def rows(j, s):
        return pl.ds(pl.multiple_of(j * R + s * sub, sub), sub)
    def item(di, d, k, s, sender):
        j = sender - d * k
        src = x_ref.at[pl.ds(s * sub, sub)] if k == 0 else o_ref.at[rows(j, s)]
        return pltpu.make_async_remote_copy(src_ref=src, dst_ref=o_ref.at[rows(j, s)], send_sem=send_sem.at[di, k, s], recv_sem=recv_sem.at[di, k, s], device_id={axis: sender + d}, device_id_type=MESH)
    for k in range(n):
        for s in range(S):
            for di, d in enumerate((1, -1)):
                if k > 0:
                    @pl.when(inside(me - d * k, n))
                    def _():
                        item(di, d, k - 1, s, me - d).wait_recv()
                if k < n - 1:
                    @pl.when(inside(me - d * k, n) & inside(me + d, n))
                    def _():
                        item(di, d, k, s, me).start()
        if k == 0:
            o_ref[pl.ds(pl.multiple_of(me * R, R), R), :] = x_ref[...]
    for k in range(n - 1):
        for s in range(S):
            for di, d in enumerate((1, -1)):
                @pl.when(inside(me - d * k, n) & inside(me + d, n))
                def _():
                    item(di, d, k, s, me).wait_send()

def ag(x, n, S=2, axis="tp", cid=1):
    R, D = x.shape
    return pl.pallas_call(functools.partial(ag_kernel, n, S, axis),
        out_shape=jax.ShapeDtypeStruct((n * R, D), x.dtype),
        in_specs=[pl.BlockSpec(memory_space=pltpu.VMEM)],
        out_specs=pl.BlockSpec(memory_space=pltpu.VMEM),
        scratch_shapes=[pltpu.SemaphoreType.DMA((2, n - 1, S)), pltpu.SemaphoreType.DMA((2, n - 1, S))],
        compiler_params=pltpu.CompilerParams(collective_id=cid, has_side_effects=True, vmem_limit_bytes=32 << 20), name="ag")(x)

def rs_kernel(n, S, axis, p_ref, o_ref, rb, send_sem, recv_sem):
    me = lax.axis_index(axis)
    R = o_ref.shape[0]; sub = R // S
    greet(me, n, axis)
    def rows(j, s):
        return pl.ds(pl.multiple_of(j * R + s * sub, sub), sub)
    def at(s):
        return pl.ds(s * sub, sub)
    def owner(d, q):
        return n - 1 - q if d > 0 else q
    def item(di, d, q, s, sender, first):
        src = p_ref.at[rows(owner(d, q), s)] if first else rb.at[di, q, at(s)]
        return pltpu.make_async_remote_copy(src_ref=src, dst_ref=rb.at[di, q, at(s)], send_sem=send_sem.at[di, q, s], recv_sem=recv_sem.at[di, q, s], device_id={axis: sender + d}, device_id_type=MESH)
    ways = ((0, 1, me), (1, -1, n - 1 - me))
    for q in range(n - 1):
        for s in range(S):
            for di, d, dist in ways:
                @pl.when(dist == 0)
                def _():
                    item(di, d, q, s, me, True).start()
    for t in range(1, n - 1):
        for s in range(S):
            for di, d, dist in ways:
                @pl.when((dist > 0) & (t >= dist))
                def _():
                    q = t - dist
                    item(di, d, q, s, me - d, False).wait_recv()
                    rb[di, q, at(s), :] = (rb[di, q, at(s), :].astype(jnp.float32) + p_ref[rows(owner(d, q), s), :].astype(jnp.float32)).astype(rb.dtype)
                    item(di, d, q, s, me, False).start()
    for s in range(S):
        for di, d, dist in ways:
            @pl.when(dist > 0)
            def _():
                item(di, d, n - 1 - dist, s, me - d, False).wait_recv()
        @pl.when(me == 0)
        def _():
            o_ref[at(s), :] = p_ref[rows(0, s), :].astype(jnp.float32) + rb[1, 0, at(s), :].astype(jnp.float32)
        @pl.when(me == n - 1)
        def _():
            o_ref[at(s), :] = p_ref[rows(n - 1, s), :].astype(jnp.float32) + rb[0, 0, at(s), :].astype(jnp.float32)
        @pl.when((me > 0) & (me < n - 1))
        def _():
            o_ref[at(s), :] = p_ref[rows(me, s), :].astype(jnp.float32) + rb[0, n - 1 - me, at(s), :].astype(jnp.float32) + rb[1, me, at(s), :].astype(jnp.float32)
    for t in range(0, n - 1):
        for s in range(S):
            for di, d, dist in ways:
                @pl.when(t >= dist)
                def _():
                    item(di, d, t - dist, s, me, False).wait_send()

def rs(p, n, S=2, axis="tp", cid=2):
    NR, D = p.shape; R = NR // n
    return pl.pallas_call(functools.partial(rs_kernel, n, S, axis),
        out_shape=jax.ShapeDtypeStruct((R, D), jnp.float32),
        in_specs=[pl.BlockSpec(memory_space=pltpu.VMEM)],
        out_specs=pl.BlockSpec(memory_space=pltpu.VMEM),
        scratch_shapes=[pltpu.VMEM((2, n - 1, R, D), p.dtype), pltpu.SemaphoreType.DMA((2, n - 1, S)), pltpu.SemaphoreType.DMA((2, n - 1, S))],
        compiler_params=pltpu.CompilerParams(collective_id=cid, has_side_effects=True, vmem_limit_bytes=32 << 20), name="rs")(p)

def per_device(
    hidden_in,
    grad_out,
    prefix_len,
    positions,
    g_attn,
    w_query,
    w_key,
    w_value,
    w_out,
    q_gain,
    k_gain,
    g_ffn,
    w_gate,
    w_up,
    w_down,
):
    parts = lax.axis_size("tp")
    groups = lax.axis_size("fsdp")
    own_rows, width = hidden_in.shape
    group_rows = own_rows * parts
    count = prefix_len.shape[0]
    length = group_rows // count
    qc, kc, fc = w_query.shape[1], w_key.shape[1], w_gate.shape[1]
    slot = g_attn.shape[0]
    head_slot = q_gain.shape[0]
    packed = jnp.concatenate([g_attn, g_ffn, q_gain, k_gain])[None]
    gains = lax.all_gather(packed, "fsdp", axis=0, tiled=True).astype(jnp.float32)
    first_gain = gains[:, :slot].reshape(-1)
    second_gain = gains[:, slot : 2 * slot].reshape(-1)
    query_gain = gains[:, 2 * slot : 2 * slot + head_slot].reshape(-1)
    key_gain = gains[:, 2 * slot + head_slot :].reshape(-1)
    attn_set = lax.all_gather(
        jnp.concatenate([w_query, w_key, w_value, w_out.T], axis=1), "fsdp", axis=0, tiled=True
    )
    full_qkv = attn_set[:, : qc + 2 * kc]
    full_out = attn_set[:, qc + 2 * kc :]
    ffn_set = lax.all_gather(
        jnp.concatenate([w_gate, w_up, w_down.T], axis=1), "fsdp", axis=0, tiled=True
    )
    full_gate, full_up, full_down = ffn_set[:, :fc], ffn_set[:, fc : 2 * fc], ffn_set[:, 2 * fc :]

    tokens_all = ag(hidden_in, parts, cid=1)
    tokens_float = tokens_all.astype(jnp.float32)
    own_float = hidden_in.astype(jnp.float32)
    normed = norm_gain(tokens_float, first_gain).astype(jnp.bfloat16)
    raw = jnp.dot(normed, full_qkv, preferred_element_type=jnp.float32)
    query_raw = raw[:, :qc].reshape(group_rows, -1, HD)
    keys_raw = raw[:, qc : qc + kc].reshape(group_rows, -1, HD)
    values_low = raw[:, qc + kc :].astype(jnp.bfloat16).reshape(group_rows, -1, HD)
    kv_local = keys_raw.shape[1]
    grouping = query_raw.shape[1] // kv_local
    cosine, sine = rope_tables(positions)
    query_low = head_prep(query_raw, query_gain, cosine, sine).astype(jnp.bfloat16)
    keys_low = head_prep(keys_raw, key_gain, cosine, sine).astype(jnp.bfloat16)
    query_seq = query_low.reshape(count, length, kv_local, grouping, HD)
    keys_seq = keys_low.reshape(count, length, kv_local, HD)
    values_seq = values_low.reshape(count, length, kv_local, HD)
    mixed, log_total = lax.map(attend_forward, (query_seq, keys_seq, values_seq, prefix_len))
    mixed_low = mixed.reshape(group_rows, -1).astype(jnp.bfloat16)
    attn_part = jnp.einsum("th,dh->td", mixed_low, full_out, preferred_element_type=jnp.float32)
    middle = own_float + rs(attn_part.astype(jnp.bfloat16), parts, cid=2)
    branch = ag(norm_gain(middle, second_gain).astype(jnp.bfloat16), parts, cid=3)
    gate = jnp.dot(branch, full_gate, preferred_element_type=jnp.float32)
    upward = jnp.dot(branch, full_up, preferred_element_type=jnp.float32)
    sigmoid_gate = jax.nn.sigmoid(gate)
    silu_gate = gate * sigmoid_gate
    product = (silu_gate * upward).astype(jnp.bfloat16)
    ffn_part = jnp.einsum("tf,df->td", product, full_down, preferred_element_type=jnp.float32)
    result = middle + lax.psum_scatter(
        ffn_part.astype(jnp.bfloat16), "tp", scatter_dimension=0, tiled=True
    ).astype(jnp.float32)
    out = result.astype(jnp.bfloat16)
    grad_all = lax.all_gather(grad_out, "tp", axis=0, tiled=True)
    grad_product = jnp.dot(grad_all, full_down, preferred_element_type=jnp.float32)
    grad_w_down = jnp.einsum("td,tf->df", grad_all, product, preferred_element_type=jnp.float32)
    grad_gate = (
        grad_product * upward * (sigmoid_gate * (1.0 + gate * (1.0 - sigmoid_gate)))
    ).astype(jnp.bfloat16)
    grad_up = (grad_product * silu_gate).astype(jnp.bfloat16)
    grad_w_gate = jnp.einsum("td,tf->df", branch, grad_gate, preferred_element_type=jnp.float32)
    grad_w_up = jnp.einsum("td,tf->df", branch, grad_up, preferred_element_type=jnp.float32)
    grad_branch = jnp.einsum("tf,df->td", grad_gate, full_gate, preferred_element_type=jnp.float32)
    grad_branch = grad_branch + jnp.einsum(
        "tf,df->td", grad_up, full_up, preferred_element_type=jnp.float32
    )
    grad_branch_own = rs(grad_branch.astype(jnp.bfloat16), parts, cid=4)
    unused_second, pull_second = jax.vjp(norm_gain, middle, second_gain)
    grad_mid_norm, grad_second = pull_second(grad_branch_own)
    grad_middle = grad_out.astype(jnp.float32) + grad_mid_norm
    grad_mid_all = ag(grad_middle.astype(jnp.bfloat16), parts, cid=5)

    def spread(value):
        return lax.psum_scatter(
            value.astype(jnp.bfloat16), "fsdp", scatter_dimension=0, tiled=True
        ).astype(jnp.float32)

    down_own = spread(grad_w_down)
    gate_own = spread(grad_w_gate)
    up_own = spread(grad_w_up)
    grad_mixed = jnp.dot(grad_mid_all, full_out, preferred_element_type=jnp.float32).astype(
        jnp.bfloat16
    )
    grad_w_out = jnp.einsum(
        "td,th->dh", grad_mid_all, mixed_low, preferred_element_type=jnp.float32
    )
    grad_mixed_seq = grad_mixed.reshape(count, length, kv_local, grouping, HD)
    grads_query, grads_keys, grads_values = lax.map(
        attend_backward, (query_seq, keys_seq, values_seq, grad_mixed_seq, log_total, prefix_len)
    )
    unused_query, pull_query = jax.vjp(
        functools.partial(head_prep, cosine=cosine, sine=sine), query_raw, query_gain
    )
    grad_query_raw, grad_q_gain = pull_query(grads_query.reshape(group_rows, -1, HD))
    unused_keys, pull_keys = jax.vjp(
        functools.partial(head_prep, cosine=cosine, sine=sine), keys_raw, key_gain
    )
    grad_keys_raw, grad_k_gain = pull_keys(grads_keys.reshape(group_rows, -1, HD))
    grad_qkv = jnp.concatenate(
        [
            grad_query_raw.reshape(group_rows, -1),
            grad_keys_raw.reshape(group_rows, -1),
            grads_values.reshape(group_rows, -1),
        ],
        axis=1,
    ).astype(jnp.bfloat16)
    grad_w_qkv = jnp.einsum("td,th->dh", normed, grad_qkv, preferred_element_type=jnp.float32)
    grad_normed = jnp.einsum("th,dh->td", grad_qkv, full_qkv, preferred_element_type=jnp.float32)
    out_own = spread(grad_w_out)
    qkv_own = spread(grad_w_qkv)
    grad_normed_own = rs(grad_normed.astype(jnp.bfloat16), parts, cid=6)
    unused_first, pull_first = jax.vjp(norm_gain, own_float, first_gain)
    grad_tokens, grad_first = pull_first(grad_normed_own)
    grad_in = grad_middle + grad_tokens
    sums = lax.psum(
        jnp.concatenate([grad_first, grad_second, grad_q_gain, grad_k_gain]), ("fsdp", "tp")
    )
    place = lax.axis_index("fsdp")
    wide = groups * slot
    narrow = groups * head_slot
    gain_first = lax.dynamic_slice_in_dim(sums, place * slot, slot)
    gain_second = lax.dynamic_slice_in_dim(sums, wide + place * slot, slot)
    gain_query = lax.dynamic_slice_in_dim(sums, 2 * wide + place * head_slot, head_slot)
    gain_key = lax.dynamic_slice_in_dim(sums, 2 * wide + narrow + place * head_slot, head_slot)
    return (
        out,
        grad_in,
        gain_first,
        qkv_own[:, :qc],
        qkv_own[:, qc : qc + kc],
        qkv_own[:, qc + kc :],
        out_own.T,
        gain_query,
        gain_key,
        gain_second,
        gate_own,
        up_own,
        down_own.T,
    )


def solution(mesh):
    in_specs = (
        P(("fsdp", "tp"), None),
        P(("fsdp", "tp"), None),
        P("fsdp"),
        P("fsdp"),
        P("fsdp"),
        P("fsdp", "tp"),
        P("fsdp", "tp"),
        P("fsdp", "tp"),
        P("tp", "fsdp"),
        P("fsdp"),
        P("fsdp"),
        P("fsdp"),
        P("fsdp", "tp"),
        P("fsdp", "tp"),
        P("tp", "fsdp"),
    )
    out_specs = (
        P(("fsdp", "tp"), None),
        P(("fsdp", "tp"), None),
        P("fsdp"),
        P("fsdp", "tp"),
        P("fsdp", "tp"),
        P("fsdp", "tp"),
        P("tp", "fsdp"),
        P("fsdp"),
        P("fsdp"),
        P("fsdp"),
        P("fsdp", "tp"),
        P("fsdp", "tp"),
        P("tp", "fsdp"),
    )
    return jax.shard_map(
        per_device, mesh=mesh, in_specs=in_specs, out_specs=out_specs, check_vma=False
    )
```

time: 1330 us -> 1090 us (0.82)
  waiting for transfers between devices: 920 us -> 151 us
  Pallas kernels: 0 us -> 505 us
  blocking collectives: 58.4 us -> 94.8 us
  local copies, waits for them, and re-layouts: 16.2 us -> 40.7 us
  matrix products: 246 us -> 222 us
    pallas_call x0 -> x6, Pallas kernels: none -> 505 us  [the longest x3 272 us: ag(): pl.pallas_call(functools.partial(ag_kernel, n, S, axis), out_shape=jax.Sh...]
    all_gather x10 -> x2, waiting for transfers between devices: 356 us -> 0.02 us  [the longest x1 0.02 us: per_device(): lax.all_gather(jnp.concatenate([w_gate, w_up, w_down.T], axis=1), 'fsdp',...]
    reduce_scatter x10 -> x5, waiting for transfers between devices: 437 us -> 150 us  [spread(): lax.psum_scatter(value.astype(jnp.bfloat16), 'fsdp', scatter_dimension=0,...]
    all_gather x1, waiting for transfers between devices: 70.5 us -> 0.02 us  [per_device(): grad_all = lax.all_gather(grad_out, 'tp', axis=0, tiled=True)]
    psum x1, blocking collectives: 12.6 us -> 68.2 us  [per_device(): lax.psum(jnp.concatenate([grad_first, grad_second, grad_q_gain, grad_k_ga...]
    reduce_scatter x1, waiting for transfers between devices: 51 us -> 0.01 us  [per_device(): lax.psum_scatter(ffn_part.astype(jnp.bfloat16), 'tp', scatter_dimension=0...]
    dot_general x15 -> x9, matrix products: 89.8 us -> 71.4 us  [the longest x1 12 us: per_device(): jnp.dot(grad_all, full_down, preferred_element_type=jnp.float32)]
    convert_element_type x17 -> x3, other arithmetic: 22.8 us -> 5.53 us  [the longest x2 4.92 us: spread(): return lax.psum_scatter(value.astype(jnp.bfloat16), 'fsdp', scatter_dimen...]
  transfers between devices with their start and end apart: 22 -> 9, of which waited for: 20 -> 3; matrix products, arithmetic and copies ran while one was open for 20% -> 16% of each run, Pallas kernels for 0% -> 35%
where the time goes in v1:
time: 1090 us; the launch traced here: 1080 us
  Pallas kernels  505 us (46%)
  matrix products  222 us (20%)
  waiting for transfers between devices  151 us (14%)
  blocking collectives  94.8 us (9%)
  other arithmetic  50.8 us (5%)
  local copies, waits for them, and re-layouts  40.7 us (4%)
  between operations  16.3 us (1%)
    pallas_call x3, Pallas kernels, ag(): pl.pallas_call(functools.partial(ag_kernel, n, S, axis), out_shape=jax.Sh...  272 us
    pallas_call x3, Pallas kernels, rs(): pl.pallas_call(functools.partial(rs_kernel, n, S, axis), out_shape=jax.Sh...  233 us
    reduce_scatter x5, waiting for transfers between devices, spread(): lax.psum_scatter(value.astype(jnp.bfloat16), 'fsdp', scatter_dimension=0,...  150 us
    psum x1, blocking collectives, per_device(): lax.psum(jnp.concatenate([grad_first, grad_second, grad_q_gain, grad_k_ga...  68.2 us
    unnamed x1, blocking collectives  26.6 us
    dot_general x1, matrix products, attend_backward(): jnp.einsum('kgqp,pkd->qkgd', grad_low, keys, preferred_element_type=jnp.f...  25 us
    dot_general x1, matrix products, attend_backward(): jnp.einsum('kgqp,qkgd->pkd', grad_low, query, preferred_element_type=jnp....  24 us
    unnamed x124, local copies, waits for them, and re-layouts  23.1 us
  transfers between devices with their start and end apart: 9, of which 3 were waited for; matrix products, arithmetic and copies ran while one was open for 16% of the time, Pallas kernels for 35%

profile of v1, /device:TPU:0, one launch (start us, length us, event | category | flops | bytes accessed | tf_op | source)
XLA Modules:
  0.0 1081.2 jit_solution(17816373039922285229)
XLA Ops:
  10.5 1.9 pad_maximum_fusion.5
  18.9 26.6 %all-reduce.4 = bf16[4352]{0:T(1024)(128)(2,1)S(1)} all-reduce(bf16[4352]{0:T(1024)(128)(2,1)S(1)} %dynamic-update-slice), channel_id=2, replica_groups=mesh['fsdp'=8,'tp'=4] {'fsdp'}, use_global_device_ids=true, to_apply=%add.4 | all-reduce | flops 4352 | bytes 17408
  48.8 135.7 %ag.3 = bf16[1024,2048]{1,0:T(8,128)(2,1)S(1)} custom-call(bf16[256,2048]{1,0:T(8,128)(2,1)S(1)} %copy-done.3), custom_call_target="tpu_custom_call" | custom-call | tf_op jit(solution)/shard_map/ag/pallas_call | solution.py:145
  184.5 2.3 copy-done.1
  189.0 8.2 fusion.38
  204.3 2.0 multiply_multiply_fusion
  207.5 2.4 copy.81
  215.3 9.6 fusion.84
  225.0 8.7 fusion.4
  233.7 8.1 fusion.52
  241.8 4.4 convolution_convert_fusion.3.p_ref
  246.2 65.2 %rs.3 = f32[256,2048]{1,0:T(8,128)S(1)} custom-call(bf16[1024,2048]{1,0:T(8,128)(2,1)S(1)} %convolution_convert_fusion.3.p_ref), custom_call_target="tpu_custom_call" | custom-call | tf_op jit(solution)/shard_map/rs/pallas_call | solution.py:204
  314.0 69.5 %ag.4 = bf16[1024,2048]{1,0:T(8,128)(2,1)S(1)} custom-call(bf16[256,2048]{1,0:T(8,128)(2,1)S(1)} %multiply_convert_fusion.1.x_ref), custom_call_target="tpu_custom_call" | custom-call | tf_op jit(solution)/shard_map/ag/pallas_call | solution.py:145
  383.5 1.9 copy-done.5
  385.6 12.0 %fusion.18 = f32[1536,1024]{0,1:T(8,128)} fusion(bf16[1024,2048]{1,0:T(8,128)(2,1)} %all-gather.9.cloned.1.call-done, bf16[2048,4608]{0,1:T(8,128)(2,1)} %all-gather.7.cloned.1.call-done), kind=kOutput, calls=%fused_computation.33 | convolution fusion | flops 6442450944 | bytes 16777216 | tf_op jit(solution)/shard_map/dot_general | solution.py:285
  397.5 8.8 fusion.28
  406.3 14.9 %fusion.15 = (bf16[1024,1536]{1,0:T(8,128)(2,1)}, bf16[1024,1536]{1,0:T(8,128)(2,1)}, bf16[1024,1536]{1,0:T(8,128)(2,1)}) fusion(f32[1536,1024]{0,1:T(8,128)} %fusion.18, f32[1024,1536]{1,0:T(8,128)S(1)} %fusion.28, bf16[1024,2048]{1,0:T(8,128)(2,1)S(1)} %copy-done.6, bf16[2048,4608]{0,1:T(8,128)(2,1)} %all-gather.7.cloned.1.call-done), kind=kOutput, calls=%fused_computation.28 | convolution fusion | flops 6466043904 | bytes 32505856 | tf_op jit(solution)/shard_map/dot_general | solution.py:275
  421.2 9.8 fusion.22
  431.1 8.9 add_convert_fusion.p_ref
  440.0 64.4 %rs.4 = f32[256,2048]{1,0:T(8,128)S(1)} custom-call(bf16[1024,2048]{1,0:T(8,128)(2,1)S(1)} %add_convert_fusion.p_ref), custom_call_target="tpu_custom_call" | custom-call | tf_op jit(solution)/shard_map/rs/pallas_call | solution.py:204
  505.6 66.4 %ag.5 = bf16[1024,2048]{1,0:T(8,128)(2,1)S(1)} custom-call(bf16[256,2048]{1,0:T(8,128)(2,1)S(1)} %fusion.79.x_ref), custom_call_target="tpu_custom_call" | custom-call | tf_op jit(solution)/shard_map/ag/pallas_call | solution.py:145
  572.1 2.0 copy-done.7
  574.1 3.7 convolution_convert_fusion.6
  577.8 5.3 fusion.53
  584.0 8.2 fusion.85
  592.2 24.0 %fusion.56 = f32[1024,2,128]{2,0,1:T(8,128)} fusion(f32[2,1024,1024,2]{2,1,3,0:T(8,128)} %fusion.85, f32[2,2,1024,1024]{2,3,1,0:T(8,128)} %get-tuple-element.140, f32[2,2,1024]{2,1,0:T(2,128)S(1)} %log_add_fusion, bf16[1024,2,2,64]{3,0,2,1:T(8,128)(2,1)} %bitcast.130, bf16[1024,2,2,64]{3,0,2,1:T(8,128)(2,1)} %bitcast.128), kind=kOutput, calls=%fused_computation.92 | convolution fusion | flops 1105204224 | bytes 35667968 | tf_op jit(solution)/shard_map/while/body/eval_jaxpr/kgqp,qkgd->pkd/dot_general | solution.py:84
  616.2 25.0 %fusion.32 = f32[2,128,2,1024]{3,1,2,0:T(8,128)} fusion(f32[2,1024,1024,2]{2,1,3,0:T(8,128)} %fusion.85, f32[2,2,1024,1024]{2,3,1,0:T(8,128)} %get-tuple-element.140, f32[2,2,1024]{2,1,0:T(2,128)S(1)} %log_add_fusion, bf16[1024,2,64]{2,0,1:T(8,128)(2,1)} %copy-done.32, bf16[1024,2,64]{2,0,1:T(8,128)(2,1)} %copy-done.31), kind=kOutput, calls=%fused_computation.47 | convolution fusion | flops 1104155648 | bytes 36192256 | tf_op jit(solution)/shard_map/while/body/eval_jaxpr/kgqp,pkd->qkgd/dot_general | solution.py:83
  641.6 2.0 multiply_add_fusion.3
  649.9 2.1 copy.96
  652.1 2.8 fusion.43
  655.0 9.6 fusion.60
  665.4 8.4 convolution_convert_fusion.4
  673.9 11.1 %fusion.34 = bf16[1024,2048]{1,0:T(8,128)(2,1)} fusion(bf16[1024,1536]{1,0:T(8,128)(2,1)} %get-tuple-element.115, bf16[2048,4608]{0,1:T(8,128)(2,1)} %all-gather.7.cloned.1.call-done), kind=kOutput, calls=%fused_computation.55 | convolution fusion | flops 6444548096 | bytes 13631488 | tf_op jit(solution)/shard_map/tf,df->td/dot_general | solution.py:279
  685.5 11.7 %convolution_convert_fusion.2 = bf16[2048,1536]{1,0:T(8,128)(2,1)} fusion(bf16[1024,2048]{1,0:T(8,128)(2,1)} %copy-done.5, bf16[1024,1536]{1,0:T(8,128)(2,1)} %get-tuple-element.113), kind=kOutput, calls=%fused_computation.23 | convolution fusion | flops 6445596672 | bytes 13631488 | tf_op jit(solution)/shard_map/td,tf->df/dot_general | solution.py:291
  697.3 11.3 %fusion.13 = bf16[2048,1536]{0,1:T(8,128)(2,1)} fusion(bf16[1024,1536]{1,0:T(8,128)(2,1)} %get-tuple-element.115, bf16[1024,2048]{1,0:T(8,128)(2,1)} %all-gather.9.cloned.1.call-done), kind=kOutput, calls=%fused_computation.24 | convolution fusion | flops 6445596672 | bytes 13631488 | tf_op jit(solution)/shard_map/td,tf->df/dot_general | solution.py:286
  708.8 11.8 %convolution_convert_fusion.1 = bf16[2048,1536]{1,0:T(8,128)(2,1)} fusion(bf16[1024,2048]{1,0:T(8,128)(2,1)} %copy-done.5, bf16[1024,1536]{1,0:T(8,128)(2,1)} %get-tuple-element.114), kind=kOutput, calls=%fused_computation.22 | convolution fusion | flops 6445596672 | bytes 13631488 | tf_op jit(solution)/shard_map/td,tf->df/dot_general | solution.py:292
  721.8 7.1 convolution_convert_fusion.5.p_ref
  728.9 103.5 %rs.5 = f32[256,2048]{1,0:T(8,128)S(1)} custom-call(bf16[1024,2048]{1,0:T(8,128)(2,1)S(1)} %convolution_convert_fusion.5.p_ref), custom_call_target="tpu_custom_call" | custom-call | tf_op jit(solution)/shard_map/rs/pallas_call | solution.py:204
  834.5 68.2 %psum.7 = f32[4352]{0:T(1024)S(1)} all-reduce(f32[4352]{0:T(1024)S(1)} %pad_maximum_fusion.8), channel_id=1, replica_groups=mesh['fsdp'=8,'tp'=4] {'fsdp','tp'}, use_global_device_ids=true, to_apply=%region_17.18 | all-reduce | flops 4352 | bytes 34816 | tf_op jit(solution)/shard_map/psum | solution.py:345
  904.0 1.9 convert_bitcast_fusion.1
  905.9 2.0 copy.98
  911.5 5.7 fusion.44
  917.2 24.7 %reduce-scatter.13.cloned.1.call-done = bf16[256,1536]{1,0:T(8,128)(2,1)} async-done(((bf16[2048,1536]{1,0:T(8,128)(2,1)}), bf16[256,1536]{1,0:T(8,128)(2,1)}) %reduce-scatter.13.cloned.1.call-update) | async-done | bytes 786448 | tf_op jit(solution)/shard_map/reduce_scatter | solution.py:304
  941.9 2.5 convert_element_type.137
  944.3 62.5 %reduce-scatter.17.cloned.1.call-done = bf16[256,1536]{0,1:T(8,128)(2,1)} async-done(((bf16[2048,1536]{0,1:T(8,128)(2,1)}), bf16[256,1536]{0,1:T(8,128)(2,1)}) %reduce-scatter.17.cloned.1.call-update) | async-done | bytes 786448 | tf_op jit(solution)/shard_map/reduce_scatter | solution.py:304
  1006.9 2.4 convert_bitcast_fusion
  1009.3 62.8 %reduce-scatter.15.cloned.1.call-done = bf16[256,1536]{1,0:T(8,128)(2,1)} async-done(((bf16[2048,1536]{1,0:T(8,128)(2,1)}), bf16[256,1536]{1,0:T(8,128)(2,1)}) %reduce-scatter.15.cloned.1.call-update) | async-done | bytes 786448 | tf_op jit(solution)/shard_map/reduce_scatter | solution.py:304
  1072.0 2.5 convert_element_type.139
  (193 shorter events, 48.6 us)
Async XLA Ops:
  7.2 6.0 copy-start.29
  7.2 7.8 copy-start.28
  7.2 181.8 %all-gather.5.cloned.1.call-start = ((), (), s32[]{:S(2)}) async-start(), calls=%async_computation.6 | async-start | bytes 7077888 | tf_op jit(solution)/shard_map/all_gather | solution.py:243
  12.4 373.1 %all-gather.9.cloned.1.call-start = ((), (), s32[]{:S(2)}) async-start(), calls=%async_computation.9 | async-start | bytes 5242880 | tf_op jit(solution)/shard_map/all_gather | solution.py:284
  13.1 372.4 %all-gather.7.cloned.1.call-start = ((), (), s32[]{:S(2)}) async-start(), calls=%async_computation.7 | async-start | bytes 21233664 | tf_op jit(solution)/shard_map/all_gather | solution.py:248
  13.5 3.8 copy-start.45
  13.5 3.9 copy-start.54
  13.5 5.1 copy-start.48
  13.5 5.1 copy-start.49
  13.5 5.1 copy-start.50
  13.5 5.1 copy-start.51
  15.0 33.8 %copy-start.3 = (bf16[256,2048]{1,0:T(8,128)(2,1)S(1)}, bf16[256,2048]{1,0:T(8,128)(2,1)}, u32[]{:S(2)}) copy-start(bf16[256,2048]{1,0:T(8,128)(2,1)} %x_ref.1) | copy-start | bytes 3145732
  16.6 887.4 %reduce-scatter.11.cloned.1.call-start = ((), (), s32[]{:S(2)}) async-start(), calls=%async_computation.11 | async-start | bytes 2359296 | tf_op jit(solution)/shard_map/reduce_scatter | solution.py:304
  45.8 157.4 %copy-start.43 = (f32[128]{0:T(128)}, f32[128]{0:T(128)S(1)}, u32[]{:S(2)}) copy-start(f32[128]{0:T(128)S(1)} %mul.476) | copy-start | bytes 1540
  45.8 143.2 %copy-start.40 = (f32[1,2,8,128]{3,1,2,0:T(2,128)}, f32[1,2,8,128]{3,1,2,0:T(2,128)S(1)}, u32[]{:S(2)}) copy-start(f32[1,2,8,128]{3,1,2,0:T(2,128)S(1)} %copy.117) | copy-start | bytes 24580
  46.8 159.5 %copy-start.17 = (f32[1024,64]{0,1:T(8,128)}, f32[1024,64]{0,1:T(8,128)S(1)}, u32[]{:S(2)}) copy-start(f32[1024,64]{0,1:T(8,128)S(1)} %get-tuple-element.138) | copy-start | bytes 786436
  187.7 9.5 copy-start.46
  197.2 2.5 copy-start.10
  211.2 4.1 copy-start.23
  211.2 4.1 copy-start.24
  211.2 4.1 copy-start.25
  215.2 9.7 copy-start.31
  215.2 9.7 copy-start.32
  225.0 8.7 copy-start.21
  241.8 4.4 copy-start.52
  385.5 12.0 %copy-start.6 = (bf16[1024,2048]{1,0:T(8,128)(2,1)S(1)}, bf16[1024,2048]{1,0:T(8,128)(2,1)}, u32[]{:S(2)}) copy-start(bf16[1024,2048]{1,0:T(8,128)(2,1)} %copy-done.5) | copy-start | bytes 12582916
  421.2 9.9 copy-start.55
  440.0 64.4 %copy-start.9 = (f32[256,2048]{1,0:T(8,128)S(1)}, f32[256,2048]{1,0:T(8,128)}, u32[]{:S(2)}) copy-start(f32[256,2048]{1,0:T(8,128)} %copy-done.8) | copy-start | bytes 6291460
  440.0 65.0 %copy-start.12 = (bf16[256,2048]{1,0:T(8,128)(2,1)S(1)}, bf16[256,2048]{1,0:T(8,128)(2,1)}, u32[]{:S(2)}) copy-start(bf16[256,2048]{1,0:T(8,128)(2,1)} %param.16) | copy-start | bytes 3145732
  505.6 68.4 %copy-start.53 = (bf16[2,128,2,1024]{3,1,2,0:T(8,128)(2,1)S(1)}, bf16[2,128,2,1024]{3,1,2,0:T(8,128)(2,1)}, u32[]{:S(2)}) copy-start(bf16[2,128,2,1024]{3,1,2,0:T(8,128)(2,1)} %copy-done.52) | copy-start | bytes 3145732
  577.8 6.3 copy-start.22
  641.3 266.6 %reduce-scatter.9.cloned.1.call-start = ((), (), s32[]{:S(2)}) async-start(), calls=%async_computation.10 | async-start | bytes 4718592 | tf_op jit(solution)/shard_map/reduce_scatter | solution.py:304
  643.8 3.0 copy-start.11
  643.8 3.6 slice-start
  643.8 3.6 copy-start.35
  643.9 3.6 copy-start.44
  647.5 4.6 copy-start.37
  649.9 5.0 copy-start.20
  654.9 9.7 copy-start.26
  654.9 10.5 copy-start.2
  654.9 10.5 copy-start.30
  654.9 10.5 copy-start.41
  655.0 10.5 copy-start.47
  673.8 237.7 %reduce-scatter.7.cloned.1.call-start = ((), (), s32[]{:S(2)}) async-start(), calls=%async_computation.8 | async-start | bytes 5242880 | tf_op jit(solution)/shard_map/reduce_scatter | solution.py:280
  685.0 256.9 %reduce-scatter.13.cloned.1.call-start = ((), (), s32[]{:S(2)}) async-start(), calls=%async_computation.12 | async-start | bytes 7077888 | tf_op jit(solution)/shard_map/reduce_scatter | solution.py:304
  697.2 309.7 %reduce-scatter.17.cloned.1.call-start = ((), (), s32[]{:S(2)}) async-start(), calls=%async_computation.14 | async-start | bytes 7077888 | tf_op jit(solution)/shard_map/reduce_scatter | solution.py:304
  708.6 363.4 %reduce-scatter.15.cloned.1.call-start = ((), (), s32[]{:S(2)}) async-start(), calls=%async_computation.13 | async-start | bytes 7077888 | tf_op jit(solution)/shard_map/reduce_scatter | solution.py:304
  728.9 104.8 %copy-start.4 = (bf16[256,2048]{1,0:T(8,128)(2,1)S(1)}, bf16[256,2048]{1,0:T(8,128)(2,1)}, u32[]{:S(2)}) copy-start(bf16[256,2048]{1,0:T(8,128)(2,1)} %x_ref.1) | copy-start | bytes 3145732
  (18 other events, 25.2 us)
Sparse Core Ops, SparseCore 0:
  12.5 49.4 all-gather.4
  63.6 112.5 all-gather.8
  178.0 102.2 all-gather.6
  641.4 52.1 reduce-scatter.10
  696.9 51.1 reduce-scatter.8
  750.2 109.6 reduce-scatter.6
  863.3 78.5 reduce-scatter.12
  945.2 61.5 reduce-scatter.16
  1010.3 61.7 reduce-scatter.14

commit v2 on v1

--- a/solution.py
+++ b/solution.py
@@ -9,6 +9,7 @@
 from jax.sharding import PartitionSpec as P
 
 MESH = pl.DeviceIdType.MESH
+VMEM_LIMIT = 67043328
 
 HD = 128
 
@@ -208,6 +209,210 @@
         scratch_shapes=[pltpu.VMEM((2, n - 1, R, D), p.dtype), pltpu.SemaphoreType.DMA((2, n - 1, S)), pltpu.SemaphoreType.DMA((2, n - 1, S))],
         compiler_params=pltpu.CompilerParams(collective_id=cid, has_side_effects=True, vmem_limit_bytes=32 << 20), name="rs")(p)
 
+def ffn_kernel(
+    n, axis, own_ref, go_ref, w_ref, gb_ref, part_ref, gw_ref,
+    branch, wbuf, act, gpart, rb, w_sem, out_sem, send_ag, recv_ag, send_rs, recv_rs,
+):
+    me = lax.axis_index(axis)
+    rows_own, width = own_ref.shape
+    hidden = wbuf.shape[2]
+    cut = hidden // 3
+    wcut = width // 4
+    loads = [
+        pltpu.make_async_copy(w_ref.at[:, pl.ds(m * hidden, hidden)], wbuf.at[m], w_sem.at[m])
+        for m in range(3)
+    ]
+    for load in loads:
+        load.start()
+    greet(me, n, axis)
+
+    def block(j):
+        return pl.ds(pl.multiple_of(j * rows_own, rows_own), rows_own)
+
+    def passing(di, d, k, sender):
+        j = sender - d * k
+        return pltpu.make_async_remote_copy(
+            src_ref=branch.at[block(j)], dst_ref=branch.at[block(j)],
+            send_sem=send_ag.at[di, k], recv_sem=recv_ag.at[di, k],
+            device_id={axis: sender + d}, device_id_type=MESH,
+        )
+
+    def first_pass(di, d):
+        return pltpu.make_async_remote_copy(
+            src_ref=own_ref, dst_ref=branch.at[block(me)],
+            send_sem=send_ag.at[di, 0], recv_sem=recv_ag.at[di, 0],
+            device_id={axis: me + d}, device_id_type=MESH,
+        )
+
+    sides = ((0, 1), (1, -1))
+    for di, d in sides:
+        @pl.when(inside(me + d, n))
+        def _():
+            first_pass(di, d).start()
+    branch[block(me), :] = own_ref[...]
+    for load in loads:
+        load.wait()
+
+    def chunk(j):
+        at = block(j)
+        for f in range(3):
+            cols = pl.ds(f * cut, cut)
+            gate = jnp.dot(branch[at, :], wbuf[0, :, cols], preferred_element_type=jnp.float32)
+            upward = jnp.dot(branch[at, :], wbuf[1, :, cols], preferred_element_type=jnp.float32)
+            sig = jax.nn.sigmoid(gate)
+            silu = gate * sig
+            act[2, at, cols] = (silu * upward).astype(jnp.bfloat16)
+            gprod = jnp.dot(go_ref[at, :], wbuf[2, :, cols], preferred_element_type=jnp.float32)
+            act[0, at, cols] = (gprod * upward * (sig * (1.0 + gate * (1.0 - sig)))).astype(jnp.bfloat16)
+            act[1, at, cols] = (gprod * silu).astype(jnp.bfloat16)
+        for f in range(4):
+            cols = pl.ds(f * wcut, wcut)
+            part_ref[at, cols] = dot_t(act[2, at, :], wbuf[2, cols, :]).astype(jnp.bfloat16)
+            gpart[at, cols] = (
+                dot_t(act[0, at, :], wbuf[0, cols, :]) + dot_t(act[1, at, :], wbuf[1, cols, :])
+            ).astype(jnp.bfloat16)
+
+    def distance(k, carry):
+        for di, d in sides:
+            @pl.when((k > 0) & inside(me - d * k, n))
+            def _():
+                passing(di, d, k - 1, me - d).wait_recv()
+                @pl.when(inside(me + d, n))
+                def _():
+                    passing(di, d, k, me).start()
+        low = inside(me - k, n)
+        high = (k > 0) & inside(me + k, n)
+        number = low.astype(jnp.int32) + high.astype(jnp.int32)
+
+        def one(i, c):
+            j = jnp.where((i == 0) & low, me - k, me + k)
+            chunk(j)
+            return c
+
+        lax.fori_loop(0, number, one, 0)
+        return carry
+
+    lax.fori_loop(0, n, distance, 0)
+
+    def owner(d, q):
+        return n - 1 - q if d > 0 else q
+
+    def item(di, d, q, sender, first):
+        src = gpart.at[block(owner(d, q))] if first else rb.at[di, q]
+        return pltpu.make_async_remote_copy(
+            src_ref=src, dst_ref=rb.at[di, q], send_sem=send_rs.at[di, q], recv_sem=recv_rs.at[di, q],
+            device_id={axis: sender + d}, device_id_type=MESH,
+        )
+
+    ways = ((0, 1, me), (1, -1, n - 1 - me))
+    for q in range(n - 1):
+        for di, d, dist in ways:
+            @pl.when(dist == 0)
+            def _():
+                item(di, d, q, me, True).start()
+
+    tile = width // 4
+
+    def leave(m, r):
+        return pltpu.make_async_copy(
+            wbuf.at[m, pl.ds(pl.multiple_of(r * tile, tile), tile)],
+            gw_ref.at[pl.ds(pl.multiple_of(r * tile, tile), tile), pl.ds(m * hidden, hidden)],
+            out_sem.at[m, r],
+        )
+
+    def weights(m, left):
+        def one(r, c):
+            at = pl.ds(pl.multiple_of(r * tile, tile), tile)
+            wbuf[m, at, :] = lax.dot_general(
+                left[:, at], act[m], (((0,), (0,)), ((), ())), preferred_element_type=jnp.float32
+            ).astype(jnp.bfloat16)
+            leave(m, r).start()
+            return c
+
+        lax.fori_loop(0, 4, one, 0)
+
+    todo = [(2, go_ref), (0, branch), (1, branch)]
+    for t in range(1, n):
+        if todo:
+            weights(*todo.pop(0))
+        if t == n - 1:
+            while todo:
+                weights(*todo.pop(0))
+            break
+        for di, d, dist in ways:
+            @pl.when((dist > 0) & (t >= dist))
+            def _():
+                q = t - dist
+                item(di, d, q, me - d, False).wait_recv()
+                rb[di, q] = (rb[di, q].astype(jnp.float32) + gpart[block(owner(d, q)), :].astype(jnp.float32)).astype(rb.dtype)
+                item(di, d, q, me, False).start()
+    for di, d, dist in ways:
+        @pl.when(dist > 0)
+        def _():
+            item(di, d, n - 1 - dist, me - d, False).wait_recv()
+    @pl.when(me == 0)
+    def _():
+        gb_ref[...] = gpart[block(0), :].astype(jnp.float32) + rb[1, 0].astype(jnp.float32)
+    @pl.when(me == n - 1)
+    def _():
+        gb_ref[...] = gpart[block(n - 1), :].astype(jnp.float32) + rb[0, 0].astype(jnp.float32)
+    @pl.when((me > 0) & (me < n - 1))
+    def _():
+        gb_ref[...] = gpart[block(me), :].astype(jnp.float32) + rb[0, n - 1 - me].astype(jnp.float32) + rb[1, me].astype(jnp.float32)
+
+    for k in range(n - 1):
+        for di, d in sides:
+            @pl.when(inside(me - d * k, n) & inside(me + d, n))
+            def _():
+                passing(di, d, k, me).wait_send()
+    for t in range(n - 1):
+        for di, d, dist in ways:
+            @pl.when(t >= dist)
+            def _():
+                item(di, d, t - dist, me, False).wait_send()
+    for m in range(3):
+        for r in range(4):
+            leave(m, r).wait()
+
+
+def dot_t(left, right):
+    return lax.dot_general(left, right, (((1,), (1,)), ((), ())), preferred_element_type=jnp.float32)
+
+
+def ffn(own, go, w, n, cid, axis="tp"):
+    rows_own, width = own.shape
+    total = rows_own * n
+    hidden = w.shape[1] // 3
+    vmem = pl.BlockSpec(memory_space=pltpu.VMEM)
+    any_space = pl.BlockSpec(memory_space=pl.ANY)
+    dma = pltpu.SemaphoreType.DMA
+    return pl.pallas_call(
+        functools.partial(ffn_kernel, n, axis),
+        out_shape=(
+            jax.ShapeDtypeStruct((rows_own, width), jnp.float32),
+            jax.ShapeDtypeStruct((total, width), jnp.bfloat16),
+            jax.ShapeDtypeStruct(w.shape, jnp.bfloat16),
+        ),
+        in_specs=[vmem, vmem, any_space],
+        out_specs=(vmem, vmem, any_space),
+        scratch_shapes=[
+            pltpu.VMEM((total, width), jnp.bfloat16),
+            pltpu.VMEM((3, width, hidden), jnp.bfloat16),
+            pltpu.VMEM((3, total, hidden), jnp.bfloat16),
+            pltpu.VMEM((total, width), jnp.bfloat16),
+            pltpu.VMEM((2, n - 1, rows_own, width), jnp.bfloat16),
+            dma((3,)), dma((3, 4)), dma((2, n - 1)), dma((2, n - 1)), dma((2, n - 1)), dma((2, n - 1)),
+        ],
+        compiler_params=pltpu.CompilerParams(
+            collective_id=cid, has_side_effects=True, vmem_limit_bytes=VMEM_LIMIT
+        ),
+        cost_estimate=pl.CostEstimate(
+            flops=18 * total * width * hidden, bytes_accessed=12 * width * hidden, transcendentals=0
+        ),
+        name="ffn",
+    )(own, go, w)
+
+
 def per_device(
     hidden_in,
     grad_out,
@@ -248,7 +453,6 @@
     ffn_set = lax.all_gather(
         jnp.concatenate([w_gate, w_up, w_down.T], axis=1), "fsdp", axis=0, tiled=True
     )
-    full_gate, full_up, full_down = ffn_set[:, :fc], ffn_set[:, fc : 2 * fc], ffn_set[:, 2 * fc :]
 
     tokens_all = ag(hidden_in, parts, cid=1)
     tokens_float = tokens_all.astype(jnp.float32)
@@ -270,31 +474,14 @@
     mixed_low = mixed.reshape(group_rows, -1).astype(jnp.bfloat16)
     attn_part = jnp.einsum("th,dh->td", mixed_low, full_out, preferred_element_type=jnp.float32)
     middle = own_float + rs(attn_part.astype(jnp.bfloat16), parts, cid=2)
-    branch = ag(norm_gain(middle, second_gain).astype(jnp.bfloat16), parts, cid=3)
-    gate = jnp.dot(branch, full_gate, preferred_element_type=jnp.float32)
-    upward = jnp.dot(branch, full_up, preferred_element_type=jnp.float32)
-    sigmoid_gate = jax.nn.sigmoid(gate)
-    silu_gate = gate * sigmoid_gate
-    product = (silu_gate * upward).astype(jnp.bfloat16)
-    ffn_part = jnp.einsum("tf,df->td", product, full_down, preferred_element_type=jnp.float32)
+    grad_held, unused_tokens = lax.optimization_barrier((grad_out, tokens_all))
+    grad_all = lax.all_gather(grad_held, "tp", axis=0, tiled=True)
+    branch_own = norm_gain(middle, second_gain).astype(jnp.bfloat16)
+    grad_branch_own, ffn_part, grad_w_ffn = ffn(branch_own, grad_all, ffn_set, parts, cid=3)
     result = middle + lax.psum_scatter(
-        ffn_part.astype(jnp.bfloat16), "tp", scatter_dimension=0, tiled=True
+        ffn_part, "tp", scatter_dimension=0, tiled=True
     ).astype(jnp.float32)
     out = result.astype(jnp.bfloat16)
-    grad_all = lax.all_gather(grad_out, "tp", axis=0, tiled=True)
-    grad_product = jnp.dot(grad_all, full_down, preferred_element_type=jnp.float32)
-    grad_w_down = jnp.einsum("td,tf->df", grad_all, product, preferred_element_type=jnp.float32)
-    grad_gate = (
-        grad_product * upward * (sigmoid_gate * (1.0 + gate * (1.0 - sigmoid_gate)))
-    ).astype(jnp.bfloat16)
-    grad_up = (grad_product * silu_gate).astype(jnp.bfloat16)
-    grad_w_gate = jnp.einsum("td,tf->df", branch, grad_gate, preferred_element_type=jnp.float32)
-    grad_w_up = jnp.einsum("td,tf->df", branch, grad_up, preferred_element_type=jnp.float32)
-    grad_branch = jnp.einsum("tf,df->td", grad_gate, full_gate, preferred_element_type=jnp.float32)
-    grad_branch = grad_branch + jnp.einsum(
-        "tf,df->td", grad_up, full_up, preferred_element_type=jnp.float32
-    )
-    grad_branch_own = rs(grad_branch.astype(jnp.bfloat16), parts, cid=4)
     unused_second, pull_second = jax.vjp(norm_gain, middle, second_gain)
     grad_mid_norm, grad_second = pull_second(grad_branch_own)
     grad_middle = grad_out.astype(jnp.float32) + grad_mid_norm
@@ -305,9 +492,7 @@
             value.astype(jnp.bfloat16), "fsdp", scatter_dimension=0, tiled=True
         ).astype(jnp.float32)
 
-    down_own = spread(grad_w_down)
-    gate_own = spread(grad_w_gate)
-    up_own = spread(grad_w_up)
+    ffn_own = spread(grad_w_ffn)
     grad_mixed = jnp.dot(grad_mid_all, full_out, preferred_element_type=jnp.float32).astype(
         jnp.bfloat16
     )
@@ -363,9 +548,9 @@
         gain_query,
         gain_key,
         gain_second,
-        gate_own,
-        up_own,
-        down_own.T,
+        ffn_own[:, :fc],
+        ffn_own[:, fc : 2 * fc],
+        ffn_own[:, 2 * fc :].T,
     )
 
 

time: 1090 us -> 902 us (0.83)
  matrix products: 222 us -> 120 us
  Pallas kernels: 505 us -> 427 us
  blocking collectives: 94.8 us -> 69.8 us
  waiting for transfers between devices: 151 us -> 173 us
    pallas_call x0 -> x1, Pallas kernels: none -> 157 us  [ffn(): pl.pallas_call(functools.partial(ffn_kernel, n, axis), out_shape=(jax.Sha...]
    pallas_call x3 -> x2, Pallas kernels: 272 us -> 140 us  [ag(): pl.pallas_call(functools.partial(ag_kernel, n, S, axis), out_shape=jax.Sh...]
    pallas_call x3 -> x2, Pallas kernels: 233 us -> 130 us  [rs(): pl.pallas_call(functools.partial(rs_kernel, n, S, axis), out_shape=jax.Sh...]
    dot_general x9 -> x0, matrix products: 100 us -> none  [the longest x1 14.9 us: per_device(): upward = jnp.dot(branch, full_up, preferred_element_type=jnp.float32)]
    all_gather x1, waiting for transfers between devices: 0.02 us -> 28.3 us  [per_device(): lax.all_gather(jnp.concatenate([w_gate, w_up, w_down.T], axis=1), 'fsdp',...]
    reduce_scatter x5 -> x3, waiting for transfers between devices: 150 us -> 125 us  [spread(): lax.psum_scatter(value.astype(jnp.bfloat16), 'fsdp', scatter_dimension=0,...]
    psum x1, blocking collectives: 68.2 us -> 45.8 us  [per_device(): lax.psum(jnp.concatenate([grad_first, grad_second, grad_q_gain, grad_k_ga...]
    reduce_scatter x1, waiting for transfers between devices: 0.01 us -> 18 us  [per_device(): lax.psum_scatter(ffn_part, 'tp', scatter_dimension=0, tiled=True)]
  transfers between devices with their start and end apart: 9 -> 7, of which waited for: 3 -> 3; matrix products, arithmetic and copies ran while one was open for 16% -> 12% of each run, Pallas kernels for 35% -> 23%
where the time goes in v2:
time: 902 us; the launch traced here: 893 us
  Pallas kernels  427 us (47%)
  waiting for transfers between devices  173 us (19%)
  matrix products  120 us (13%)
  blocking collectives  69.8 us (8%)
  other arithmetic  50 us (6%)
  local copies, waits for them, and re-layouts  35.7 us (4%)
  between operations  17.1 us (2%)
    pallas_call x1, Pallas kernels, ffn(): pl.pallas_call(functools.partial(ffn_kernel, n, axis), out_shape=(jax.Sha...  157 us
    pallas_call x2, Pallas kernels, ag(): pl.pallas_call(functools.partial(ag_kernel, n, S, axis), out_shape=jax.Sh...  140 us
    pallas_call x2, Pallas kernels, rs(): pl.pallas_call(functools.partial(rs_kernel, n, S, axis), out_shape=jax.Sh...  130 us
    reduce_scatter x3, waiting for transfers between devices, spread(): lax.psum_scatter(value.astype(jnp.bfloat16), 'fsdp', scatter_dimension=0,...  125 us
    psum x1, blocking collectives, per_device(): lax.psum(jnp.concatenate([grad_first, grad_second, grad_q_gain, grad_k_ga...  45.8 us
    all_gather x1, waiting for transfers between devices, per_device(): lax.all_gather(jnp.concatenate([w_gate, w_up, w_down.T], axis=1), 'fsdp',...  28.3 us
    dot_general x1, matrix products, attend_backward(): jnp.einsum('kgqp,pkd->qkgd', grad_low, keys, preferred_element_type=jnp.f...  25.1 us
    unnamed x1, blocking collectives  24.1 us
  transfers between devices with their start and end apart: 7, of which 3 were waited for; matrix products, arithmetic and copies ran while one was open for 12% of the time, Pallas kernels for 23%

profile of v2, /device:TPU:0, one launch (start us, length us, event | category | flops | bytes accessed | tf_op | source)
XLA Modules:
  0.0 892.8 jit_solution(5450204396968603948)
XLA Ops:
  10.3 2.0 pad_maximum_fusion.5
  12.4 1.3 copy-done.2
  13.7 72.7 %ag.2 = bf16[1024,2048]{1,0:T(8,128)(2,1)S(1)} custom-call(bf16[256,2048]{1,0:T(8,128)(2,1)S(1)} %copy-done.2), custom_call_target="tpu_custom_call" | custom-call | tf_op jit(solution)/shard_map/ag/pallas_call | solution.py:146
  86.3 2.1 copy-done
  88.9 1.6 pad_maximum_fusion
  92.1 24.1 %all-reduce.4 = bf16[4352]{0:T(1024)(128)(2,1)S(1)} all-reduce(bf16[4352]{0:T(1024)(128)(2,1)S(1)} %dynamic-update-slice), channel_id=2, replica_groups=mesh['fsdp'=8,'tp'=4] {'fsdp'}, use_global_device_ids=true, to_apply=%add.4 | all-reduce | flops 4352 | bytes 17408
  118.7 3.1 fusion.6
  121.8 1.3 fusion.16
  123.1 7.7 fusion.18
  135.3 2.4 copy.80
  137.7 1.3 copy.79
  139.4 1.7 multiply_reduce_fusion.8
  143.2 8.3 fusion.63
  151.5 8.0 fusion.4
  159.5 7.6 fusion.30
  167.2 4.4 convolution_convert_fusion.p_ref
  171.6 65.0 %rs.2 = f32[256,2048]{1,0:T(8,128)S(1)} custom-call(bf16[1024,2048]{1,0:T(8,128)(2,1)S(1)} %convolution_convert_fusion.p_ref), custom_call_target="tpu_custom_call" | custom-call | tf_op jit(solution)/shard_map/rs/pallas_call | solution.py:205
  240.2 28.3 %all-gather.9.cloned.1.call-done.w_ref = bf16[2048,4608]{1,0:T(8,128)(2,1)} async-done(((bf16[256,4608]{1,0:T(8,128)(2,1)}), bf16[2048,4608]{1,0:T(8,128)(2,1)}) %all-gather.9.cloned.1.call-update) | async-done | bytes 18874384 | tf_op jit(solution)/shard_map/all_gather | solution.py:453
  268.5 156.8 %ffn.1 = (f32[256,2048]{1,0:T(8,128)}, bf16[1024,2048]{1,0:T(8,128)(2,1)}, bf16[2048,4608]{1,0:T(8,128)(2,1)}) custom-call(bf16[256,2048]{1,0:T(8,128)(2,1)} %multiply_convert_fusion.own_ref, bf16[1024,2048]{1,0:T(8,128)(2,1)} %all-gather.7.cloned.1.call-done.go_ref, bf16[2048,4608]{1,0:T(8,128)(2,1)} %all-gather.9.cloned.1.call-done.w_ref), custom_call_target="tpu_custom_call" | custom-call | flops 57982058496 | bytes 37748736 | tf_op jit(solution)/shard_map/ffn/pallas_call | solution.py:389
  425.4 2.9 multiply_reduce_fusion.1
  428.9 2.0 fusion.57.x_ref
  430.8 67.6 %ag.3 = bf16[1024,2048]{1,0:T(8,128)(2,1)S(1)} custom-call(bf16[256,2048]{1,0:T(8,128)(2,1)S(1)} %fusion.57.x_ref), custom_call_target="tpu_custom_call" | custom-call | tf_op jit(solution)/shard_map/ag/pallas_call | solution.py:146
  498.4 5.5 fusion.31
  504.9 8.2 fusion.64
  513.1 22.7 %fusion.34 = f32[1024,2,128]{2,0,1:T(8,128)S(1)} fusion(f32[2,1024,1024,2]{2,1,3,0:T(8,128)} %fusion.64, f32[2,2,1024,1024]{2,3,1,0:T(8,128)} %get-tuple-element.147, f32[2,2,1024]{2,1,0:T(2,128)S(1)} %copy-done.57, bf16[1024,2,2,64]{3,0,2,1:T(8,128)(2,1)S(1)} %bitcast.107, bf16[1024,2,2,64]{3,0,2,1:T(8,128)(2,1)S(1)} %bitcast.109), kind=kOutput, calls=%fused_computation.66 | convolution fusion | flops 1105204224 | bytes 35667968 | tf_op jit(solution)/shard_map/while/body/eval_jaxpr/kgqp,qkgd->pkd/dot_general | solution.py:85
  535.8 25.1 %fusion.15 = f32[2,128,2,1024]{3,1,2,0:T(8,128)} fusion(f32[2,1024,1024,2]{2,1,3,0:T(8,128)} %fusion.64, f32[2,2,1024,1024]{2,3,1,0:T(8,128)} %get-tuple-element.147, f32[2,2,1024]{2,1,0:T(2,128)S(1)} %copy-done.57, bf16[1024,2,64]{2,0,1:T(8,128)(2,1)} %copy-done.44, bf16[1024,2,64]{2,0,1:T(8,128)(2,1)} %copy-done.43), kind=kOutput, calls=%fused_computation.22 | convolution fusion | flops 1104155648 | bytes 36192256 | tf_op jit(solution)/shard_map/while/body/eval_jaxpr/kgqp,pkd->qkgd/dot_general | solution.py:84
  561.0 6.0 convolution_convert_fusion.3
  569.9 1.6 multiply_add_fusion.3
  571.7 3.2 multiply_reduce_fusion
  574.9 1.9 fusion.43
  576.8 2.2 copy.92
  579.0 2.3 fusion.21
  581.4 9.3 %fusion.38 = bf16[2,128,1024]{2,1,0:T(8,128)(2,1)S(1)} fusion(bf16[1024,2,2,128]{0,3,2,1:T(8,128)(2,1)S(1)} %bitcast.101, f32[2,2,1024,1024]{2,3,1,0:T(8,128)} %get-tuple-element.147, f32[2,2,1024]{2,1,0:T(2,128)S(1)} %copy-done.57), kind=kOutput, calls=%fused_computation.68 | convolution fusion | flops 1082392576 | bytes 18366464 | tf_op jit(solution)/shard_map/while/body/eval_jaxpr/kgqp,qkgd->pkd/dot_general | solution.py:86
  590.7 8.4 convolution_convert_fusion.1
  601.0 7.0 convolution_convert_fusion.2.p_ref
  608.0 65.1 %rs.3 = f32[256,2048]{1,0:T(8,128)S(1)} custom-call(bf16[1024,2048]{1,0:T(8,128)(2,1)S(1)} %convolution_convert_fusion.2.p_ref), custom_call_target="tpu_custom_call" | custom-call | tf_op jit(solution)/shard_map/rs/pallas_call | solution.py:205
  673.9 45.8 %psum.7 = f32[4352]{0:T(1024)S(1)} all-reduce(f32[4352]{0:T(1024)S(1)} %pad_maximum_fusion.8), channel_id=1, replica_groups=mesh['fsdp'=8,'tp'=4] {'fsdp','tp'}, use_global_device_ids=true, to_apply=%region_17.18 | all-reduce | flops 4352 | bytes 34816 | tf_op jit(solution)/shard_map/psum | solution.py:530
  720.9 1.8 convert_bitcast_fusion
  722.7 2.0 copy.94
  724.8 1.8 slice.90
  726.6 1.8 fusion.59
  728.4 18.0 %reduce-scatter.5.cloned.1.call-done = bf16[256,2048]{1,0:T(8,128)(2,1)} async-done(((bf16[1024,2048]{1,0:T(8,128)(2,1)}), bf16[256,2048]{1,0:T(8,128)(2,1)}) %reduce-scatter.5.cloned.1.call-update) | async-done | bytes 1048592 | tf_op jit(solution)/shard_map/reduce_scatter | solution.py:481
  746.4 5.6 fusion.22
  751.9 125.0 %reduce-scatter.11.cloned.1.call-done = bf16[256,4608]{1,0:T(8,128)(2,1)} async-done(((bf16[2048,4608]{1,0:T(8,128)(2,1)}), bf16[256,4608]{1,0:T(8,128)(2,1)}) %reduce-scatter.11.cloned.1.call-update) | async-done | bytes 2359312 | tf_op jit(solution)/shard_map/reduce_scatter | solution.py:491
  876.9 2.2 convert_element_type.100
  879.1 1.3 slice_bitcast_fusion
  880.4 3.1 copy.95
  883.4 2.1 fusion.58
  (220 shorter events, 24.9 us)
Async XLA Ops:
  7.2 115.9 %all-gather.5.cloned.1.call-start = ((), (), s32[]{:S(2)}) async-start(), calls=%async_computation.4 | async-start | bytes 7077888 | tf_op jit(solution)/shard_map/all_gather | solution.py:448
  10.3 78.3 %copy-start.41 = (bf16[1536,256]{1,0:T(8,128)(2,1)S(1)}, bf16[1536,256]{1,0:T(8,128)(2,1)}, u32[]{:S(2)}) copy-start(bf16[1536,256]{1,0:T(8,128)(2,1)} %param.29) | copy-start | bytes 2359300
  12.3 76.6 %copy-start.39 = (bf16[256,1536]{1,0:T(8,128)(2,1)S(1)}, bf16[256,1536]{1,0:T(8,128)(2,1)}, u32[]{:S(2)}) copy-start(bf16[256,1536]{1,0:T(8,128)(2,1)} %param.28) | copy-start | bytes 2359300
  12.3 227.9 %all-gather.7.cloned.1.call-start = ((), (), s32[]{:S(2)}) async-start(), calls=%async_computation.5 | async-start | bytes 5242880 | tf_op jit(solution)/shard_map/all_gather | solution.py:478
  13.7 75.2 %copy-start.40 = (bf16[256,1536]{1,0:T(8,128)(2,1)S(1)}, bf16[256,1536]{1,0:T(8,128)(2,1)}, u32[]{:S(2)}) copy-start(bf16[256,1536]{1,0:T(8,128)(2,1)} %param.27) | copy-start | bytes 2359300
  88.5 27.9 %copy-start.67 = (s32[1024]{0:T(1024)S(1)}, s32[1024]{0:T(1024)}, u32[]{:S(2)}) copy-start(s32[1024]{0:T(1024)} %param.18) | copy-start | bytes 12292
  88.5 179.9 %all-gather.9.cloned.1.call-start = ((), (), s32[]{:S(2)}) async-start(), calls=%async_computation.6 | async-start | bytes 21233664 | tf_op jit(solution)/shard_map/all_gather | solution.py:453
  90.5 630.4 %reduce-scatter.9.cloned.1.call-start = ((), (), s32[]{:S(2)}) async-start(), calls=%async_computation.9 | async-start | bytes 2359296 | tf_op jit(solution)/shard_map/reduce_scatter | solution.py:491
  116.3 14.6 %copy-start.55 = (f32[1,2,8,128]{3,1,2,0:T(2,128)}, f32[1,2,8,128]{3,1,2,0:T(2,128)S(1)}, u32[]{:S(2)}) copy-start(f32[1,2,8,128]{3,1,2,0:T(2,128)S(1)} %copy.113) | copy-start | bytes 24580
  116.4 15.7 %copy-start.65 = (f32[128]{0:T(128)}, f32[128]{0:T(128)S(1)}, u32[]{:S(2)}) copy-start(f32[128]{0:T(128)S(1)} %mul.455) | copy-start | bytes 1540
  116.5 25.2 %copy-start.63 = (f32[128]{0:T(128)}, f32[128]{0:T(128)S(1)}, u32[]{:S(2)}) copy-start(f32[128]{0:T(128)S(1)} %mul.436) | copy-start | bytes 1540
  117.5 16.6 %copy-start.23 = (f32[1024,64]{0,1:T(8,128)}, f32[1024,64]{0,1:T(8,128)S(1)}, u32[]{:S(2)}) copy-start(f32[1024,64]{0,1:T(8,128)S(1)} %get-tuple-element.144) | copy-start | bytes 786436
  117.5 16.6 %copy-start.25 = (f32[1024,64]{0,1:T(8,128)}, f32[1024,64]{0,1:T(8,128)S(1)}, u32[]{:S(2)}) copy-start(f32[1024,64]{0,1:T(8,128)S(1)} %get-tuple-element.145) | copy-start | bytes 786436
  117.8 24.9 %copy-start.19 = (f32[1024,64]{1,0:T(8,128)}, f32[1024,64]{1,0:T(8,128)S(1)}, u32[]{:S(2)}) copy-start(f32[1024,64]{1,0:T(8,128)S(1)} %copy.78) | copy-start | bytes 786436
  118.0 24.7 %copy-start.21 = (f32[1024,64]{1,0:T(8,128)}, f32[1024,64]{1,0:T(8,128)S(1)}, u32[]{:S(2)}) copy-start(f32[1024,64]{1,0:T(8,128)S(1)} %copy.77) | copy-start | bytes 786436
  118.6 119.7 %copy-start.47 = (f32[1,2,8,128]{3,1,2,0:T(2,128)}, f32[1,2,8,128]{3,1,2,0:T(2,128)S(1)}, u32[]{:S(2)}) copy-start(f32[1,2,8,128]{3,1,2,0:T(2,128)S(1)} %copy.114) | copy-start | bytes 24580
  121.8 9.1 %copy-start.68 = (f32[1024]{0:T(1024)}, f32[1024]{0:T(1024)S(1)}, u32[]{:S(2)}) copy-start(f32[1024]{0:T(1024)S(1)} %add_rsqrt_fusion) | copy-start | bytes 12292
  134.1 4.8 slice-start
  139.3 12.1 %copy-start.10 = (f32[1024,2,128]{2,0,1:T(8,128)}, f32[1024,2,128]{2,0,1:T(8,128)S(1)}, u32[]{:S(2)}) copy-start(f32[1024,2,128]{2,0,1:T(8,128)S(1)} %copy.76) | copy-start | bytes 3145732
  139.3 3.8 copy-start.32
  139.3 3.8 copy-start.34
  143.1 8.3 copy-start.43
  143.1 8.3 copy-start.44
  151.5 8.1 copy-start.29
  167.2 4.4 copy-start.74
  171.6 65.0 %copy-start.3 = (bf16[256,2048]{1,0:T(8,128)(2,1)S(1)}, bf16[256,2048]{1,0:T(8,128)(2,1)}, u32[]{:S(2)}) copy-start(bf16[256,2048]{1,0:T(8,128)(2,1)} %x_ref.1) | copy-start | bytes 3145732
  498.4 5.5 copy-start.5
  498.4 6.5 copy-start.30
  504.9 8.2 copy-start.33
  504.9 8.2 copy-start.35
  504.9 8.2 copy-start.57
  535.8 25.2 %copy-start.75 = (bf16[2,128,2,1024]{3,1,2,0:T(8,128)(2,1)S(1)}, bf16[2,128,2,1024]{3,1,2,0:T(8,128)(2,1)}, u32[]{:S(2)}) copy-start(bf16[2,128,2,1024]{3,1,2,0:T(8,128)(2,1)} %copy-done.74) | copy-start | bytes 3145732
  561.0 6.1 copy-start.20
  561.0 6.1 copy-start.22
  571.6 153.2 %reduce-scatter.7.cloned.1.call-start = ((), (), s32[]{:S(2)}) async-start(), calls=%async_computation.8 | async-start | bytes 4718592 | tf_op jit(solution)/shard_map/reduce_scatter | solution.py:491
  571.7 7.3 copy-start.50
  574.9 4.1 copy-start.17
  574.9 4.1 copy-start.18
  576.8 4.5 copy-start.28
  581.3 9.4 %copy-start.37 = (bf16[1024,4,128]{0,2,1:T(8,128)(2,1)}, bf16[1024,4,128]{0,2,1:T(8,128)(2,1)S(1)}, u32[]{:S(2)}) copy-start(bf16[1024,4,128]{0,2,1:T(8,128)(2,1)S(1)} %fusion.21) | copy-start | bytes 3145732
  581.3 9.4 %copy-start.1 = (bf16[1024,2048]{1,0:T(8,128)(2,1)S(1)}, bf16[1024,2048]{1,0:T(8,128)(2,1)}, u32[]{:S(2)}) copy-start(bf16[1024,2048]{1,0:T(8,128)(2,1)} %copy-done) | copy-start | bytes 12582916
  581.3 9.4 %copy-start.42 = (bf16[1024,2,128]{0,2,1:T(8,128)(2,1)S(1)}, bf16[1024,2,128]{0,2,1:T(8,128)(2,1)}, u32[]{:S(2)}) copy-start(bf16[1024,2,128]{0,2,1:T(8,128)(2,1)} %copy.92) | copy-start | bytes 1572868
  581.3 9.4 %copy-start.56 = (f32[1,2,8,128]{3,1,2,0:T(2,128)S(1)}, f32[1,2,8,128]{3,1,2,0:T(2,128)}, u32[]{:S(2)}) copy-start(f32[1,2,8,128]{3,1,2,0:T(2,128)} %copy-done.55) | copy-start | bytes 24580
  581.3 9.4 %copy-start.69 = (f32[1024]{0:T(1024)S(1)}, f32[1024]{0:T(1024)}, u32[]{:S(2)}) copy-start(f32[1024]{0:T(1024)} %copy-done.68) | copy-start | bytes 12292
  599.1 147.3 %reduce-scatter.5.cloned.1.call-start = ((), (), s32[]{:S(2)}) async-start(), calls=%async_computation.7 | async-start | bytes 5242880 | tf_op jit(solution)/shard_map/reduce_scatter | solution.py:481
  599.7 277.3 %reduce-scatter.11.cloned.1.call-start = ((), (), s32[]{:S(2)}) async-start(), calls=%async_computation.10 | async-start | bytes 21233664 | tf_op jit(solution)/shard_map/reduce_scatter | solution.py:491
  608.0 65.2 %copy-start.4 = (bf16[256,2048]{1,0:T(8,128)(2,1)S(1)}, bf16[256,2048]{1,0:T(8,128)(2,1)}, u32[]{:S(2)}) copy-start(bf16[256,2048]{1,0:T(8,128)(2,1)} %x_ref.1) | copy-start | bytes 3145732
  879.1 4.3 copy-start.12
  (38 other events, 84.0 us)
Sparse Core Ops, SparseCore 0:
  12.4 49.2 all-gather.4
  88.6 80.8 all-gather.6
  171.4 97.0 all-gather.8
  571.7 40.1 reduce-scatter.8
  615.1 51.1 reduce-scatter.6
  668.5 77.8 reduce-scatter.4
  750.0 126.9 reduce-scatter.10

commit v3 on v2

--- a/solution.py
+++ b/solution.py
@@ -69,27 +69,6 @@
         "kgqp,pkd->qkgd", shares.astype(jnp.bfloat16), values, preferred_element_type=jnp.float32
     )
     return (mixed, (peak + jnp.log(total))[..., 0])
-
-
-def attend_backward(item):
-    query, keys, values, grad_mixed, log_total, prefix = item
-    scale = 1.0 / math.sqrt(HD)
-    scores = masked_scores(query, keys, prefix)
-    shares = jnp.exp(scores - log_total[..., None])
-    grad_shares = jnp.einsum(
-        "qkgd,pkd->kgqp", grad_mixed, values, preferred_element_type=jnp.float32
-    )
-    grad_scores = shares * (grad_shares - jnp.sum(grad_shares * shares, axis=-1, keepdims=True))
-    grad_low = (grad_scores * scale).astype(jnp.bfloat16)
-    grad_query = jnp.einsum("kgqp,pkd->qkgd", grad_low, keys, preferred_element_type=jnp.float32)
-    grad_keys = jnp.einsum("kgqp,qkgd->pkd", grad_low, query, preferred_element_type=jnp.float32)
-    grad_values = jnp.einsum(
-        "kgqp,qkgd->pkd",
-        shares.astype(jnp.bfloat16),
-        grad_mixed,
-        preferred_element_type=jnp.float32,
-    )
-    return (grad_query, grad_keys, grad_values)
 
 
 def greet(me, n, axis):
@@ -210,11 +189,11 @@
         compiler_params=pltpu.CompilerParams(collective_id=cid, has_side_effects=True, vmem_limit_bytes=32 << 20), name="rs")(p)
 
 def ffn_kernel(
-    n, axis, own_ref, go_ref, w_ref, gb_ref, part_ref, gw_ref,
+    n, axis, mid_ref, gain_ref, go_ref, w_ref, gmid_ref, gffn_ref, part_ref, gw_ref,
     branch, wbuf, act, gpart, rb, w_sem, out_sem, send_ag, recv_ag, send_rs, recv_rs,
 ):
     me = lax.axis_index(axis)
-    rows_own, width = own_ref.shape
+    rows_own, width = mid_ref.shape
     hidden = wbuf.shape[2]
     cut = hidden // 3
     wcut = width // 4
@@ -224,10 +203,14 @@
     ]
     for load in loads:
         load.start()
-    greet(me, n, axis)
 
     def block(j):
         return pl.ds(pl.multiple_of(j * rows_own, rows_own), rows_own)
+
+    mid = mid_ref[...]
+    inverse = lax.rsqrt(jnp.mean(mid * mid, axis=-1, keepdims=True) + EPS)
+    branch[block(me), :] = (mid * inverse * gain_ref[...]).astype(jnp.bfloat16)
+    greet(me, n, axis)
 
     def passing(di, d, k, sender):
         j = sender - d * k
@@ -237,19 +220,11 @@
             device_id={axis: sender + d}, device_id_type=MESH,
         )
 
-    def first_pass(di, d):
-        return pltpu.make_async_remote_copy(
-            src_ref=own_ref, dst_ref=branch.at[block(me)],
-            send_sem=send_ag.at[di, 0], recv_sem=recv_ag.at[di, 0],
-            device_id={axis: me + d}, device_id_type=MESH,
-        )
-
     sides = ((0, 1), (1, -1))
     for di, d in sides:
         @pl.when(inside(me + d, n))
         def _():
-            first_pass(di, d).start()
-    branch[block(me), :] = own_ref[...]
+            passing(di, d, 0, me).start()
     for load in loads:
         load.wait()
 
@@ -352,13 +327,20 @@
             item(di, d, n - 1 - dist, me - d, False).wait_recv()
     @pl.when(me == 0)
     def _():
-        gb_ref[...] = gpart[block(0), :].astype(jnp.float32) + rb[1, 0].astype(jnp.float32)
+        gmid_ref[...] = gpart[block(0), :].astype(jnp.float32) + rb[1, 0].astype(jnp.float32)
     @pl.when(me == n - 1)
     def _():
-        gb_ref[...] = gpart[block(n - 1), :].astype(jnp.float32) + rb[0, 0].astype(jnp.float32)
+        gmid_ref[...] = gpart[block(n - 1), :].astype(jnp.float32) + rb[0, 0].astype(jnp.float32)
     @pl.when((me > 0) & (me < n - 1))
     def _():
-        gb_ref[...] = gpart[block(me), :].astype(jnp.float32) + rb[0, n - 1 - me].astype(jnp.float32) + rb[1, me].astype(jnp.float32)
+        gmid_ref[...] = gpart[block(me), :].astype(jnp.float32) + rb[0, n - 1 - me].astype(jnp.float32) + rb[1, me].astype(jnp.float32)
+    mid = mid_ref[...]
+    inverse = lax.rsqrt(jnp.mean(mid * mid, axis=-1, keepdims=True) + EPS)
+    unit = mid * inverse
+    grad = gmid_ref[...]
+    gffn_ref[...] = jnp.sum(grad * unit, axis=0, keepdims=True)
+    scaled = grad * gain_ref[...]
+    gmid_ref[...] = go_ref[block(me), :].astype(jnp.float32) + inverse * (scaled - unit * jnp.mean(scaled * unit, axis=-1, keepdims=True))
 
     for k in range(n - 1):
         for di, d in sides:
@@ -379,8 +361,8 @@
     return lax.dot_general(left, right, (((1,), (1,)), ((), ())), preferred_element_type=jnp.float32)
 
 
-def ffn(own, go, w, n, cid, axis="tp"):
-    rows_own, width = own.shape
+def ffn(mid, gain, go, w, n, cid, axis="tp"):
+    rows_own, width = mid.shape
     total = rows_own * n
     hidden = w.shape[1] // 3
     vmem = pl.BlockSpec(memory_space=pltpu.VMEM)
@@ -390,11 +372,12 @@
         functools.partial(ffn_kernel, n, axis),
         out_shape=(
             jax.ShapeDtypeStruct((rows_own, width), jnp.float32),
+            jax.ShapeDtypeStruct((1, width), jnp.float32),
             jax.ShapeDtypeStruct((total, width), jnp.bfloat16),
             jax.ShapeDtypeStruct(w.shape, jnp.bfloat16),
         ),
-        in_specs=[vmem, vmem, any_space],
-        out_specs=(vmem, vmem, any_space),
+        in_specs=[vmem, vmem, vmem, any_space],
+        out_specs=(vmem, vmem, vmem, any_space),
         scratch_shapes=[
             pltpu.VMEM((total, width), jnp.bfloat16),
             pltpu.VMEM((3, width, hidden), jnp.bfloat16),
@@ -410,7 +393,415 @@
             flops=18 * total * width * hidden, bytes_accessed=12 * width * hidden, transcendentals=0
         ),
         name="ffn",
-    )(own, go, w)
+    )(mid, gain, go, w)
+
+
+def exchange_plan(n, me):
+    return ((0, 1, me), (1, -1, n - 1 - me))
+
+
+def unroll_rot(value, cos2, sin2):
+    return value * cos2 - pltpu.roll(value, HD // 2, 1) * sin2
+
+
+def attn_back_kernel(
+    n, axis, heads, kv_heads,
+    gmid_ref, mid_ref, cos_ref, sin_ref, lse_ref, gain_ref, prefix_ref,
+    w_hbm, normed_hbm, qkv_hbm, raw_hbm, mixed_hbm, part_hbm,
+    out_ref, gn_ref, gsum_ref, gw_ref,
+    wbuf, normed, qkv, raw, mixed, part, gm, gmix, keys_t, dk, dv, gqkv, rb,
+    load_sem, out_sem, send_ag, recv_ag, send_rs, recv_rs,
+):
+    me = lax.axis_index(axis)
+    rows_own, width = gmid_ref.shape
+    total = rows_own * n
+    qc, kc = heads * HD, kv_heads * HD
+    group = heads // kv_heads
+    scale = 1.0 / math.sqrt(HD)
+    pairs = ((w_hbm, wbuf), (qkv_hbm, qkv), (raw_hbm, raw), (part_hbm, part), (normed_hbm, normed), (mixed_hbm, mixed))
+    loads = [pltpu.make_async_copy(src, dst, load_sem.at[i]) for i, (src, dst) in enumerate(pairs)]
+    for load in loads:
+        load.start()
+
+    def block(j):
+        return pl.ds(pl.multiple_of(j * rows_own, rows_own), rows_own)
+
+    gm[block(me), :] = gmid_ref[...].astype(jnp.bfloat16)
+    dk[...] = jnp.zeros_like(dk)
+    dv[...] = jnp.zeros_like(dv)
+    gsum_ref[...] = jnp.zeros_like(gsum_ref)
+    greet(me, n, axis)
+
+    def passing(di, d, k, sender):
+        j = sender - d * k
+        return pltpu.make_async_remote_copy(
+            src_ref=gm.at[block(j)], dst_ref=gm.at[block(j)],
+            send_sem=send_ag.at[di, k], recv_sem=recv_ag.at[di, k],
+            device_id={axis: sender + d}, device_id_type=MESH,
+        )
+
+    def owner(d, q):
+        return n - 1 - q if d > 0 else q
+
+    def item(di, d, q, sender, first):
+        src = part.at[block(owner(d, q))] if first else rb.at[di, q]
+        return pltpu.make_async_remote_copy(
+            src_ref=src, dst_ref=rb.at[di, q], send_sem=send_rs.at[di, q], recv_sem=recv_rs.at[di, q],
+            device_id={axis: sender + d}, device_id_type=MESH,
+        )
+
+    sides = ((0, 1), (1, -1))
+    ways = exchange_plan(n, me)
+    for di, d in sides:
+        @pl.when(inside(me + d, n))
+        def _():
+            passing(di, d, 0, me).start()
+    for load in loads[:3]:
+        load.wait()
+    for g in range(kv_heads):
+        keys_t[g] = qkv[:, qc + g * HD : qc + (g + 1) * HD].T
+    loads[3].wait()
+    prefix = prefix_ref[0]
+
+    def unit_of(at, first):
+        value = raw[at, first : first + HD]
+        inverse = lax.rsqrt(jnp.mean(value * value, axis=-1, keepdims=True) + EPS)
+        return value * inverse, inverse
+
+    def normed_back(grad, at, first, gain, place):
+        unit, inverse = unit_of(at, first)
+        turned = unroll_rot(grad, cos_ref[at, :], sin_ref[at, :])
+        gsum_ref[place : place + 1, :] += jnp.sum(turned * unit, axis=0, keepdims=True)
+        scaled = turned * gain
+        return (inverse * (scaled - unit * jnp.mean(scaled * unit, axis=-1, keepdims=True))).astype(jnp.bfloat16)
+
+    def chunk(j):
+        at = block(j)
+        gmix[...] = jnp.dot(gm[at, :], wbuf[:, qc + 2 * kc :], preferred_element_type=jnp.float32).astype(jnp.bfloat16)
+        key_at = lax.broadcasted_iota(jnp.int32, (total, rows_own), 0)
+        query_at = lax.broadcasted_iota(jnp.int32, (total, rows_own), 1) + j * rows_own
+        seen = (key_at <= query_at) | (key_at < prefix)
+        for h in range(heads):
+            g = h // group
+            ks, vs, hs = qc + g * HD, qc + kc + g * HD, h * HD
+            q = qkv[at, hs : hs + HD]
+            gx = gmix[:, hs : hs + HD]
+            scores = dot_t(qkv[:, ks : ks + HD], q) * scale
+            shares = jnp.where(seen, jnp.exp(scores - lse_ref[h : h + 1, at]), 0.0)
+            grad_shares = dot_t(qkv[:, vs : vs + HD], gx)
+            delta = jnp.sum(grad_shares * shares, axis=0, keepdims=True)
+            low = (shares * (grad_shares - delta) * scale).astype(jnp.bfloat16)
+            gcols = pl.ds(g * HD, HD)
+            dk[:, gcols] += jnp.dot(low, q, preferred_element_type=jnp.float32)
+            dv[:, gcols] += jnp.dot(shares.astype(jnp.bfloat16), gx, preferred_element_type=jnp.float32)
+            dq = jnp.dot(keys_t[g], low, preferred_element_type=jnp.float32).T
+            gqkv[at, hs : hs + HD] = normed_back(dq, at, hs, gain_ref[0:1, :], 0)
+
+    def sums_step(t):
+        for di, d, dist in ways:
+            @pl.when((dist > 0) & (t >= dist))
+            def _():
+                q = t - dist
+                item(di, d, q, me - d, False).wait_recv()
+                rb[di, q] = (rb[di, q].astype(jnp.float32) + part[block(owner(d, q)), :].astype(jnp.float32)).astype(rb.dtype)
+                item(di, d, q, me, False).start()
+
+    def distance(k, carry):
+        for di, d in sides:
+            @pl.when((k > 0) & inside(me - d * k, n))
+            def _():
+                passing(di, d, k - 1, me - d).wait_recv()
+                @pl.when(inside(me + d, n))
+                def _():
+                    passing(di, d, k, me).start()
+
+        for di, d, dist in ways:
+            @pl.when((k == 1) & (dist == 0))
+            def _():
+                for q in range(n - 1):
+                    item(di, d, q, me, True).start()
+
+        @pl.when(k > 1)
+        def _():
+            sums_step(k - 1)
+
+        low = inside(me - k, n)
+        high = (k > 0) & inside(me + k, n)
+        number = low.astype(jnp.int32) + high.astype(jnp.int32)
+
+        def one(i, c):
+            chunk(jnp.where((i == 0) & low, me - k, me + k))
+            return c
+
+        lax.fori_loop(0, number, one, 0)
+        return carry
+
+    lax.fori_loop(0, n, distance, 0)
+
+    for load in loads[4:]:
+        load.wait()
+
+    def finish(j, carry):
+        at = block(j)
+        for g in range(kv_heads):
+            ks, vs = qc + g * HD, qc + kc + g * HD
+            gqkv[at, ks : ks + HD] = normed_back(dk[at, g * HD : (g + 1) * HD], at, ks, gain_ref[1:2, :], 1)
+            gqkv[at, vs : vs + HD] = dv[at, g * HD : (g + 1) * HD].astype(jnp.bfloat16)
+        cut = width // 4
+        for f in range(4):
+            cols = pl.ds(f * cut, cut)
+            gn_ref[at, cols] = dot_t(gqkv[at, :], wbuf[cols, : qc + 2 * kc]).astype(jnp.bfloat16)
+        return carry
+
+    lax.fori_loop(0, n, finish, 0)
+
+    tile = width // 4
+
+    def leave(r):
+        at = pl.ds(pl.multiple_of(r * tile, tile), tile)
+        return pltpu.make_async_copy(wbuf.at[at], gw_ref.at[at], out_sem.at[r])
+
+    def weights(r, carry):
+        at = pl.ds(pl.multiple_of(r * tile, tile), tile)
+        wbuf[at, : qc + 2 * kc] = lax.dot_general(
+            normed[:, at], gqkv[...], (((0,), (0,)), ((), ())), preferred_element_type=jnp.float32
+        ).astype(jnp.bfloat16)
+        wbuf[at, qc + 2 * kc :] = lax.dot_general(
+            gm[:, at], mixed[...], (((0,), (0,)), ((), ())), preferred_element_type=jnp.float32
+        ).astype(jnp.bfloat16)
+        leave(r).start()
+        return carry
+
+    lax.fori_loop(0, 4, weights, 0)
+
+    for di, d, dist in ways:
+        @pl.when(dist > 0)
+        def _():
+            item(di, d, n - 1 - dist, me - d, False).wait_recv()
+    own = mid_ref[...] + part[block(me), :].astype(jnp.float32)
+    @pl.when(me == 0)
+    def _():
+        out_ref[...] = (own + rb[1, 0].astype(jnp.float32)).astype(out_ref.dtype)
+    @pl.when(me == n - 1)
+    def _():
+        out_ref[...] = (own + rb[0, 0].astype(jnp.float32)).astype(out_ref.dtype)
+    @pl.when((me > 0) & (me < n - 1))
+    def _():
+        out_ref[...] = (own + rb[0, n - 1 - me].astype(jnp.float32) + rb[1, me].astype(jnp.float32)).astype(out_ref.dtype)
+
+    for k in range(n - 1):
+        for di, d in sides:
+            @pl.when(inside(me - d * k, n) & inside(me + d, n))
+            def _():
+                passing(di, d, k, me).wait_send()
+    for t in range(n - 1):
+        for di, d, dist in ways:
+            @pl.when(t >= dist)
+            def _():
+                item(di, d, t - dist, me, False).wait_send()
+    for r in range(4):
+        leave(r).wait()
+
+
+def attn_back(gmid, mid, cos2, sin2, lse, gains, prefix, w, normed, qkv, raw, mixed, part, n, heads, kv_heads, cid, axis="tp"):
+    rows_own, width = gmid.shape
+    total = rows_own * n
+    vmem = pl.BlockSpec(memory_space=pltpu.VMEM)
+    any_space = pl.BlockSpec(memory_space=pl.ANY)
+    dma = pltpu.SemaphoreType.DMA
+    return pl.pallas_call(
+        functools.partial(attn_back_kernel, n, axis, heads, kv_heads),
+        out_shape=(
+            jax.ShapeDtypeStruct((rows_own, width), jnp.bfloat16),
+            jax.ShapeDtypeStruct((total, width), jnp.bfloat16),
+            jax.ShapeDtypeStruct((8, HD), jnp.float32),
+            jax.ShapeDtypeStruct(w.shape, jnp.bfloat16),
+        ),
+        in_specs=[vmem] * 6 + [pl.BlockSpec(memory_space=pltpu.SMEM)] + [any_space] * 6,
+        out_specs=(vmem, vmem, vmem, any_space),
+        scratch_shapes=[
+            pltpu.VMEM(w.shape, jnp.bfloat16),
+            pltpu.VMEM(normed.shape, jnp.bfloat16),
+            pltpu.VMEM(qkv.shape, jnp.bfloat16),
+            pltpu.VMEM(raw.shape, jnp.float32),
+            pltpu.VMEM(mixed.shape, jnp.bfloat16),
+            pltpu.VMEM(part.shape, jnp.bfloat16),
+            pltpu.VMEM((total, width), jnp.bfloat16),
+            pltpu.VMEM((rows_own, heads * HD), jnp.bfloat16),
+            pltpu.VMEM((kv_heads, HD, total), jnp.bfloat16),
+            pltpu.VMEM((total, kv_heads * HD), jnp.float32),
+            pltpu.VMEM((total, kv_heads * HD), jnp.float32),
+            pltpu.VMEM(qkv.shape, jnp.bfloat16),
+            pltpu.VMEM((2, n - 1, rows_own, width), jnp.bfloat16),
+            dma((6,)), dma((4,)), dma((2, n - 1)), dma((2, n - 1)), dma((2, n - 1)), dma((2, n - 1)),
+        ],
+        compiler_params=pltpu.CompilerParams(
+            collective_id=cid, has_side_effects=True, vmem_limit_bytes=VMEM_LIMIT
+        ),
+        cost_estimate=pl.CostEstimate(flops=30 * total * width * HD, bytes_accessed=40 * total * width, transcendentals=0),
+        name="attn_back",
+    )(gmid, mid, cos2, sin2, lse, gains, prefix, w, normed, qkv, raw, mixed, part)
+
+
+def final_kernel(
+    n, groups, p_ref, x_ref, gmid_ref, gain_ref, gffn_ref, small_ref, dx_ref, total_ref,
+    rb, gsend, grecv, tsend, trecv, send_sem, recv_sem, gs_sem, gr_sem, ts_sem, tr_sem,
+):
+    me = lax.axis_index("tp")
+    mine = lax.axis_index("fsdp")
+    rows_own, width = dx_ref.shape
+    slot = width // groups
+    barrier = pltpu.get_barrier_semaphore()
+    for f in range(groups):
+        @pl.when(mine != f)
+        def _():
+            pl.semaphore_signal(barrier, inc=1, device_id={"fsdp": f}, device_id_type=MESH)
+    for p in range(n):
+        @pl.when(me != p)
+        def _():
+            pl.semaphore_signal(barrier, inc=1, device_id={"tp": p}, device_id_type=MESH)
+    pl.semaphore_wait(barrier, groups + n - 2)
+
+    def block(j):
+        return pl.ds(pl.multiple_of(j * rows_own, rows_own), rows_own)
+
+    def owner(d, q):
+        return n - 1 - q if d > 0 else q
+
+    halves = 2
+    half = rows_own // halves
+
+    def item(di, d, q, s, sender, first):
+        at = pl.ds(s * half, half)
+        src = p_ref.at[pl.ds(pl.multiple_of(owner(d, q) * rows_own + s * half, half), half)] if first else rb.at[di, q, at]
+        return pltpu.make_async_remote_copy(
+            src_ref=src, dst_ref=rb.at[di, q, at], send_sem=send_sem.at[di, q, s], recv_sem=recv_sem.at[di, q, s],
+            device_id={"tp": sender + d}, device_id_type=MESH,
+        )
+
+    ways = exchange_plan(n, me)
+    for q in range(n - 1):
+        for s in range(halves):
+            for di, d, dist in ways:
+                @pl.when(dist == 0)
+                def _():
+                    item(di, d, q, s, me, True).start()
+    for t in range(1, n - 1):
+        for s in range(halves):
+            for di, d, dist in ways:
+                @pl.when((dist > 0) & (t >= dist))
+                def _():
+                    q = t - dist
+                    at = pl.ds(s * half, half)
+                    item(di, d, q, s, me - d, False).wait_recv()
+                    mine_at = pl.ds(pl.multiple_of(owner(d, q) * rows_own + s * half, half), half)
+                    rb[di, q, at, :] = (rb[di, q, at, :].astype(jnp.float32) + p_ref[mine_at, :].astype(jnp.float32)).astype(rb.dtype)
+                    item(di, d, q, s, me, False).start()
+    for s in range(halves):
+        for di, d, dist in ways:
+            @pl.when(dist > 0)
+            def _():
+                item(di, d, n - 1 - dist, s, me - d, False).wait_recv()
+    own = p_ref[block(me), :].astype(jnp.float32)
+    @pl.when(me == 0)
+    def _():
+        dx_ref[...] = own + rb[1, 0].astype(jnp.float32)
+    @pl.when(me == n - 1)
+    def _():
+        dx_ref[...] = own + rb[0, 0].astype(jnp.float32)
+    @pl.when((me > 0) & (me < n - 1))
+    def _():
+        dx_ref[...] = own + rb[0, n - 1 - me].astype(jnp.float32) + rb[1, me].astype(jnp.float32)
+
+    x = x_ref[...].astype(jnp.float32)
+    inverse = lax.rsqrt(jnp.mean(x * x, axis=-1, keepdims=True) + EPS)
+    first = x * inverse
+    grad = dx_ref[...]
+    gattn = jnp.sum(grad * first, axis=0, keepdims=True)
+    for f in range(groups):
+        gsend[f, :, :slot] = gattn[:, f * slot : (f + 1) * slot]
+        gsend[f, :, slot : 2 * slot] = gffn_ref[:, f * slot : (f + 1) * slot]
+        gsend[f, :, 2 * slot : 2 * slot + HD] = small_ref[0:1, :]
+        gsend[f, :, 2 * slot + HD :] = small_ref[1:2, :]
+
+    def to_slot(f, sender):
+        return pltpu.make_async_remote_copy(
+            src_ref=gsend.at[f], dst_ref=grecv.at[sender], send_sem=gs_sem.at[f], recv_sem=gr_sem.at[sender],
+            device_id={"fsdp": f}, device_id_type=MESH,
+        )
+
+    scaled = grad * gain_ref[...]
+    dx_ref[...] = gmid_ref[...] + inverse * (scaled - first * jnp.mean(scaled * first, axis=-1, keepdims=True))
+    for f in range(groups):
+        @pl.when(mine != f)
+        def _():
+            to_slot(f, mine).start()
+    grecv[mine] = gsend[mine]
+    for f in range(groups):
+        @pl.when(mine != f)
+        def _():
+            to_slot(f, f).wait_recv()
+    tsend[...] = jnp.sum(grecv[...], axis=0)
+
+    def to_part(p, sender):
+        return pltpu.make_async_remote_copy(
+            src_ref=tsend, dst_ref=trecv.at[sender], send_sem=ts_sem.at[p], recv_sem=tr_sem.at[sender],
+            device_id={"tp": p}, device_id_type=MESH,
+        )
+
+    for p in range(n):
+        @pl.when(me != p)
+        def _():
+            to_part(p, me).start()
+    trecv[me] = tsend[...]
+    for p in range(n):
+        @pl.when(me != p)
+        def _():
+            to_part(p, p).wait_recv()
+    total_ref[...] = jnp.sum(trecv[...], axis=0)
+    for f in range(groups):
+        @pl.when(mine != f)
+        def _():
+            to_slot(f, mine).wait_send()
+    for p in range(n):
+        @pl.when(me != p)
+        def _():
+            to_part(p, me).wait_send()
+    for t in range(n - 1):
+        for s in range(halves):
+            for di, d, dist in ways:
+                @pl.when(t >= dist)
+                def _():
+                    item(di, d, t - dist, s, me, False).wait_send()
+
+
+def final(p, x, gmid, gain, gffn, small, n, groups, cid):
+    rows_own, width = gmid.shape
+    wide = 2 * (width // groups) + 2 * HD
+    vmem = pl.BlockSpec(memory_space=pltpu.VMEM)
+    dma = pltpu.SemaphoreType.DMA
+    return pl.pallas_call(
+        functools.partial(final_kernel, n, groups),
+        out_shape=(
+            jax.ShapeDtypeStruct((rows_own, width), jnp.float32),
+            jax.ShapeDtypeStruct((1, wide), jnp.float32),
+        ),
+        in_specs=[vmem] * 6,
+        out_specs=(vmem, vmem),
+        scratch_shapes=[
+            pltpu.VMEM((2, n - 1, rows_own, width), jnp.bfloat16),
+            pltpu.VMEM((groups, 1, wide), jnp.float32),
+            pltpu.VMEM((groups, 1, wide), jnp.float32),
+            pltpu.VMEM((1, wide), jnp.float32),
+            pltpu.VMEM((n, 1, wide), jnp.float32),
+            dma((2, n - 1, 2)), dma((2, n - 1, 2)), dma((groups,)), dma((groups,)), dma((n,)), dma((n,)),
+        ],
+        compiler_params=pltpu.CompilerParams(
+            collective_id=cid, has_side_effects=True, vmem_limit_bytes=40 << 20
+        ),
+        cost_estimate=pl.CostEstimate(flops=1 << 34, bytes_accessed=200 << 20, transcendentals=0),
+        name="final",
+    )(p, x, gmid, gain, gffn, small)
 
 
 def per_device(
@@ -476,78 +867,45 @@
     middle = own_float + rs(attn_part.astype(jnp.bfloat16), parts, cid=2)
     grad_held, unused_tokens = lax.optimization_barrier((grad_out, tokens_all))
     grad_all = lax.all_gather(grad_held, "tp", axis=0, tiled=True)
-    branch_own = norm_gain(middle, second_gain).astype(jnp.bfloat16)
-    grad_branch_own, ffn_part, grad_w_ffn = ffn(branch_own, grad_all, ffn_set, parts, cid=3)
-    result = middle + lax.psum_scatter(
-        ffn_part, "tp", scatter_dimension=0, tiled=True
-    ).astype(jnp.float32)
-    out = result.astype(jnp.bfloat16)
-    unused_second, pull_second = jax.vjp(norm_gain, middle, second_gain)
-    grad_mid_norm, grad_second = pull_second(grad_branch_own)
-    grad_middle = grad_out.astype(jnp.float32) + grad_mid_norm
-    grad_mid_all = ag(grad_middle.astype(jnp.bfloat16), parts, cid=5)
+    grad_middle, grad_second, ffn_part, grad_w_ffn = ffn(
+        middle, second_gain[None], grad_all, ffn_set, parts, cid=3
+    )
 
     def spread(value):
-        return lax.psum_scatter(
-            value.astype(jnp.bfloat16), "fsdp", scatter_dimension=0, tiled=True
-        ).astype(jnp.float32)
+        return lax.psum_scatter(value, "fsdp", scatter_dimension=0, tiled=True)
 
     ffn_own = spread(grad_w_ffn)
-    grad_mixed = jnp.dot(grad_mid_all, full_out, preferred_element_type=jnp.float32).astype(
-        jnp.bfloat16
-    )
-    grad_w_out = jnp.einsum(
-        "td,th->dh", grad_mid_all, mixed_low, preferred_element_type=jnp.float32
-    )
-    grad_mixed_seq = grad_mixed.reshape(count, length, kv_local, grouping, HD)
-    grads_query, grads_keys, grads_values = lax.map(
-        attend_backward, (query_seq, keys_seq, values_seq, grad_mixed_seq, log_total, prefix_len)
-    )
-    unused_query, pull_query = jax.vjp(
-        functools.partial(head_prep, cosine=cosine, sine=sine), query_raw, query_gain
-    )
-    grad_query_raw, grad_q_gain = pull_query(grads_query.reshape(group_rows, -1, HD))
-    unused_keys, pull_keys = jax.vjp(
-        functools.partial(head_prep, cosine=cosine, sine=sine), keys_raw, key_gain
-    )
-    grad_keys_raw, grad_k_gain = pull_keys(grads_keys.reshape(group_rows, -1, HD))
-    grad_qkv = jnp.concatenate(
-        [
-            grad_query_raw.reshape(group_rows, -1),
-            grad_keys_raw.reshape(group_rows, -1),
-            grads_values.reshape(group_rows, -1),
-        ],
+    cos_all = jnp.concatenate([cosine[:, 0], cosine[:, 0]], axis=1)
+    sin_all = jnp.concatenate([-sine[:, 0], sine[:, 0]], axis=1)
+    heads = query_raw.shape[1]
+    qkv_low = jnp.concatenate(
+        [query_low.reshape(group_rows, -1), keys_low.reshape(group_rows, -1), values_low.reshape(group_rows, -1)],
         axis=1,
-    ).astype(jnp.bfloat16)
-    grad_w_qkv = jnp.einsum("td,th->dh", normed, grad_qkv, preferred_element_type=jnp.float32)
-    grad_normed = jnp.einsum("th,dh->td", grad_qkv, full_qkv, preferred_element_type=jnp.float32)
-    out_own = spread(grad_w_out)
-    qkv_own = spread(grad_w_qkv)
-    grad_normed_own = rs(grad_normed.astype(jnp.bfloat16), parts, cid=6)
-    unused_first, pull_first = jax.vjp(norm_gain, own_float, first_gain)
-    grad_tokens, grad_first = pull_first(grad_normed_own)
-    grad_in = grad_middle + grad_tokens
-    sums = lax.psum(
-        jnp.concatenate([grad_first, grad_second, grad_q_gain, grad_k_gain]), ("fsdp", "tp")
-    )
-    place = lax.axis_index("fsdp")
-    wide = groups * slot
-    narrow = groups * head_slot
-    gain_first = lax.dynamic_slice_in_dim(sums, place * slot, slot)
-    gain_second = lax.dynamic_slice_in_dim(sums, wide + place * slot, slot)
-    gain_query = lax.dynamic_slice_in_dim(sums, 2 * wide + place * head_slot, head_slot)
-    gain_key = lax.dynamic_slice_in_dim(sums, 2 * wide + narrow + place * head_slot, head_slot)
+    )
+    log_rows = jnp.pad(log_total.reshape(heads, group_rows), ((0, 8 - heads), (0, 0)))
+    gain_rows = jnp.pad(jnp.stack([query_gain, key_gain]), ((0, 6), (0, 0)))
+    out, grad_normed, grad_small, grad_w_attn = attn_back(
+        grad_middle, middle, cos_all, sin_all, log_rows, gain_rows, prefix_len, attn_set,
+        normed, qkv_low, raw[:, : qc + kc], mixed_low, ffn_part, parts, heads, kv_local, cid=5,
+    )
+    grad_w_attn, ffn_own = lax.optimization_barrier((grad_w_attn, ffn_own))
+    attn_own = spread(grad_w_attn).astype(jnp.float32)
+    ffn_own = ffn_own.astype(jnp.float32)
+    grad_in, sums = final(
+        grad_normed, hidden_in, grad_middle, first_gain[None], grad_second, grad_small, parts, groups, cid=6
+    )
+    place = lax.axis_index("fsdp") * head_slot
     return (
         out,
         grad_in,
-        gain_first,
-        qkv_own[:, :qc],
-        qkv_own[:, qc : qc + kc],
-        qkv_own[:, qc + kc :],
-        out_own.T,
-        gain_query,
-        gain_key,
-        gain_second,
+        sums[0, :slot],
+        attn_own[:, :qc],
+        attn_own[:, qc : qc + kc],
+        attn_own[:, qc + kc : qc + 2 * kc],
+        attn_own[:, qc + 2 * kc :].T,
+        lax.dynamic_slice_in_dim(sums[0, 2 * slot : 2 * slot + HD], place, head_slot),
+        lax.dynamic_slice_in_dim(sums[0, 2 * slot + HD :], place, head_slot),
+        sums[0, slot : 2 * slot],
         ffn_own[:, :fc],
         ffn_own[:, fc : 2 * fc],
         ffn_own[:, 2 * fc :].T,

time: 902 us -> 666 us (0.74)
  waiting for transfers between devices: 173 us -> 43.1 us
  matrix products: 120 us -> 21.6 us
  Pallas kernels: 427 us -> 474 us
  blocking collectives: 69.8 us -> 24.1 us
  other arithmetic: 50 us -> 35 us
  local copies, waits for them, and re-layouts: 35.7 us -> 46.1 us
    pallas_call x0 -> x2, Pallas kernels: none -> 177 us  [the longest x1 95.9 us: attn_back(): pl.pallas_call(functools.partial(attn_back_kernel, n, axis, heads, kv_hea...]
    reduce_scatter x4 -> x2, waiting for transfers between devices: 143 us -> 14.2 us  [spread(): return lax.psum_scatter(value, 'fsdp', scatter_dimension=0, tiled=True)]
    dot_general x8 -> x0, matrix products: 92.2 us -> none  [the longest x1 25.1 us: attend_backward(): jnp.einsum('kgqp,pkd->qkgd', grad_low, keys, preferred_element_type=jnp.f...]
    pallas_call x2 -> x1, Pallas kernels: 140 us -> 72.7 us  [ag(): pl.pallas_call(functools.partial(ag_kernel, n, S, axis), out_shape=jax.Sh...]
    pallas_call x2 -> x1, Pallas kernels: 130 us -> 65.1 us  [rs(): pl.pallas_call(functools.partial(rs_kernel, n, S, axis), out_shape=jax.Sh...]
    psum x1 -> x0, blocking collectives: 45.8 us -> none  [per_device(): lax.psum(jnp.concatenate([grad_first, grad_second, grad_q_gain, grad_k_ga...]
    unnamed x166 -> x109, local copies, waits for them, and re-layouts: 19.7 us -> 24.6 us
  transfers between devices with their start and end apart: 7 -> 5, of which waited for: 3 -> 2; matrix products, arithmetic and copies ran while one was open for 12% -> 12% of each run, Pallas kernels for 23% -> 48%
where the time goes in v3:
time: 666 us; the launch traced here: 660 us
  Pallas kernels  474 us (71%)
  local copies, waits for them, and re-layouts  46.1 us (7%)
  waiting for transfers between devices  43.1 us (6%)
  other arithmetic  35 us (5%)
  blocking collectives  24.1 us (4%)
  matrix products  21.6 us (3%)
  between operations  16.4 us (2%)
    pallas_call x1, Pallas kernels, ffn(): pl.pallas_call(functools.partial(ffn_kernel, n, axis), out_shape=(jax.Sha...  159 us
    pallas_call x1, Pallas kernels, attn_back(): pl.pallas_call(functools.partial(attn_back_kernel, n, axis, heads, kv_hea...  95.9 us
    pallas_call x1, Pallas kernels, final(): pl.pallas_call(functools.partial(final_kernel, n, groups), out_shape=(jax...  81.3 us
    pallas_call x1, Pallas kernels, ag(): pl.pallas_call(functools.partial(ag_kernel, n, S, axis), out_shape=jax.Sh...  72.7 us
    pallas_call x1, Pallas kernels, rs(): pl.pallas_call(functools.partial(rs_kernel, n, S, axis), out_shape=jax.Sh...  65.1 us
    all_gather x1, waiting for transfers between devices, per_device(): lax.all_gather(jnp.concatenate([w_gate, w_up, w_down.T], axis=1), 'fsdp',...  28.8 us
    unnamed x109, local copies, waits for them, and re-layouts  24.6 us
    unnamed x1, blocking collectives  24.1 us
  transfers between devices with their start and end apart: 5, of which 2 were waited for; matrix products, arithmetic and copies ran while one was open for 12% of the time, Pallas kernels for 48%

profile of v3, /device:TPU:0, one launch (start us, length us, event | category | flops | bytes accessed | tf_op | source)
XLA Modules:
  0.0 660.0 jit_solution(16256068273371722145)
XLA Ops:
  7.2 1.1 copy.42
  8.3 2.1 pad_maximum_fusion.3
  10.5 1.3 copy-done.2
  11.8 72.7 %ag.1 = bf16[1024,2048]{1,0:T(8,128)(2,1)S(1)} custom-call(bf16[256,2048]{1,0:T(8,128)(2,1)S(1)} %copy-done.2), custom_call_target="tpu_custom_call" | custom-call | tf_op jit(solution)/shard_map/ag/pallas_call | solution.py:125
  84.5 2.1 copy-done
  87.0 1.5 pad_maximum_fusion
  90.9 24.1 %all-reduce.2 = bf16[4352]{0:T(1024)(128)(2,1)S(1)} all-reduce(bf16[4352]{0:T(1024)(128)(2,1)S(1)} %dynamic-update-slice), channel_id=2, replica_groups=mesh['fsdp'=8,'tp'=4] {'fsdp'}, use_global_device_ids=true, to_apply=%add.2 | all-reduce | flops 4352 | bytes 17408
  116.5 3.0 fusion.16
  120.6 3.2 fusion.2
  124.2 3.1 fusion.4.normed_hbm
  127.3 8.2 %fusion.6 = f32[1024,1024]{0,1:T(8,128)S(1)} fusion(bf16[1024,2048]{1,0:T(8,128)(2,1)} %fusion.4.normed_hbm, bf16[2048,1536]{1,0:T(8,128)(2,1)} %all-gather.5.cloned.1.call-done.w_hbm), kind=kOutput, calls=%fused_computation.11 | convolution fusion | flops 4294967296 | bytes 12582912 | tf_op jit(solution)/shard_map/dot_general | solution.py:852
  135.5 1.9 copy-done.9
  137.4 1.1 slice.104
  138.7 1.0 copy.61
  139.8 2.5 copy.44
  142.3 1.9 multiply_reduce_fusion
  144.2 2.0 multiply_multiply_fusion
  146.6 1.3 copy.47
  147.9 1.3 copy.48
  149.2 1.5 multiply_reduce_fusion.1
  150.7 1.6 multiply_multiply_fusion.1
  152.8 4.0 fusion.1
  156.9 3.7 fusion
  160.6 5.4 fusion.10
  166.1 1.0 copy-done.27
  167.0 4.0 convolution_convert_fusion.p_ref
  171.0 65.1 %rs.1 = f32[256,2048]{1,0:T(8,128)S(1)} custom-call(bf16[1024,2048]{1,0:T(8,128)(2,1)S(1)} %convolution_convert_fusion.p_ref), custom_call_target="tpu_custom_call" | custom-call | tf_op jit(solution)/shard_map/rs/pallas_call | solution.py:184
  236.1 1.7 convert_add_fusion.mid_ref
  237.8 28.8 %all-gather.9.cloned.1.call-done.w_ref = bf16[2048,4608]{1,0:T(8,128)(2,1)} async-done(((bf16[256,4608]{1,0:T(8,128)(2,1)}), bf16[2048,4608]{1,0:T(8,128)(2,1)}) %all-gather.9.cloned.1.call-update) | async-done | bytes 18874384 | tf_op jit(solution)/shard_map/all_gather | solution.py:844
  266.6 158.7 %ffn.1 = (f32[256,2048]{1,0:T(8,128)}, f32[1,2048]{1,0:T(1,128)}, bf16[1024,2048]{1,0:T(8,128)(2,1)}, bf16[2048,4608]{1,0:T(8,128)(2,1)}) custom-call(f32[256,2048]{1,0:T(8,128)} %convert_add_fusion.mid_ref, f32[1,2048]{1,0:T(1,128)} %bitcast.79, bf16[1024,2048]{1,0:T(8,128)(2,1)} %all-gather.7.cloned.1.call-done.go_ref, ...), custom_call_target="tpu_custom_call" | custom-call | flops 57982058496 | bytes 37748736 | tf_op jit(solution)/shard_map/ffn/pallas_call | solution.py:371
  426.7 1.3 pad_maximum_fusion.4
  428.1 2.7 copy.62.mixed_hbm
  431.4 2.6 copy.65.raw_hbm
  434.0 1.6 pad_maximum_fusion.2
  436.8 1.4 copy_bitcast_fusion
  438.2 1.6 pad_maximum_fusion.1.qkv_hbm
  439.8 95.9 %attn_back.1 = (bf16[256,2048]{1,0:T(8,128)(2,1)}, bf16[1024,2048]{1,0:T(8,128)(2,1)}, f32[8,128]{1,0:T(8,128)}, bf16[2048,1536]{1,0:T(8,128)(2,1)}) custom-call(f32[256,2048]{1,0:T(8,128)} %get-tuple-element.48.gmid_ref, f32[256,2048]{1,0:T(8,128)} %convert_add_fusion.mid_ref, f32[1024,128]{1,0:T(8,128)} %get-tuple-element.108.cos_ref, ...), custom_call_target="tpu_custom_call" | custom-call | flops 8053063680 | bytes 83886080 | tf_op jit(solution)/shard_map/attn_back/pallas_call | solution.py:612
  535.7 14.2 %reduce-scatter.3.cloned.1.call-done = bf16[256,4608]{1,0:T(8,128)(2,1)} async-done(((bf16[2048,4608]{1,0:T(8,128)(2,1)}), bf16[256,4608]{1,0:T(8,128)(2,1)}) %reduce-scatter.3.cloned.1.call-update) | async-done | bytes 2359312 | tf_op jit(solution)/shard_map/reduce_scatter | solution.py:875
  550.1 2.2 copy-done.5
  552.2 1.6 copy-done.6
  553.8 81.3 %final.1 = (f32[256,2048]{1,0:T(8,128)S(1)}, f32[1,768]{1,0:T(1,128)S(1)}) custom-call(bf16[1024,2048]{1,0:T(8,128)(2,1)S(1)} %copy-done.5, bf16[256,2048]{1,0:T(8,128)(2,1)S(1)} %copy-done.4, f32[256,2048]{1,0:T(8,128)S(1)} %copy-done.6, f32[1,2048]{1,0:T(1,128)S(1)} %bitcast.68, f32[1,2048]{1,0:T(1,128)S(1)} %copy-done.8, f32[8,128]{1,0:T(8,128)S(1)} %copy-done.7), custom_call_target="tpu_custom_call" | custom-call | flops 17179869184 | bytes 209715200 | tf_op jit(solution)/shard_map/final/pallas_call | solution.py:783
  637.5 1.3 slice_bitcast_fusion
  638.7 3.0 copy.57
  641.8 3.4 fusion.20
  645.2 1.4 convert_element_type.66
  646.6 1.0 copy.56
  649.3 2.3 copy.75
  651.6 1.3 copy.76
  (144 shorter events, 12.9 us)
Async XLA Ops:
  7.2 120.1 %all-gather.5.cloned.1.call-start = ((), (), s32[]{:S(2)}) async-start(), calls=%async_computation.2 | async-start | bytes 7077888 | tf_op jit(solution)/shard_map/all_gather | solution.py:839
  8.3 78.4 %copy-start.30 = (bf16[1536,256]{1,0:T(8,128)(2,1)S(1)}, bf16[1536,256]{1,0:T(8,128)(2,1)}, u32[]{:S(2)}) copy-start(bf16[1536,256]{1,0:T(8,128)(2,1)} %param.29) | copy-start | bytes 2359300
  10.4 76.6 %copy-start.28 = (bf16[256,1536]{1,0:T(8,128)(2,1)S(1)}, bf16[256,1536]{1,0:T(8,128)(2,1)}, u32[]{:S(2)}) copy-start(bf16[256,1536]{1,0:T(8,128)(2,1)} %param.28) | copy-start | bytes 2359300
  10.4 227.4 %all-gather.7.cloned.1.call-start = ((), (), s32[]{:S(2)}) async-start(), calls=%async_computation.3 | async-start | bytes 5242880 | tf_op jit(solution)/shard_map/all_gather | solution.py:869
  11.8 75.2 %copy-start.29 = (bf16[256,1536]{1,0:T(8,128)(2,1)S(1)}, bf16[256,1536]{1,0:T(8,128)(2,1)}, u32[]{:S(2)}) copy-start(bf16[256,1536]{1,0:T(8,128)(2,1)} %param.27) | copy-start | bytes 2359300
  84.4 2.1 copy-start
  86.6 2.7 copy-start.41
  86.6 2.7 copy-start.46
  86.6 4.0 copy-start.42
  86.6 3.9 copy-start.43
  86.6 3.9 copy-start.44
  86.6 3.9 copy-start.45
  86.6 179.9 %all-gather.9.cloned.1.call-start = ((), (), s32[]{:S(2)}) async-start(), calls=%async_computation.4 | async-start | bytes 21233664 | tf_op jit(solution)/shard_map/all_gather | solution.py:844
  88.6 461.4 %reduce-scatter.3.cloned.1.call-start = ((), (), s32[]{:S(2)}) async-start(), calls=%async_computation.5 | async-start | bytes 21233664 | tf_op jit(solution)/shard_map/reduce_scatter | solution.py:875
  115.1 1.4 copy-start.38
  119.4 32.8 %copy-start.11 = (f32[1024,64]{1,0:T(8,128)}, f32[1024,64]{1,0:T(8,128)S(1)}, u32[]{:S(2)}) copy-start(f32[1024,64]{1,0:T(8,128)S(1)} %get-tuple-element.100) | copy-start | bytes 786436
  119.5 32.8 %copy-start.13 = (f32[1024,64]{1,0:T(8,128)}, f32[1024,64]{1,0:T(8,128)S(1)}, u32[]{:S(2)}) copy-start(f32[1024,64]{1,0:T(8,128)S(1)} %get-tuple-element.101) | copy-start | bytes 786436
  120.5 3.6 copy-start.1
  135.4 2.0 copy-start.9
  138.7 5.4 copy-start.17
  142.3 3.9 copy-start.24
  146.6 6.2 copy-start.15
  146.6 6.2 copy-start.16
  149.2 3.6 copy-start.25
  149.2 3.6 copy-start.26
  152.8 4.1 copy-start.21
  152.8 4.1 copy-start.23
  156.9 3.7 copy-start.32
  156.9 3.7 copy-start.31
  160.6 5.5 copy-start.34
  171.0 65.1 %copy-start.3 = (bf16[256,2048]{1,0:T(8,128)(2,1)S(1)}, bf16[256,2048]{1,0:T(8,128)(2,1)}, u32[]{:S(2)}) copy-start(bf16[256,2048]{1,0:T(8,128)(2,1)} %x_ref.3) | copy-start | bytes 3145732
  425.3 1.4 copy-start.12
  425.3 1.4 copy-start.14
  425.3 1.4 copy-start.20
  425.4 219.8 %reduce-scatter.5.cloned.1.call-start = ((), (), s32[]{:S(2)}) async-start(), calls=%async_computation.6 | async-start | bytes 7077888 | tf_op jit(solution)/shard_map/reduce_scatter | solution.py:875
  428.1 3.3 slice-start
  431.4 4.8 copy-start.33
  431.4 4.8 copy-start.35
  433.9 2.9 copy-start.22
  433.9 4.3 copy-start.18
  535.7 14.3 %copy-start.40 = (f32[1,1,8,256]{3,2,1,0:T(8,128)S(1)}, f32[1,1,8,256]{3,2,1,0:T(8,128)}, u32[]{:S(2)}) copy-start(f32[1,1,8,256]{3,2,1,0:T(8,128)} %get-tuple-element.94) | copy-start | bytes 24580
  535.7 14.3 %copy-start.4 = (bf16[256,2048]{1,0:T(8,128)(2,1)S(1)}, bf16[256,2048]{1,0:T(8,128)(2,1)}, u32[]{:S(2)}) copy-start(bf16[256,2048]{1,0:T(8,128)(2,1)} %x_ref.3) | copy-start | bytes 3145732
  535.7 14.3 %copy-start.7 = (f32[8,128]{1,0:T(8,128)S(1)}, f32[8,128]{1,0:T(8,128)}, u32[]{:S(2)}) copy-start(f32[8,128]{1,0:T(8,128)} %get-tuple-element.53.small_ref) | copy-start | bytes 12292
  535.7 14.3 %copy-start.8 = (f32[1,2048]{1,0:T(1,128)S(1)}, f32[1,2048]{1,0:T(1,128)}, u32[]{:S(2)}) copy-start(f32[1,2048]{1,0:T(1,128)} %get-tuple-element.52.gffn_ref) | copy-start | bytes 24580
  550.1 2.2 copy-start.5
  552.2 1.6 copy-start.6
  553.8 83.1 %copy-start.10 = (bf16[256,4608]{1,0:T(8,128)(2,1)S(1)}, bf16[256,4608]{1,0:T(8,128)(2,1)}, u32[]{:S(2)}) copy-start(bf16[256,4608]{1,0:T(8,128)(2,1)} %reduce-scatter.3.cloned.1.call-done) | copy-start | bytes 7077892
  645.2 2.4 copy-start.19
  (5 other events, 5.1 us)
Sparse Core Ops, SparseCore 0:
  10.6 48.1 all-gather.4
  86.7 80.8 all-gather.6
  169.5 97.0 all-gather.8
  425.5 124.4 reduce-scatter.2
  553.2 61.7 reduce-scatter.4

commit v4 on v3

--- a/solution.py
+++ b/solution.py
@@ -18,57 +18,13 @@
 ROPE_BASE = 1000000.0
 
 
-def rms_scale(value):
-    return lax.rsqrt(jnp.mean(value * value, axis=-1, keepdims=True) + EPS)
-
-
-def norm_gain(value, gain):
-    return value * rms_scale(value) * gain
-
-
 def rope_tables(places):
     half = HD // 2
     ladder = jnp.arange(half, dtype=jnp.float32) * (2.0 / HD)
     frequency = jnp.exp(-ladder * math.log(ROPE_BASE))
     angle = places.astype(jnp.float32)[:, None] * frequency[None, :]
-    return (jnp.cos(angle)[:, None, :], jnp.sin(angle)[:, None, :])
-
-
-def rotate(value, cosine, sine):
-    half = value.shape[-1] // 2
-    first = value[..., :half]
-    second = value[..., half:]
-    return jnp.concatenate(
-        [first * cosine - second * sine, second * cosine + first * sine], axis=-1
-    )
-
-
-def head_prep(raw, gain, cosine, sine):
-    return rotate(norm_gain(raw, gain), cosine, sine)
-
-
-def visibility(length, prefix):
-    places = jnp.arange(length, dtype=jnp.int32)
-    return (places[None, :] <= places[:, None]) | (places[None, :] < prefix)
-
-
-def masked_scores(query, keys, prefix):
-    scale = 1.0 / math.sqrt(HD)
-    scores = jnp.einsum("qkgd,pkd->kgqp", query, keys, preferred_element_type=jnp.float32) * scale
-    return jnp.where(visibility(query.shape[0], prefix), scores, -1e30)
-
-
-def attend_forward(item):
-    query, keys, values, prefix = item
-    scores = masked_scores(query, keys, prefix)
-    peak = jnp.max(scores, axis=-1, keepdims=True)
-    raised = jnp.exp(scores - peak)
-    total = jnp.sum(raised, axis=-1, keepdims=True)
-    shares = raised / total
-    mixed = jnp.einsum(
-        "kgqp,pkd->qkgd", shares.astype(jnp.bfloat16), values, preferred_element_type=jnp.float32
-    )
-    return (mixed, (peak + jnp.log(total))[..., 0])
+    cosine, sine = jnp.cos(angle), jnp.sin(angle)
+    return jnp.concatenate([cosine, cosine], axis=1), jnp.concatenate([-sine, sine], axis=1)
 
 
 def greet(me, n, axis):
@@ -90,103 +46,315 @@
 def inside(v, n):
     return (v >= 0) & (v < n)
 
-def ag_kernel(n, S, axis, x_ref, o_ref, send_sem, recv_sem):
-    me = lax.axis_index(axis)
-    R = x_ref.shape[0]; sub = R // S
-    greet(me, n, axis)
-    def rows(j, s):
-        return pl.ds(pl.multiple_of(j * R + s * sub, sub), sub)
-    def item(di, d, k, s, sender):
+def exchange_plan(n, me):
+    return ((0, 1, me), (1, -1, n - 1 - me))
+
+
+def dot_t(left, right):
+    return lax.dot_general(left, right, (((1,), (1,)), ((), ())), preferred_element_type=jnp.float32)
+
+
+def entry_kernel(
+    n, groups, head_slot, x_ref, pack_ref, normed_ref, gattn_ref, gffn_ref, small_ref,
+    tokens, grecv, send_sem, recv_sem, gs_sem, gr_sem,
+):
+    me = lax.axis_index("tp")
+    mine = lax.axis_index("fsdp")
+    rows_own, width = x_ref.shape
+    slot = width // groups
+    barrier = pltpu.get_barrier_semaphore()
+    for f in range(groups):
+        @pl.when(mine != f)
+        def _():
+            pl.semaphore_signal(barrier, inc=1, device_id={"fsdp": f}, device_id_type=MESH)
+    for d in (1, -1):
+        @pl.when(inside(me + d, n))
+        def _():
+            pl.semaphore_signal(barrier, inc=1, device_id={"tp": me + d}, device_id_type=MESH)
+    edge = (me == 0) | (me == n - 1)
+
+    @pl.when(edge)
+    def _():
+        pl.semaphore_wait(barrier, groups)
+
+    @pl.when(~edge)
+    def _():
+        pl.semaphore_wait(barrier, groups + 1)
+
+    def block(j):
+        return pl.ds(pl.multiple_of(j * rows_own, rows_own), rows_own)
+
+    def passing(di, d, k, sender):
         j = sender - d * k
-        src = x_ref.at[pl.ds(s * sub, sub)] if k == 0 else o_ref.at[rows(j, s)]
-        return pltpu.make_async_remote_copy(src_ref=src, dst_ref=o_ref.at[rows(j, s)], send_sem=send_sem.at[di, k, s], recv_sem=recv_sem.at[di, k, s], device_id={axis: sender + d}, device_id_type=MESH)
-    for k in range(n):
-        for s in range(S):
-            for di, d in enumerate((1, -1)):
-                if k > 0:
-                    @pl.when(inside(me - d * k, n))
-                    def _():
-                        item(di, d, k - 1, s, me - d).wait_recv()
-                if k < n - 1:
-                    @pl.when(inside(me - d * k, n) & inside(me + d, n))
-                    def _():
-                        item(di, d, k, s, me).start()
-        if k == 0:
-            o_ref[pl.ds(pl.multiple_of(me * R, R), R), :] = x_ref[...]
-    for k in range(n - 1):
-        for s in range(S):
-            for di, d in enumerate((1, -1)):
+        src = x_ref if k == 0 else tokens.at[block(j)]
+        return pltpu.make_async_remote_copy(
+            src_ref=src, dst_ref=tokens.at[block(j)], send_sem=send_sem.at[di, k], recv_sem=recv_sem.at[di, k],
+            device_id={"tp": sender + d}, device_id_type=MESH,
+        )
+
+    def to_peer(f, sender):
+        return pltpu.make_async_remote_copy(
+            src_ref=pack_ref, dst_ref=grecv.at[sender], send_sem=gs_sem.at[f], recv_sem=gr_sem.at[sender],
+            device_id={"fsdp": f}, device_id_type=MESH,
+        )
+
+    sides = ((0, 1), (1, -1))
+    for di, d in sides:
+        @pl.when(inside(me + d, n))
+        def _():
+            passing(di, d, 0, me).start()
+    for f in range(groups):
+        @pl.when(mine != f)
+        def _():
+            to_peer(f, mine).start()
+    grecv[mine] = pack_ref[...]
+    for f in range(groups):
+        @pl.when(mine != f)
+        def _():
+            to_peer(f, f).wait_recv()
+    small_ref[...] = jnp.zeros_like(small_ref)
+    for f in range(groups):
+        at = slice(f * slot, (f + 1) * slot)
+        gattn_ref[:, at] = grecv[f, :, :slot]
+        gffn_ref[:, at] = grecv[f, :, slot : 2 * slot]
+        for row in range(2):
+            part = grecv[f, :, 2 * slot + row * HD : 2 * slot + (row + 1) * HD]
+            small_ref[row : row + 1, :] += part if f == 0 else pltpu.roll(part, f * head_slot, 1)
+
+    def normalize(source, at):
+        value = source.astype(jnp.float32)
+        inverse = lax.rsqrt(jnp.mean(value * value, axis=-1, keepdims=True) + EPS)
+        normed_ref[at, :] = (value * inverse * gattn_ref[...]).astype(jnp.bfloat16)
+
+    normalize(x_ref[...], block(me))
+    for k in range(1, n):
+        for di, d in sides:
+            @pl.when(inside(me - d * k, n))
+            def _():
+                passing(di, d, k - 1, me - d).wait_recv()
+            if k < n - 1:
                 @pl.when(inside(me - d * k, n) & inside(me + d, n))
                 def _():
-                    item(di, d, k, s, me).wait_send()
-
-def ag(x, n, S=2, axis="tp", cid=1):
-    R, D = x.shape
-    return pl.pallas_call(functools.partial(ag_kernel, n, S, axis),
-        out_shape=jax.ShapeDtypeStruct((n * R, D), x.dtype),
-        in_specs=[pl.BlockSpec(memory_space=pltpu.VMEM)],
-        out_specs=pl.BlockSpec(memory_space=pltpu.VMEM),
-        scratch_shapes=[pltpu.SemaphoreType.DMA((2, n - 1, S)), pltpu.SemaphoreType.DMA((2, n - 1, S))],
-        compiler_params=pltpu.CompilerParams(collective_id=cid, has_side_effects=True, vmem_limit_bytes=32 << 20), name="ag")(x)
-
-def rs_kernel(n, S, axis, p_ref, o_ref, rb, send_sem, recv_sem):
+                    passing(di, d, k, me).start()
+        for di, d in sides:
+            @pl.when(inside(me - d * k, n))
+            def _():
+                normalize(tokens[block(me - d * k), :], block(me - d * k))
+    for k in range(n - 1):
+        for di, d in sides:
+            @pl.when(inside(me - d * k, n) & inside(me + d, n))
+            def _():
+                passing(di, d, k, me).wait_send()
+    for f in range(groups):
+        @pl.when(mine != f)
+        def _():
+            to_peer(f, mine).wait_send()
+
+
+def entry(x, pack, n, groups, head_slot, cid):
+    rows_own, width = x.shape
+    vmem = pl.BlockSpec(memory_space=pltpu.VMEM)
+    dma = pltpu.SemaphoreType.DMA
+    return pl.pallas_call(
+        functools.partial(entry_kernel, n, groups, head_slot),
+        out_shape=(
+            jax.ShapeDtypeStruct((rows_own * n, width), jnp.bfloat16),
+            jax.ShapeDtypeStruct((1, width), jnp.float32),
+            jax.ShapeDtypeStruct((1, width), jnp.float32),
+            jax.ShapeDtypeStruct((8, HD), jnp.float32),
+        ),
+        in_specs=[vmem] * 2,
+        out_specs=(vmem,) * 4,
+        scratch_shapes=[
+            pltpu.VMEM((rows_own * n, width), jnp.bfloat16),
+            pltpu.VMEM((groups,) + pack.shape, jnp.float32),
+            dma((2, n - 1)), dma((2, n - 1)), dma((groups,)), dma((groups,)),
+        ],
+        compiler_params=pltpu.CompilerParams(
+            collective_id=cid, has_side_effects=True, vmem_limit_bytes=32 << 20
+        ),
+        cost_estimate=pl.CostEstimate(flops=1 << 34, bytes_accessed=200 << 20, transcendentals=0),
+        name="entry",
+    )(x, pack)
+
+
+def attn_kernel(
+    n, axis, heads, kv_heads,
+    x_ref, go_ref, normed_ref, cos_ref, sin_ref, gain_ref, prefix_ref, w_hbm,
+    mid_ref, go_all, qkv, raw, mixed, lse_ref,
+    wbuf, part, values_t, rb, load_sem, send_ag, recv_ag, send_rs, recv_rs,
+):
     me = lax.axis_index(axis)
-    R = o_ref.shape[0]; sub = R // S
+    rows_own, width = x_ref.shape
+    total = rows_own * n
+    qc, kc = heads * HD, kv_heads * HD
+    group = heads // kv_heads
+    scale = 1.0 / math.sqrt(HD)
+    load = pltpu.make_async_copy(w_hbm, wbuf, load_sem.at[0])
+    load.start()
     greet(me, n, axis)
-    def rows(j, s):
-        return pl.ds(pl.multiple_of(j * R + s * sub, sub), sub)
-    def at(s):
-        return pl.ds(s * sub, sub)
+
+    def block(j):
+        return pl.ds(pl.multiple_of(j * rows_own, rows_own), rows_own)
+
+    def passing(di, d, k, sender):
+        j = sender - d * k
+        src = go_ref if k == 0 else go_all.at[block(j)]
+        return pltpu.make_async_remote_copy(
+            src_ref=src, dst_ref=go_all.at[block(j)], send_sem=send_ag.at[di, k], recv_sem=recv_ag.at[di, k],
+            device_id={axis: sender + d}, device_id_type=MESH,
+        )
+
     def owner(d, q):
         return n - 1 - q if d > 0 else q
-    def item(di, d, q, s, sender, first):
-        src = p_ref.at[rows(owner(d, q), s)] if first else rb.at[di, q, at(s)]
-        return pltpu.make_async_remote_copy(src_ref=src, dst_ref=rb.at[di, q, at(s)], send_sem=send_sem.at[di, q, s], recv_sem=recv_sem.at[di, q, s], device_id={axis: sender + d}, device_id_type=MESH)
-    ways = ((0, 1, me), (1, -1, n - 1 - me))
-    for q in range(n - 1):
-        for s in range(S):
-            for di, d, dist in ways:
-                @pl.when(dist == 0)
+
+    def item(di, d, q, sender, first):
+        src = part.at[block(owner(d, q))] if first else rb.at[di, q]
+        return pltpu.make_async_remote_copy(
+            src_ref=src, dst_ref=rb.at[di, q], send_sem=send_rs.at[di, q], recv_sem=recv_rs.at[di, q],
+            device_id={axis: sender + d}, device_id_type=MESH,
+        )
+
+    sides = ((0, 1), (1, -1))
+    ways = exchange_plan(n, me)
+
+    def gather_step(k):
+        for di, d in sides:
+            if k > 0:
+                @pl.when(inside(me - d * k, n))
                 def _():
-                    item(di, d, q, s, me, True).start()
-    for t in range(1, n - 1):
-        for s in range(S):
-            for di, d, dist in ways:
-                @pl.when((dist > 0) & (t >= dist))
+                    passing(di, d, k - 1, me - d).wait_recv()
+            if k < n - 1:
+                @pl.when(inside(me - d * k, n) & inside(me + d, n))
                 def _():
-                    q = t - dist
-                    item(di, d, q, s, me - d, False).wait_recv()
-                    rb[di, q, at(s), :] = (rb[di, q, at(s), :].astype(jnp.float32) + p_ref[rows(owner(d, q), s), :].astype(jnp.float32)).astype(rb.dtype)
-                    item(di, d, q, s, me, False).start()
-    for s in range(S):
+                    passing(di, d, k, me).start()
+
+    def sums_step(t):
         for di, d, dist in ways:
-            @pl.when(dist > 0)
-            def _():
-                item(di, d, n - 1 - dist, s, me - d, False).wait_recv()
-        @pl.when(me == 0)
-        def _():
-            o_ref[at(s), :] = p_ref[rows(0, s), :].astype(jnp.float32) + rb[1, 0, at(s), :].astype(jnp.float32)
-        @pl.when(me == n - 1)
-        def _():
-            o_ref[at(s), :] = p_ref[rows(n - 1, s), :].astype(jnp.float32) + rb[0, 0, at(s), :].astype(jnp.float32)
-        @pl.when((me > 0) & (me < n - 1))
-        def _():
-            o_ref[at(s), :] = p_ref[rows(me, s), :].astype(jnp.float32) + rb[0, n - 1 - me, at(s), :].astype(jnp.float32) + rb[1, me, at(s), :].astype(jnp.float32)
-    for t in range(0, n - 1):
-        for s in range(S):
-            for di, d, dist in ways:
-                @pl.when(t >= dist)
-                def _():
-                    item(di, d, t - dist, s, me, False).wait_send()
-
-def rs(p, n, S=2, axis="tp", cid=2):
-    NR, D = p.shape; R = NR // n
-    return pl.pallas_call(functools.partial(rs_kernel, n, S, axis),
-        out_shape=jax.ShapeDtypeStruct((R, D), jnp.float32),
-        in_specs=[pl.BlockSpec(memory_space=pltpu.VMEM)],
-        out_specs=pl.BlockSpec(memory_space=pltpu.VMEM),
-        scratch_shapes=[pltpu.VMEM((2, n - 1, R, D), p.dtype), pltpu.SemaphoreType.DMA((2, n - 1, S)), pltpu.SemaphoreType.DMA((2, n - 1, S))],
-        compiler_params=pltpu.CompilerParams(collective_id=cid, has_side_effects=True, vmem_limit_bytes=32 << 20), name="rs")(p)
+            @pl.when((dist > 0) & (t >= dist))
+            def _():
+                q = t - dist
+                item(di, d, q, me - d, False).wait_recv()
+                rb[di, q] = (rb[di, q].astype(jnp.float32) + part[block(owner(d, q)), :].astype(jnp.float32)).astype(rb.dtype)
+                item(di, d, q, me, False).start()
+
+    gather_step(0)
+    go_all[block(me), :] = go_ref[...]
+    lse_ref[...] = jnp.zeros_like(lse_ref)
+    load.wait()
+
+    def project(j, carry):
+        at = block(j)
+        value = jnp.dot(normed_ref[at, :], wbuf[:, : qc + 2 * kc], preferred_element_type=jnp.float32)
+        raw[at, :] = value[:, : qc + kc]
+        for h in range(heads + kv_heads):
+            head = value[:, h * HD : (h + 1) * HD]
+            gain = gain_ref[0:1, :] if h < heads else gain_ref[1:2, :]
+            scaled = head * lax.rsqrt(jnp.mean(head * head, axis=-1, keepdims=True) + EPS) * gain
+            turned = scaled * cos_ref[at, :] + pltpu.roll(scaled, HD // 2, 1) * sin_ref[at, :]
+            qkv[at, h * HD : (h + 1) * HD] = turned.astype(jnp.bfloat16)
+        qkv[at, qc + kc :] = value[:, qc + kc :].astype(jnp.bfloat16)
+        return carry
+
+    lax.fori_loop(0, n, project, 0)
+    for g in range(kv_heads):
+        values_t[g] = qkv[:, qc + kc + g * HD : qc + kc + (g + 1) * HD].T
+    prefix = prefix_ref[0]
+
+    def attend(i, carry):
+        @pl.when(i == 2)
+        def _():
+            gather_step(1)
+        j = jnp.where(2 * me < n, n - 1 - i, i)
+        at = block(j)
+        key_at = lax.broadcasted_iota(jnp.int32, (total, rows_own), 0)
+        query_at = lax.broadcasted_iota(jnp.int32, (total, rows_own), 1) + j * rows_own
+        seen = (key_at <= query_at) | (key_at < prefix)
+        for h in range(heads):
+            g = h // group
+            ks, hs = qc + g * HD, h * HD
+            scores = jnp.where(seen, dot_t(qkv[:, ks : ks + HD], qkv[at, hs : hs + HD]) * scale, -1e30)
+            peak = jnp.max(scores, axis=0, keepdims=True)
+            raised = jnp.exp(scores - peak)
+            weight = jnp.sum(raised, axis=0, keepdims=True)
+            lse_ref[h : h + 1, at] = peak + jnp.log(weight)
+            shares = (raised * (1.0 / weight)).astype(jnp.bfloat16)
+            mixed[at, hs : hs + HD] = jnp.dot(values_t[g], shares, preferred_element_type=jnp.float32).T.astype(jnp.bfloat16)
+        cut = width // 4
+        for f in range(4):
+            cols = pl.ds(f * cut, cut)
+            part[at, cols] = dot_t(mixed[at, :], wbuf[cols, qc + 2 * kc :]).astype(jnp.bfloat16)
+        for di, d, dist in ways:
+            @pl.when((dist == 0) & (i < n - 1))
+            def _():
+                item(di, d, i, me, True).start()
+        return carry
+
+    lax.fori_loop(0, n, attend, 0)
+    for t in range(1, n):
+        if t < n - 1:
+            sums_step(t)
+        if t + 1 < n:
+            gather_step(t + 1)
+    for di, d, dist in ways:
+        @pl.when(dist > 0)
+        def _():
+            item(di, d, n - 1 - dist, me - d, False).wait_recv()
+    own = x_ref[...].astype(jnp.float32) + part[block(me), :].astype(jnp.float32)
+    @pl.when(me == 0)
+    def _():
+        mid_ref[...] = own + rb[1, 0].astype(jnp.float32)
+    @pl.when(me == n - 1)
+    def _():
+        mid_ref[...] = own + rb[0, 0].astype(jnp.float32)
+    @pl.when((me > 0) & (me < n - 1))
+    def _():
+        mid_ref[...] = own + rb[0, n - 1 - me].astype(jnp.float32) + rb[1, me].astype(jnp.float32)
+    for k in range(n - 1):
+        for di, d in sides:
+            @pl.when(inside(me - d * k, n) & inside(me + d, n))
+            def _():
+                passing(di, d, k, me).wait_send()
+    for t in range(n - 1):
+        for di, d, dist in ways:
+            @pl.when(t >= dist)
+            def _():
+                item(di, d, t - dist, me, False).wait_send()
+
+
+def attn(x, go, normed, cos2, sin2, gains, prefix, w, n, heads, kv_heads, cid, axis="tp"):
+    rows_own, width = x.shape
+    total = rows_own * n
+    vmem = pl.BlockSpec(memory_space=pltpu.VMEM)
+    any_space = pl.BlockSpec(memory_space=pl.ANY)
+    dma = pltpu.SemaphoreType.DMA
+    cols = (heads + 2 * kv_heads) * HD
+    return pl.pallas_call(
+        functools.partial(attn_kernel, n, axis, heads, kv_heads),
+        out_shape=(
+            jax.ShapeDtypeStruct((rows_own, width), jnp.float32),
+            jax.ShapeDtypeStruct((total, width), jnp.bfloat16),
+            jax.ShapeDtypeStruct((total, cols), jnp.bfloat16),
+            jax.ShapeDtypeStruct((total, cols - kv_heads * HD), jnp.float32),
+            jax.ShapeDtypeStruct((total, heads * HD), jnp.bfloat16),
+            jax.ShapeDtypeStruct((8, total), jnp.float32),
+        ),
+        in_specs=[vmem] * 6 + [pl.BlockSpec(memory_space=pltpu.SMEM), any_space],
+        out_specs=(vmem,) * 6,
+        scratch_shapes=[
+            pltpu.VMEM(w.shape, jnp.bfloat16),
+            pltpu.VMEM((total, width), jnp.bfloat16),
+            pltpu.VMEM((kv_heads, HD, total), jnp.bfloat16),
+            pltpu.VMEM((2, n - 1, rows_own, width), jnp.bfloat16),
+            dma((1,)), dma((2, n - 1)), dma((2, n - 1)), dma((2, n - 1)), dma((2, n - 1)),
+        ],
+        compiler_params=pltpu.CompilerParams(
+            collective_id=cid, has_side_effects=True, vmem_limit_bytes=VMEM_LIMIT
+        ),
+        cost_estimate=pl.CostEstimate(flops=1 << 34, bytes_accessed=300 << 20, transcendentals=0),
+        name="attn",
+    )(x, go, normed, cos2, sin2, gains, prefix, w)
+
 
 def ffn_kernel(
     n, axis, mid_ref, gain_ref, go_ref, w_ref, gmid_ref, gffn_ref, part_ref, gw_ref,
@@ -355,10 +523,6 @@
     for m in range(3):
         for r in range(4):
             leave(m, r).wait()
-
-
-def dot_t(left, right):
-    return lax.dot_general(left, right, (((1,), (1,)), ((), ())), preferred_element_type=jnp.float32)
 
 
 def ffn(mid, gain, go, w, n, cid, axis="tp"):
@@ -394,10 +558,6 @@
         ),
         name="ffn",
     )(mid, gain, go, w)
-
-
-def exchange_plan(n, me):
-    return ((0, 1, me), (1, -1, n - 1 - me))
 
 
 def unroll_rot(value, cos2, sin2):
@@ -823,76 +983,46 @@
 ):
     parts = lax.axis_size("tp")
     groups = lax.axis_size("fsdp")
-    own_rows, width = hidden_in.shape
-    group_rows = own_rows * parts
-    count = prefix_len.shape[0]
-    length = group_rows // count
     qc, kc, fc = w_query.shape[1], w_key.shape[1], w_gate.shape[1]
     slot = g_attn.shape[0]
     head_slot = q_gain.shape[0]
-    packed = jnp.concatenate([g_attn, g_ffn, q_gain, k_gain])[None]
-    gains = lax.all_gather(packed, "fsdp", axis=0, tiled=True).astype(jnp.float32)
-    first_gain = gains[:, :slot].reshape(-1)
-    second_gain = gains[:, slot : 2 * slot].reshape(-1)
-    query_gain = gains[:, 2 * slot : 2 * slot + head_slot].reshape(-1)
-    key_gain = gains[:, 2 * slot + head_slot :].reshape(-1)
     attn_set = lax.all_gather(
         jnp.concatenate([w_query, w_key, w_value, w_out.T], axis=1), "fsdp", axis=0, tiled=True
     )
-    full_qkv = attn_set[:, : qc + 2 * kc]
-    full_out = attn_set[:, qc + 2 * kc :]
     ffn_set = lax.all_gather(
         jnp.concatenate([w_gate, w_up, w_down.T], axis=1), "fsdp", axis=0, tiled=True
     )
 
-    tokens_all = ag(hidden_in, parts, cid=1)
-    tokens_float = tokens_all.astype(jnp.float32)
-    own_float = hidden_in.astype(jnp.float32)
-    normed = norm_gain(tokens_float, first_gain).astype(jnp.bfloat16)
-    raw = jnp.dot(normed, full_qkv, preferred_element_type=jnp.float32)
-    query_raw = raw[:, :qc].reshape(group_rows, -1, HD)
-    keys_raw = raw[:, qc : qc + kc].reshape(group_rows, -1, HD)
-    values_low = raw[:, qc + kc :].astype(jnp.bfloat16).reshape(group_rows, -1, HD)
-    kv_local = keys_raw.shape[1]
-    grouping = query_raw.shape[1] // kv_local
-    cosine, sine = rope_tables(positions)
-    query_low = head_prep(query_raw, query_gain, cosine, sine).astype(jnp.bfloat16)
-    keys_low = head_prep(keys_raw, key_gain, cosine, sine).astype(jnp.bfloat16)
-    query_seq = query_low.reshape(count, length, kv_local, grouping, HD)
-    keys_seq = keys_low.reshape(count, length, kv_local, HD)
-    values_seq = values_low.reshape(count, length, kv_local, HD)
-    mixed, log_total = lax.map(attend_forward, (query_seq, keys_seq, values_seq, prefix_len))
-    mixed_low = mixed.reshape(group_rows, -1).astype(jnp.bfloat16)
-    attn_part = jnp.einsum("th,dh->td", mixed_low, full_out, preferred_element_type=jnp.float32)
-    middle = own_float + rs(attn_part.astype(jnp.bfloat16), parts, cid=2)
-    grad_held, unused_tokens = lax.optimization_barrier((grad_out, tokens_all))
-    grad_all = lax.all_gather(grad_held, "tp", axis=0, tiled=True)
+    def lane_pad(value):
+        return jnp.pad(value.astype(jnp.float32), (0, HD - head_slot))
+
+    packed = jnp.concatenate(
+        [g_attn.astype(jnp.float32), g_ffn.astype(jnp.float32), lane_pad(q_gain), lane_pad(k_gain)]
+    )[None]
+    heads, kv_heads = qc // HD, kc // HD
+    cos_all, sin_all = rope_tables(positions)
+    normed, gain_first, gain_second, gain_rows = entry(hidden_in, packed, parts, groups, head_slot, cid=1)
+    middle, grad_all, qkv_low, raw, mixed_low, log_rows = attn(
+        hidden_in, grad_out, normed, cos_all, sin_all, gain_rows, prefix_len, attn_set,
+        parts, heads, kv_heads, cid=2,
+    )
     grad_middle, grad_second, ffn_part, grad_w_ffn = ffn(
-        middle, second_gain[None], grad_all, ffn_set, parts, cid=3
+        middle, gain_second, grad_all, ffn_set, parts, cid=3
     )
 
     def spread(value):
         return lax.psum_scatter(value, "fsdp", scatter_dimension=0, tiled=True)
 
     ffn_own = spread(grad_w_ffn)
-    cos_all = jnp.concatenate([cosine[:, 0], cosine[:, 0]], axis=1)
-    sin_all = jnp.concatenate([-sine[:, 0], sine[:, 0]], axis=1)
-    heads = query_raw.shape[1]
-    qkv_low = jnp.concatenate(
-        [query_low.reshape(group_rows, -1), keys_low.reshape(group_rows, -1), values_low.reshape(group_rows, -1)],
-        axis=1,
-    )
-    log_rows = jnp.pad(log_total.reshape(heads, group_rows), ((0, 8 - heads), (0, 0)))
-    gain_rows = jnp.pad(jnp.stack([query_gain, key_gain]), ((0, 6), (0, 0)))
     out, grad_normed, grad_small, grad_w_attn = attn_back(
         grad_middle, middle, cos_all, sin_all, log_rows, gain_rows, prefix_len, attn_set,
-        normed, qkv_low, raw[:, : qc + kc], mixed_low, ffn_part, parts, heads, kv_local, cid=5,
+        normed, qkv_low, raw, mixed_low, ffn_part, parts, heads, kv_heads, cid=4,
     )
     grad_w_attn, ffn_own = lax.optimization_barrier((grad_w_attn, ffn_own))
     attn_own = spread(grad_w_attn).astype(jnp.float32)
     ffn_own = ffn_own.astype(jnp.float32)
     grad_in, sums = final(
-        grad_normed, hidden_in, grad_middle, first_gain[None], grad_second, grad_small, parts, groups, cid=6
+        grad_normed, hidden_in, grad_middle, gain_first, grad_second, grad_small, parts, groups, cid=5
     )
     place = lax.axis_index("fsdp") * head_slot
     return (

time: 666 us -> 591 us (0.89)
  Pallas kernels: 474 us -> 508 us
  other arithmetic: 35 us -> 8.74 us
  blocking collectives: 24.1 us -> 0 us
  matrix products: 21.6 us -> 0 us
  local copies, waits for them, and re-layouts: 46.1 us -> 25.4 us
  waiting for transfers between devices: 43.1 us -> 27.6 us
    pallas_call x2, Pallas kernels: 138 us -> 178 us  [the longest x1 99.6 us: attn(): pl.pallas_call(functools.partial(attn_kernel, n, axis, heads, kv_heads),...]
    all_gather x1, waiting for transfers between devices: 28.8 us -> 0.02 us  [per_device(): lax.all_gather(jnp.concatenate([w_gate, w_up, w_down.T], axis=1), 'fsdp',...]
    unnamed x1 -> x0, blocking collectives: 24.1 us -> none
    dot_general x4 -> x0, matrix products: 21.6 us -> none  [the longest x1 8.16 us: per_device(): raw = jnp.dot(normed, full_qkv, preferred_element_type=jnp.float32)]
    reduce_scatter x2, waiting for transfers between devices: 14.2 us -> 27.5 us  [spread(): return lax.psum_scatter(value, 'fsdp', scatter_dimension=0, tiled=True)]
    reduce_sum x4 -> x0, other arithmetic: 10.3 us -> none  [the longest x3 6.57 us: rms_scale(): return lax.rsqrt(jnp.mean(value * value, axis=-1, keepdims=True) + EPS)]
    pallas_call x1, Pallas kernels: 159 us -> 150 us  [ffn(): pl.pallas_call(functools.partial(ffn_kernel, n, axis), out_shape=(jax.Sha...]
    unnamed x109 -> x50, local copies, waits for them, and re-layouts: 24.6 us -> 17.3 us
  transfers between devices with their start and end apart: 5 -> 4, of which waited for: 2 -> 1; matrix products, arithmetic and copies ran while one was open for 12% -> 3% of each run, Pallas kernels for 48% -> 61%
where the time goes in v4:
time: 591 us; the launch traced here: 585 us
  Pallas kernels  508 us (86%)
  waiting for transfers between devices  27.6 us (5%)
  local copies, waits for them, and re-layouts  25.4 us (4%)
  between operations  14.9 us (3%)
  other arithmetic  8.74 us (1%)
    pallas_call x1, Pallas kernels, ffn(): pl.pallas_call(functools.partial(ffn_kernel, n, axis), out_shape=(jax.Sha...  150 us
    pallas_call x1, Pallas kernels, attn_back(): pl.pallas_call(functools.partial(attn_back_kernel, n, axis, heads, kv_hea...  100 us
    pallas_call x1, Pallas kernels, attn(): pl.pallas_call(functools.partial(attn_kernel, n, axis, heads, kv_heads),...  99.6 us
    pallas_call x1, Pallas kernels, final(): pl.pallas_call(functools.partial(final_kernel, n, groups), out_shape=(jax...  81 us
    pallas_call x1, Pallas kernels, entry(): pl.pallas_call(functools.partial(entry_kernel, n, groups, head_slot), out...  78.1 us
    reduce_scatter x2, waiting for transfers between devices, spread(): return lax.psum_scatter(value, 'fsdp', scatter_dimension=0, tiled=True)  27.5 us
    unnamed x50, local copies, waits for them, and re-layouts  17.3 us
  transfers between devices with their start and end apart: 4, of which 1 were waited for; matrix products, arithmetic and copies ran while one was open for 3% of the time, Pallas kernels for 61%

profile of v4, /device:TPU:0, one launch (start us, length us, event | category | flops | bytes accessed | tf_op | source)
XLA Modules:
  0.0 585.3 jit_solution(2524925750153226745)
XLA Ops:
  7.2 0.0 copy-start.16
  7.2 0.0 copy-start.15
  7.2 0.0 all-gather.3.cloned.1.call-start
  7.3 1.2 copy.28
  8.5 2.0 pad_maximum_fusion.1
  10.5 0.0 all-gather.3.cloned.1.call-update
  10.5 0.0 all-gather.5.cloned.1.call-start
  10.6 0.3 copy.29
  10.9 1.6 pad_maximum_fusion
  12.5 0.0 copy-start.21
  12.5 0.0 all-gather.5.cloned.1.call-update
  12.5 0.0 copy-start
  12.5 0.0 reduce-scatter.3.cloned.1.call-start
  12.6 0.6 copy-done.17
  13.2 0.0 copy-done.20
  13.2 0.0 copy-done.21
  13.9 1.9 fusion
  15.8 1.3 pad_maximum_fusion.2
  17.1 78.1 %entry.1 = (bf16[1024,2048]{1,0:T(8,128)(2,1)S(1)}, f32[1,2048]{1,0:T(1,128)S(1)}, f32[1,2048]{1,0:T(1,128)S(1)}, f32[8,128]{1,0:T(8,128)S(1)}) custom-call(bf16[256,2048]{1,0:T(8,128)(2,1)S(1)} %copy-done, f32[1,768]{1,0:T(1,128)S(1)} %reshape.36.pack_ref), custom_call_target="tpu_custom_call" | custom-call | flops 17179869184 | bytes 209715200 | tf_op jit(solution)/shard_map/entry/pallas_call | solution.py:158
  95.2 2.1 copy-done.3
  97.3 0.6 copy-done.6
  97.9 0.6 copy-done.7
  98.5 0.6 copy-done.10
  99.1 99.6 %attn.1 = (f32[256,2048]{1,0:T(8,128)}, bf16[1024,2048]{1,0:T(8,128)(2,1)}, bf16[1024,1024]{1,0:T(8,128)(2,1)}, f32[1024,768]{1,0:T(8,128)}, bf16[1024,512]{1,0:T(8,128)(2,1)}, /*index=5*/f32[8,1024]{1,0:T(8,128)}) custom-call(bf16[256,2048]{1,0:T(8,128)(2,1)} %x_ref.5, bf16[256,2048]{1,0:T(8,128)(2,1)} %go_ref.1, bf16[1024,2048]{1,0:T(8,128)(2,1)} %copy-done.3, ...), custom_call_target="tpu_custom_call" | custom-call | flops 17179869184 | bytes 314572800 | tf_op jit(solution)/shard_map/attn/pallas_call | solution.py:332
  198.7 0.0 all-gather.5.cloned.1.call-done.w_ref
  198.7 149.6 %ffn.1 = (f32[256,2048]{1,0:T(8,128)}, f32[1,2048]{1,0:T(1,128)}, bf16[1024,2048]{1,0:T(8,128)(2,1)}, bf16[2048,4608]{1,0:T(8,128)(2,1)}) custom-call(f32[256,2048]{1,0:T(8,128)} %get-tuple-element.37.mid_ref, f32[1,2048]{1,0:T(1,128)} %copy-done.10, bf16[1024,2048]{1,0:T(8,128)(2,1)} %get-tuple-element.39.go_ref, ...), custom_call_target="tpu_custom_call" | custom-call | flops 57982058496 | bytes 37748736 | tf_op jit(solution)/shard_map/ffn/pallas_call | solution.py:535
  348.3 0.0 reduce-scatter.3.cloned.1.call-update
  348.4 0.0 reduce-scatter.5.cloned.1.call-start
  348.4 100.1 %attn_back.1 = (bf16[256,2048]{1,0:T(8,128)(2,1)}, bf16[1024,2048]{1,0:T(8,128)(2,1)}, f32[8,128]{1,0:T(8,128)}, bf16[2048,1536]{1,0:T(8,128)(2,1)}) custom-call(f32[256,2048]{1,0:T(8,128)} %get-tuple-element.40.gmid_ref, f32[256,2048]{1,0:T(8,128)} %get-tuple-element.37.mid_ref, f32[1024,128]{1,0:T(8,128)} %get-tuple-element.81.cos_ref, ...), custom_call_target="tpu_custom_call" | custom-call | flops 8053063680 | bytes 83886080 | tf_op jit(solution)/shard_map/attn_back/pallas_call | solution.py:772
  448.6 27.5 %reduce-scatter.3.cloned.1.call-done = bf16[256,4608]{1,0:T(8,128)(2,1)} async-done(((bf16[2048,4608]{1,0:T(8,128)(2,1)}), bf16[256,4608]{1,0:T(8,128)(2,1)}) %reduce-scatter.3.cloned.1.call-update) | async-done | bytes 2359312 | tf_op jit(solution)/shard_map/reduce_scatter | solution.py:1014
  476.1 0.0 reduce-scatter.5.cloned.1.call-update
  476.1 1.2 copy-done.1
  477.3 2.2 copy-done.2
  479.5 1.6 copy-done.4
  481.1 81.0 %final.1 = (f32[256,2048]{1,0:T(8,128)S(1)}, f32[1,768]{1,0:T(1,128)S(1)}) custom-call(bf16[1024,2048]{1,0:T(8,128)(2,1)S(1)} %copy-done.2, bf16[256,2048]{1,0:T(8,128)(2,1)S(1)} %copy-done.1, f32[256,2048]{1,0:T(8,128)S(1)} %copy-done.4, f32[1,2048]{1,0:T(1,128)S(1)} %copy-done.8, f32[1,2048]{1,0:T(1,128)S(1)} %copy-done.9, f32[8,128]{1,0:T(8,128)S(1)} %copy-done.5), custom_call_target="tpu_custom_call" | custom-call | flops 17179869184 | bytes 209715200 | tf_op jit(solution)/shard_map/final/pallas_call | solution.py:943
  562.1 0.6 dynamic-slice_bitcast_fusion
  562.7 0.6 dynamic-slice_bitcast_fusion.1
  563.3 0.6 fusion.9
  563.9 0.5 convert_element_type.18
  564.4 1.3 slice_bitcast_fusion
  565.7 3.0 copy.31
  568.7 3.4 fusion.7
  572.1 1.4 convert_element_type.17
  573.6 1.0 copy.30
  574.6 0.8 fusion.8
  575.4 0.9 slice.44
  576.2 1.0 copy.35
  577.2 1.3 copy.36
  (38 shorter events, 0.1 us)
Async XLA Ops:
  7.2 3.4 copy-start.16
  7.2 3.7 copy-start.15
  7.2 3.7 copy-start.14
  7.2 91.9 %all-gather.3.cloned.1.call-start = ((), (), s32[]{:S(2)}) async-start(), calls=%async_computation.2 | async-start | bytes 7077888 | tf_op jit(solution)/shard_map/all_gather | solution.py:989
  10.5 188.2 %all-gather.5.cloned.1.call-start = ((), (), s32[]{:S(2)}) async-start(), calls=%async_computation.3 | async-start | bytes 21233664 | tf_op jit(solution)/shard_map/all_gather | solution.py:992
  12.5 0.7 copy-start.17
  12.5 0.7 copy-start.18
  12.5 0.7 copy-start.19
  12.5 0.7 copy-start.20
  12.5 0.7 copy-start.21
  12.5 4.6 copy-start
  12.5 463.5 %reduce-scatter.3.cloned.1.call-start = ((), (), s32[]{:S(2)}) async-start(), calls=%async_computation.4 | async-start | bytes 21233664 | tf_op jit(solution)/shard_map/reduce_scatter | solution.py:1014
  95.2 2.1 copy-start.3
  97.3 0.6 copy-start.6
  97.9 0.6 copy-start.7
  98.5 0.6 copy-start.10
  348.4 223.8 %reduce-scatter.5.cloned.1.call-start = ((), (), s32[]{:S(2)}) async-start(), calls=%async_computation.5 | async-start | bytes 7077888 | tf_op jit(solution)/shard_map/reduce_scatter | solution.py:1014
  476.1 1.2 copy-start.1
  476.1 1.2 copy-start.5
  476.1 1.2 copy-start.8
  476.1 1.2 copy-start.9
  477.3 2.2 copy-start.2
  479.5 1.6 copy-start.4
  481.1 82.8 %copy-start.11 = (bf16[256,4608]{1,0:T(8,128)(2,1)S(1)}, bf16[256,4608]{1,0:T(8,128)(2,1)}, u32[]{:S(2)}) copy-start(bf16[256,4608]{1,0:T(8,128)(2,1)} %reduce-scatter.3.cloned.1.call-done) | copy-start | bytes 7077892
  572.1 2.4 copy-start.12
  574.6 1.7 copy-start.13
Sparse Core Ops, SparseCore 0:
  10.7 48.1 all-gather.2
  60.8 98.5 all-gather.4
  348.5 127.5 reduce-scatter.2
  479.3 61.7 reduce-scatter.4

commit v5 on v4

--- a/solution.py
+++ b/solution.py
@@ -1018,12 +1018,14 @@
         grad_middle, middle, cos_all, sin_all, log_rows, gain_rows, prefix_len, attn_set,
         normed, qkv_low, raw, mixed_low, ffn_part, parts, heads, kv_heads, cid=4,
     )
-    grad_w_attn, ffn_own = lax.optimization_barrier((grad_w_attn, ffn_own))
-    attn_own = spread(grad_w_attn).astype(jnp.float32)
-    ffn_own = ffn_own.astype(jnp.float32)
+    attn_own = spread(grad_w_attn)
     grad_in, sums = final(
         grad_normed, hidden_in, grad_middle, gain_first, grad_second, grad_small, parts, groups, cid=5
     )
+    ffn_own = ffn_own.astype(jnp.float32)
+    gate_own, up_own, down_own = ffn_own[:, :fc], ffn_own[:, fc : 2 * fc], ffn_own[:, 2 * fc :].T
+    attn_own, gate_own, up_own, down_own = lax.optimization_barrier((attn_own, gate_own, up_own, down_own))
+    attn_own = attn_own.astype(jnp.float32)
     place = lax.axis_index("fsdp") * head_slot
     return (
         out,
@@ -1036,9 +1038,9 @@
         lax.dynamic_slice_in_dim(sums[0, 2 * slot : 2 * slot + HD], place, head_slot),
         lax.dynamic_slice_in_dim(sums[0, 2 * slot + HD :], place, head_slot),
         sums[0, slot : 2 * slot],
-        ffn_own[:, :fc],
-        ffn_own[:, fc : 2 * fc],
-        ffn_own[:, 2 * fc :].T,
+        gate_own,
+        up_own,
+        down_own,
     )
 
 

time: 591 us -> 565 us (0.956)
  waiting for transfers between devices: 27.6 us -> 0.09 us
    reduce_scatter x2, waiting for transfers between devices: 27.5 us -> 0.01 us  [spread(): return lax.psum_scatter(value, 'fsdp', scatter_dimension=0, tiled=True)]
  transfers between devices with their start and end apart: 4 -> 4, of which waited for: 1 -> 0; matrix products, arithmetic and copies ran while one was open for 3% -> 2% of each run, Pallas kernels for 61% -> 64%
where the time goes in v5:
time: 565 us; the launch traced here: 559 us
  Pallas kernels  508 us (90%)
  local copies, waits for them, and re-layouts  25.1 us (4%)
  between operations  14.9 us (3%)
  other arithmetic  10.5 us (2%)
    pallas_call x1, Pallas kernels, ffn(): pl.pallas_call(functools.partial(ffn_kernel, n, axis), out_shape=(jax.Sha...  150 us
    pallas_call x1, Pallas kernels, attn_back(): pl.pallas_call(functools.partial(attn_back_kernel, n, axis, heads, kv_hea...  100 us
    pallas_call x1, Pallas kernels, attn(): pl.pallas_call(functools.partial(attn_kernel, n, axis, heads, kv_heads),...  99.6 us
    pallas_call x1, Pallas kernels, final(): pl.pallas_call(functools.partial(final_kernel, n, groups), out_shape=(jax...  80.9 us
    pallas_call x1, Pallas kernels, entry(): pl.pallas_call(functools.partial(entry_kernel, n, groups, head_slot), out...  78.1 us
    unnamed x50, local copies, waits for them, and re-layouts  18.3 us
  transfers between devices with their start and end apart: 4, of which 0 were waited for; matrix products, arithmetic and copies ran while one was open for 2% of the time, Pallas kernels for 64%

profile of v5, /device:TPU:0, one launch (start us, length us, event | category | flops | bytes accessed | tf_op | source)
XLA Modules:
  0.0 559.1 jit_solution(17043140420422974925)
XLA Ops:
  7.2 0.0 all-gather.3.cloned.1.call-start
  7.3 1.2 copy.28
  8.5 2.0 pad_maximum_fusion.1
  10.5 0.0 all-gather.3.cloned.1.call-update
  10.5 0.0 all-gather.5.cloned.1.call-start
  10.6 0.3 copy.29
  10.9 1.6 pad_maximum_fusion
  12.5 0.0 copy-start.21
  12.5 0.0 all-gather.5.cloned.1.call-update
  12.5 0.0 copy-start
  12.5 0.0 reduce-scatter.5.cloned.1.call-start
  12.6 0.6 copy-done.17
  13.2 0.0 copy-done.20
  13.2 0.0 copy-done.21
  13.9 1.9 fusion
  15.8 1.3 pad_maximum_fusion.2
  17.1 78.1 %entry.1 = (bf16[1024,2048]{1,0:T(8,128)(2,1)S(1)}, f32[1,2048]{1,0:T(1,128)S(1)}, f32[1,2048]{1,0:T(1,128)S(1)}, f32[8,128]{1,0:T(8,128)S(1)}) custom-call(bf16[256,2048]{1,0:T(8,128)(2,1)S(1)} %copy-done, f32[1,768]{1,0:T(1,128)S(1)} %reshape.36.pack_ref), custom_call_target="tpu_custom_call" | custom-call | flops 17179869184 | bytes 209715200 | tf_op jit(solution)/shard_map/entry/pallas_call | solution.py:158
  95.2 2.1 copy-done.3
  97.3 0.6 copy-done.6
  97.9 0.6 copy-done.7
  98.5 0.6 copy-done.10
  99.1 99.6 %attn.1 = (f32[256,2048]{1,0:T(8,128)}, bf16[1024,2048]{1,0:T(8,128)(2,1)}, bf16[1024,1024]{1,0:T(8,128)(2,1)}, f32[1024,768]{1,0:T(8,128)}, bf16[1024,512]{1,0:T(8,128)(2,1)}, /*index=5*/f32[8,1024]{1,0:T(8,128)}) custom-call(bf16[256,2048]{1,0:T(8,128)(2,1)} %x_ref.5, bf16[256,2048]{1,0:T(8,128)(2,1)} %go_ref.1, bf16[1024,2048]{1,0:T(8,128)(2,1)} %copy-done.3, ...), custom_call_target="tpu_custom_call" | custom-call | flops 17179869184 | bytes 314572800 | tf_op jit(solution)/shard_map/attn/pallas_call | solution.py:332
  198.7 0.0 all-gather.5.cloned.1.call-done.w_ref
  198.7 149.6 %ffn.1 = (f32[256,2048]{1,0:T(8,128)}, f32[1,2048]{1,0:T(1,128)}, bf16[1024,2048]{1,0:T(8,128)(2,1)}, bf16[2048,4608]{1,0:T(8,128)(2,1)}) custom-call(f32[256,2048]{1,0:T(8,128)} %get-tuple-element.39.mid_ref, f32[1,2048]{1,0:T(1,128)} %copy-done.10, bf16[1024,2048]{1,0:T(8,128)(2,1)} %get-tuple-element.41.go_ref, ...), custom_call_target="tpu_custom_call" | custom-call | flops 57982058496 | bytes 37748736 | tf_op jit(solution)/shard_map/ffn/pallas_call | solution.py:535
  348.3 0.0 reduce-scatter.5.cloned.1.call-update
  348.4 0.0 reduce-scatter.3.cloned.1.call-start
  348.4 100.1 %attn_back.1 = (bf16[256,2048]{1,0:T(8,128)(2,1)}, bf16[1024,2048]{1,0:T(8,128)(2,1)}, f32[8,128]{1,0:T(8,128)}, bf16[2048,1536]{1,0:T(8,128)(2,1)}) custom-call(f32[256,2048]{1,0:T(8,128)} %get-tuple-element.42.gmid_ref, f32[256,2048]{1,0:T(8,128)} %get-tuple-element.39.mid_ref, f32[1024,128]{1,0:T(8,128)} %get-tuple-element.85.cos_ref, ...), custom_call_target="tpu_custom_call" | custom-call | flops 8053063680 | bytes 83886080 | tf_op jit(solution)/shard_map/attn_back/pallas_call | solution.py:772
  448.6 0.0 copy-start.1
  448.6 0.0 copy-start.8
  448.6 0.0 reduce-scatter.3.cloned.1.call-update
  448.6 1.2 copy-done.1
  449.8 2.2 copy-done.2
  452.0 1.6 copy-done.4
  453.6 80.9 %final.1 = (f32[256,2048]{1,0:T(8,128)S(1)}, f32[1,768]{1,0:T(1,128)S(1)}) custom-call(bf16[1024,2048]{1,0:T(8,128)(2,1)S(1)} %copy-done.2, bf16[256,2048]{1,0:T(8,128)(2,1)S(1)} %copy-done.1, f32[256,2048]{1,0:T(8,128)S(1)} %copy-done.4, f32[1,2048]{1,0:T(1,128)S(1)} %copy-done.8, f32[1,2048]{1,0:T(1,128)S(1)} %copy-done.9, f32[8,128]{1,0:T(8,128)S(1)} %copy-done.5), custom_call_target="tpu_custom_call" | custom-call | flops 17179869184 | bytes 209715200 | tf_op jit(solution)/shard_map/final/pallas_call | solution.py:943
  534.5 0.6 dynamic-slice_bitcast_fusion
  535.1 0.6 dynamic-slice_bitcast_fusion.1
  535.7 0.6 fusion.9
  536.3 2.2 convert_element_type.17
  538.5 1.3 slice_bitcast_fusion
  539.8 1.0 copy-done.11
  540.8 2.1 fusion.7
  542.9 1.4 convert_element_type.18
  544.2 0.8 fusion.8
  545.1 0.9 slice.47
  546.0 1.0 copy.30
  547.0 3.1 copy.31
  550.1 1.0 copy.35
  551.0 1.3 copy.36
  (38 shorter events, 0.1 us)
Async XLA Ops:
  7.2 3.4 copy-start.16
  7.2 3.7 copy-start.15
  7.2 3.7 copy-start.14
  7.2 91.9 %all-gather.3.cloned.1.call-start = ((), (), s32[]{:S(2)}) async-start(), calls=%async_computation.2 | async-start | bytes 7077888 | tf_op jit(solution)/shard_map/all_gather | solution.py:989
  10.5 188.2 %all-gather.5.cloned.1.call-start = ((), (), s32[]{:S(2)}) async-start(), calls=%async_computation.3 | async-start | bytes 21233664 | tf_op jit(solution)/shard_map/all_gather | solution.py:992
  12.5 0.7 copy-start.17
  12.5 0.7 copy-start.18
  12.5 0.7 copy-start.19
  12.5 0.7 copy-start.20
  12.5 0.7 copy-start.21
  12.5 4.6 copy-start
  12.5 523.7 %reduce-scatter.5.cloned.1.call-start = ((), (), s32[]{:S(2)}) async-start(), calls=%async_computation.5 | async-start | bytes 21233664 | tf_op jit(solution)/shard_map/reduce_scatter | solution.py:1014
  95.2 2.1 copy-start.3
  97.3 0.6 copy-start.6
  97.9 0.6 copy-start.7
  98.5 0.6 copy-start.10
  348.4 194.5 %reduce-scatter.3.cloned.1.call-start = ((), (), s32[]{:S(2)}) async-start(), calls=%async_computation.4 | async-start | bytes 7077888 | tf_op jit(solution)/shard_map/reduce_scatter | solution.py:1014
  448.6 1.2 copy-start.1
  448.6 1.2 copy-start.5
  448.6 1.2 copy-start.8
  448.6 1.2 copy-start.9
  449.8 2.2 copy-start.2
  452.0 1.6 copy-start.4
  538.5 2.2 copy-start.11
  542.8 1.4 copy-start.12
  547.0 3.1 copy-start.13
Sparse Core Ops, SparseCore 0:
  10.7 48.1 all-gather.2
  60.8 98.5 all-gather.4
  348.5 127.5 reduce-scatter.4
  479.3 61.9 reduce-scatter.2
